TPU v7x, 32 devices: a whole 2x2x4 slice. The times are simulated.
32 devices in a mesh: batch: 8 (over z, x), mp: 4 (over y, core).
Axes of the slice: x: 2, y: 2, z: 4, core: 2. Of those that a mesh axis runs over, the one named last changes fastest.
Arguments:
- image_states: bfloat16 [96, 197, 768], P('batch'), may hold values from -6 to 6
- text_states: bfloat16 [96, 40, 768], P('batch'), may hold values from -6 to 6
- caption_lengths: int32 [96], P('batch'), may hold values from 8 to 40, as said below
- image_cotangent: bfloat16 [96, 197, 768], P('batch'), may hold values from -6 to 6
- text_cotangent: bfloat16 [96, 40, 768], P('batch'), may hold values from -6 to 6
- first_gain: float32 [768], replicated, may hold values from 0.5 to 1.5
- first_shift: float32 [768], replicated, may hold values from -0.6 to 0.6
- query_key_value: bfloat16 [768, 3, 768], P(None, None, 'mp'), may hold values from -0.21875 to 0.21875
- query_value_bias: float32 [2, 768], P(None, 'mp'), may hold values from -1.2 to 1.2
- output_weight: bfloat16 [768, 768], P('mp'), may hold values from -1.25 to 1.25
- output_bias: float32 [768], replicated, may hold values from -0.6 to 0.6
- attention_scale: float32 [768], replicated, may hold values from 0.5 to 1.5
- expert_gain: float32 [2, 768], replicated, may hold values from 0.5 to 1.5
- expert_shift: float32 [2, 768], replicated, may hold values from -0.6 to 0.6
- expert_up: bfloat16 [2, 768, 3072], P(None, None, 'mp'), may hold values from -0.21875 to 0.21875
- expert_up_bias: float32 [2, 3072], P(None, 'mp'), may hold values from -1.2 to 1.2
- expert_down: bfloat16 [2, 3072, 768], P(None, 'mp'), may hold values from -0.109375 to 0.109375
- expert_down_bias: float32 [2, 768], replicated, may hold values from -0.6 to 0.6
- feedforward_scale: float32 [768], replicated, may hold values from 0.5 to 1.5
- head_gain: float32 [2, 768], replicated, may hold values from 0.5 to 1.5
- head_shift: float32 [2, 768], replicated, may hold values from -0.6 to 0.6
- head_weight: bfloat16 [2, 768, 768], replicated, may hold values from -0.21875 to 0.21875
- logit_scale: float32 [1], replicated, may hold values from 3.7 to 4.4
Outputs:
- image_output: bfloat16 [96, 197, 768], P('batch')
- text_output: bfloat16 [96, 40, 768], P('batch')
- contrast_loss: float32 [1], replicated
- image_grad: bfloat16 [96, 197, 768], P('batch')
- text_grad: bfloat16 [96, 40, 768], P('batch')
- grad_first_gain: float32 [768], P('batch')
- grad_first_shift: float32 [768], P('batch')
- grad_query_key_value: float32 [768, 3, 768], P('batch', None, 'mp')
- grad_query_value_bias: float32 [2, 768], P(None, 'mp')
- grad_output_weight: float32 [768, 768], P('mp', 'batch')
- grad_output_bias: float32 [768], P('batch')
- grad_attention_scale: float32 [768], P('batch')
- grad_expert_gain: float32 [2, 768], P(None, 'batch')
- grad_expert_shift: float32 [2, 768], P(None, 'batch')
- grad_expert_up: float32 [2, 768, 3072], P(None, 'batch', 'mp')
- grad_expert_up_bias: float32 [2, 3072], P(None, 'mp')
- grad_expert_down: float32 [2, 3072, 768], P(None, 'mp', 'batch')
- grad_expert_down_bias: float32 [2, 768], P(None, 'batch')
- grad_feedforward_scale: float32 [768], P('batch')
- grad_head_gain: float32 [2, 768], P(None, 'batch')
- grad_head_shift: float32 [2, 768], P(None, 'batch')
- grad_head_weight: float32 [2, 768, 768], P(None, 'batch')
- grad_logit_scale: float32 [1], replicated
Inputs may be any that keep to these rules, and one draw needn't show every extreme that they name: Caption p occupies positions 0 to caption_lengths[p] - 1 of its row; the rest is padding. In every draw some caption has all 40 positions.
All inputs are finite; a program needn't handle non-finite values.
Results may differ from a plain program's by a relative error of at most 0.02.
Values may be sent and summed in bfloat16 or wider, within the bound.
A program may use at most 256 MiB of HBM per device.

v0:
```python
import functools
from typing import NamedTuple

import jax
import jax.numpy as jnp
from jax import lax
from jax.experimental import pallas as pl
from jax.experimental.pallas import tpu as pltpu
from jax.sharding import PartitionSpec as P

HEAD_DIM = 64
F32 = jnp.float32
BF16 = jnp.bfloat16
NEG = -1e9
EPS = 1e-5
ORDER = (0, 2, 1, 3)

VMEM_LIMIT = 60 * 1024 * 1024


def params(**kw):
    return pltpu.CompilerParams(vmem_limit_bytes=VMEM_LIMIT, **kw)


def up16(n):
    return -(-n // 16) * 16


def dot(a, b):
    return jnp.dot(a, b, preferred_element_type=F32)


def dot_t(a, b):
    return lax.dot_general(a, b, (((1,), (1,)), ((), ())), preferred_element_type=F32)


def t_dot(a, b):
    return lax.dot_general(a, b, (((0,), (0,)), ((), ())), preferred_element_type=F32)


def normalise(x):
    c = x - jnp.mean(x, axis=-1, keepdims=True)
    v = jnp.mean(c * c, axis=-1, keepdims=True)
    r = lax.rsqrt(v + EPS)
    return c * r, r


def norm_back(n, r, dn):
    a = jnp.mean(dn, axis=-1, keepdims=True)
    b = jnp.mean(dn * n, axis=-1, keepdims=True)
    return (dn - a - n * b) * r


def gelu_parts(u):
    big = 0.5 * (1.0 + lax.erf(u * 0.7071067811865476))
    small = 0.3989422804014327 * jnp.exp(-0.5 * u * u)
    return big, small


def gelu_low(u):
    return (u * (0.5 * (1.0 + lax.erf(u * 0.7071067811865476)))).astype(BF16)


def softmax_rows(scores):
    m = jnp.max(scores, axis=-1, keepdims=True)
    e = jnp.exp(scores - m)
    return e * (1.0 / jnp.sum(e, axis=-1, keepdims=True))


def tie(value, *after):
    return lax.optimization_barrier((value,) + after)[0]


def load_rows(dims, p, img, txt, rows):
    rows[0:dims.patches, :] = img[p].astype(F32)
    rows[dims.ip:dims.ip + dims.caption, :] = txt[p].astype(F32)


def spec_whole(a):
    return pl.BlockSpec(a.shape, lambda *_: (0,) * a.ndim)


class Dims(NamedTuple):
    patches: int
    caption: int
    ip: int
    tp: int
    slab: int
    quarter: int
    local: int


GAIN1, SHIFT1, A_SCALE, A_BIAS, GAIN2, SHIFT2, F_SCALE, F_BIAS, H_GAIN, H_SHIFT = 0, 1, 2, 3, 4, 6, 8, 9, 11, 13


def vector(table, at, count=1):
    return table[at:at + count, :]


def copy_rows(dst, at, src, start, count):
    dst[at:at + count, :] = src[start:start + count, :]


def parts_of(dims):
    return 2 * HEAD_DIM, HEAD_DIM


def key_tail(dims, length):
    at = dims.patches // 16 * 16
    return ((0, dims.ip, at, dims.patches), (dims.ip, dims.slab, 0, length))


def hide(scores, start, limit):
    if start >= scores.shape[0]:
        return scores
    tail = scores[start:]
    at = start + lax.broadcasted_iota(jnp.int32, (tail.shape[0], 1), 0)
    tail = jnp.where(at < limit, tail, NEG)
    return tail if start == 0 else jnp.concatenate([scores[:start], tail], axis=0)


def split_pair(value):
    low = lax.broadcasted_iota(jnp.int32, (1, 128), 1) < HEAD_DIM
    zero = jnp.zeros_like(value)
    return jnp.concatenate([jnp.where(low, value, zero), jnp.where(low, zero, value)], axis=0)


def join_pair(value):
    low = lax.broadcasted_iota(jnp.int32, (1, 128), 1) < HEAD_DIM
    half = value.shape[0] // 2
    return jnp.where(low, value[:half], value[half:])


def softmax_keys(scores):
    e = jnp.exp(scores - jnp.max(scores, axis=0, keepdims=True))
    return e * (1.0 / jnp.sum(e, axis=0, keepdims=True))


def pair_weights(q, k, start, limit):
    return softmax_keys(hide(dot_t(k, split_pair(q)), start, limit))


def scaled(q):
    return q * jnp.asarray(HEAD_DIM ** -0.5, BF16)


def attend_tiles(dims, lens, quarter_at, qkv, mixed):
    tiles = mixed.shape[-1] // 128

    def one_pair(p, c):
        length = lens[quarter_at * dims.quarter + p]
        for lo, hi, start, limit in key_tail(dims, length):
            for g in range(tiles):
                q, k, v = [qkv[p, lo:hi, (t * tiles + g) * 128:(t * tiles + g + 1) * 128] for t in range(3)]
                w = pair_weights(scaled(q), k, start, limit).astype(BF16)
                mixed[p, lo:hi, g * 128:(g + 1) * 128] = join_pair(t_dot(w, v)).astype(BF16)
        return c

    lax.fori_loop(0, dims.quarter, one_pair, 0)


def attend_own_kernel(dims, order, lens, img, txt, vec, bias, wo, normed, qkv, rest, mixed, rows, w, b):
    i = pl.program_id(0)
    local = dims.local
    two, one_head = parts_of(dims)

    @pl.when(i == 0)
    def _():
        rows[...] = jnp.zeros_like(rows)
        w[...] = jnp.zeros_like(w)
        b[...] = jnp.zeros_like(b)
        for t in range(3):
            copy_rows(w, t * 2 * two, wo, t * local, local)
        b[0:1, 0:local] = bias[0:1, :]
        b[0:1, 4 * two:4 * two + local] = bias[1:2, :]

    def one_norm(p, c):
        load_rows(dims, p, img, txt, rows)
        n, _ = normalise(rows[...])
        normed[p] = (n * vector(vec, GAIN1) + vector(vec, SHIFT1)).astype(BF16)
        return c

    lax.fori_loop(0, dims.quarter, one_norm, 0)
    model = normed.shape[-1]
    proj = (dot_t(normed[...].reshape(dims.quarter * dims.slab, model), w[...]) + b[0:1, :]).astype(BF16)
    proj = proj.reshape(dims.quarter, dims.slab, 6 * two)
    for t in range(3):
        qkv[:, :, t * two:(t + 1) * two] = proj[:, :, 2 * t * two:(2 * t + 1) * two]
        rest[:, :, t * two:(t + 1) * two] = proj[:, :, (2 * t + 1) * two:(2 * t + 2) * two]
    attend_tiles(dims, lens, order[i], qkv, mixed)


def attend_own(dims, order, lens, img, txt, vec, bias, wo):
    model = img.shape[-1]
    pairs = 4 * dims.quarter
    block = lambda cols: pl.BlockSpec((dims.quarter, dims.slab, cols), lambda i, o, n: (i, 0, 0))
    shape = lambda cols: jax.ShapeDtypeStruct((pairs, dims.slab, cols), BF16)
    return pl.pallas_call(
        functools.partial(attend_own_kernel, dims),
        grid_spec=pltpu.PrefetchScalarGridSpec(
            num_scalar_prefetch=2,
            grid=(4,),
            in_specs=[
                pl.BlockSpec((dims.quarter, dims.patches, model), lambda i, o, n: (o[i], 0, 0)),
                pl.BlockSpec((dims.quarter, dims.caption, model), lambda i, o, n: (o[i], 0, 0)),
                spec_whole(vec), spec_whole(bias), spec_whole(wo),
            ],
            out_specs=[block(model), block(384), block(384), block(128)],
            scratch_shapes=[pltpu.VMEM((dims.slab, model), F32), pltpu.VMEM((768, model), BF16),
                            pltpu.VMEM((8, 768), F32)],
        ),
        out_shape=[shape(model), shape(384), shape(384), shape(128)],
        compiler_params=params(),
        cost_estimate=pl.CostEstimate(
            flops=1536 * pairs * dims.slab * model, bytes_accessed=30_000_000, transcendentals=0),
        name="attend_own",
    )(order, lens, img, txt, vec, bias, wo)


def attend_far_kernel(dims, order, lens, normed, rest, own, bias, wo, wf, qkv, mixed, keep, send, w, ow, b):
    i = pl.program_id(0)
    local = dims.local
    two, one_head = parts_of(dims)
    count = dims.quarter * dims.slab
    model = normed.shape[-1]

    @pl.when(i == 0)
    def _():
        w[...] = jnp.zeros_like(w)
        b[...] = jnp.zeros_like(b)
        for t in range(3):
            copy_rows(w, t * 2 * two, wf, t * local, two)
            copy_rows(w, t * 2 * two + two + one_head, wf, t * local + two, one_head)
        for t, at in ((0, 0), (1, 4 * two)):
            b[0:1, at:at + two] = bias[t:t + 1, 0:two]
            b[0:1, at + two + one_head:at + 2 * two] = bias[t:t + 1, two:]
        copy_rows(ow, 0, wo, 3 * local, two)
        copy_rows(ow, two, wf, 3 * local, two)
        copy_rows(ow, 2 * two, wo, 3 * local + two, one_head)
        copy_rows(ow, 2 * two + one_head, wf, 3 * local + two, one_head)

    proj = (dot_t(normed[...].reshape(count, model), w[...]) + b[0:1, :]).astype(BF16)
    proj = proj.reshape(dims.quarter, dims.slab, 6 * two)
    for t in range(3):
        at = 2 * t * two
        qkv[:, :, at:at + two] = proj[:, :, at:at + two]
        qkv[:, :, at + two:at + 2 * two] = proj[:, :, at + two:at + 2 * two] + rest[:, :, t * two:(t + 1) * two]
    attend_tiles(dims, lens, order[(i + 2) % 4], qkv, mixed)
    part = dot(own[...].reshape(count, two), ow[0:two, :])
    part = part + dot(mixed[...].reshape(count, 2 * two), ow[two:, :])
    part = part.astype(BF16).reshape(dims.quarter, dims.slab, model)

    @pl.when(i < 2)
    def _():
        send[...] = part

    @pl.when(i >= 2)
    def _():
        keep[...] = part


def attend_far(dims, order, lens, normed, rest, own, bias, wo, wf):
    model = normed.shape[-1]
    pairs = 4 * dims.quarter
    at = lambda i: (i + 2) % 4
    block = lambda cols, f: pl.BlockSpec((dims.quarter, dims.slab, cols), lambda i, o, n: (f(i), 0, 0))
    shape = lambda count, cols: jax.ShapeDtypeStruct((count, dims.slab, cols), BF16)
    return pl.pallas_call(
        functools.partial(attend_far_kernel, dims),
        grid_spec=pltpu.PrefetchScalarGridSpec(
            num_scalar_prefetch=2,
            grid=(4,),
            in_specs=[
                block(model, at), block(384, at), block(128, at),
                spec_whole(bias), spec_whole(wo), spec_whole(wf),
            ],
            out_specs=[
                block(768, at), block(256, at),
                block(model, lambda i: jnp.maximum(i - 2, 0)), block(model, lambda i: jnp.minimum(i, 1)),
            ],
            scratch_shapes=[pltpu.VMEM((768, model), BF16), pltpu.VMEM((384, model), BF16),
                            pltpu.VMEM((8, 768), F32)],
        ),
        out_shape=[
            shape(pairs, 768), shape(pairs, 256),
            shape(2 * dims.quarter, model), shape(2 * dims.quarter, model),
        ],
        compiler_params=params(),
        cost_estimate=pl.CostEstimate(
            flops=2304 * pairs * dims.slab * model, bytes_accessed=30_000_000, transcendentals=0),
        name="attend_far",
    )(order, lens, normed, rest, own, bias, wo, wf)


def residual_kernel(dims, order, keep, recv, img, txt, vec, attended, attn, expert, cls, rows):
    i = pl.program_id(0)
    ip = dims.ip

    @pl.when(i == 0)
    def _():
        rows[...] = jnp.zeros_like(rows)
        cls[...] = jnp.zeros_like(cls)

    load_rows(dims, 0, img, txt, rows)
    a = keep[0].astype(F32) + recv[0].astype(F32)
    x = rows[...] + vector(vec, A_SCALE) * (a + vector(vec, A_BIAS))
    n, _ = normalise(x)
    e_img = n[0:ip] * vector(vec, GAIN2) + vector(vec, SHIFT2)
    e_txt = n[ip:] * vector(vec, GAIN2 + 1) + vector(vec, SHIFT2 + 1)
    expert[0, 0:ip, :] = e_img.astype(BF16)
    expert[0, ip:, :] = e_txt.astype(BF16)
    for j, v in enumerate((x[0:1], x[ip:ip + 1], e_img[0:1], e_txt[0:1])):
        cls[j, pl.ds(i, 1), :] = v

    @pl.when(i < dims.quarter)
    def _():
        attended[0] = x
        attn[0] = a


def residual(dims, order, keep, recv, img, txt, vec):
    model = img.shape[-1]
    quarter = dims.quarter
    block = pl.BlockSpec((1, dims.slab, model), lambda i, o: (i, 0, 0))
    pair = lambda i, o: (o[i // quarter] * quarter + i % quarter, 0, 0)
    return pl.pallas_call(
        functools.partial(residual_kernel, dims),
        grid_spec=pltpu.PrefetchScalarGridSpec(
            num_scalar_prefetch=1,
            grid=(2 * quarter,),
            in_specs=[
                block, block,
                pl.BlockSpec((1, dims.patches, model), pair),
                pl.BlockSpec((1, dims.caption, model), pair),
                spec_whole(vec),
            ],
            out_specs=[
                pl.BlockSpec((1, dims.slab, model), lambda i, o: (jnp.minimum(i, quarter - 1), 0, 0)),
                pl.BlockSpec((1, dims.slab, model), lambda i, o: (jnp.minimum(i, quarter - 1), 0, 0)),
                block,
                pl.BlockSpec((4, 8, model), lambda i, o: (0, 0, 0)),
            ],
            scratch_shapes=[pltpu.VMEM((dims.slab, model), F32)],
        ),
        out_shape=[
            jax.ShapeDtypeStruct((quarter, dims.slab, model), F32),
            jax.ShapeDtypeStruct((quarter, dims.slab, model), F32),
            jax.ShapeDtypeStruct((2 * quarter, dims.slab, model), BF16),
            jax.ShapeDtypeStruct((4, 8, model), F32),
        ],
        compiler_params=params(),
        cost_estimate=pl.CostEstimate(flops=40_000_000, bytes_accessed=20_000_000, transcendentals=0),
        name="residual",
    )(order, keep, recv, img, txt, vec)


def expert_kernel(dims, seq, peer, own, img, txt, vec, up, up_bias, down,
                  act, dup, ddown, d_send, d_keep, x_send, x_keep, bias_grad, cot, ins, rows):
    ip, slab, quarter = dims.ip, dims.slab, dims.quarter
    i = pl.program_id(0)
    model = own.shape[-1]

    @pl.when(i == 0)
    def _():
        rows[...] = jnp.zeros_like(rows)
        bias_grad[...] = jnp.zeros_like(bias_grad)
        cot[...] = jnp.zeros_like(cot)
        ins[...] = peer[...]

    @pl.when(i == 1)
    def _():
        ins[...] = own[...]

    at = lax.broadcasted_iota(jnp.int32, (slab, 1), 0)
    inner = (at != 0) & (at != ip)

    def one(p, c):
        load_rows(dims, p, img, txt, rows)
        cot[0, pl.ds(8 * i + p, 1), :] = rows[0:1, :]
        cot[1, pl.ds(8 * i + p, 1), :] = rows[ip:ip + 1, :]
        ddown[p] = jnp.where(inner, rows[...] * vector(vec, F_SCALE), 0.0).astype(BF16)
        return c

    lax.fori_loop(0, quarter, one, 0)
    for m, lo, hi in ((0, 0, ip), (1, ip, slab)):
        count = quarter * (hi - lo)
        e = ins[:, lo:hi, :].reshape(count, model)
        u = dot(e, up[m]) + up_bias[m:m + 1]
        big, small = gelu_parts(u)
        a = (u * big).astype(BF16)
        act[:, lo:hi, :] = a.reshape(quarter, hi - lo, -1)
        slope = big + u * small
        d = dot(a, down[m]).astype(BF16).reshape(quarter, hi - lo, model)
        g = ddown[:, lo:hi, :].reshape(count, model)
        du = dot_t(g, down[m]) * slope
        bias_grad[m:m + 1, :] += jnp.sum(du, axis=0, keepdims=True)
        low = du.astype(BF16)
        dup[:, lo:hi, :] = low.reshape(quarter, hi - lo, -1)
        x = dot_t(low, up[m]).astype(BF16).reshape(quarter, hi - lo, model)

        @pl.when(i == 0)
        def _():
            d_send[:, lo:hi, :] = d
            x_send[:, lo:hi, :] = x

        @pl.when(i == 1)
        def _():
            d_keep[:, lo:hi, :] = d
            x_keep[:, lo:hi, :] = x


def experts(dims, name, half, seq, peer, own, img, txt, vec, up, up_bias, down):
    model = own.shape[-1]
    hidden = up.shape[-1]
    slab, quarter = dims.slab, dims.quarter
    fixed = pl.BlockSpec((quarter, slab, model), lambda i, o: (half, 0, 0))
    first = pl.BlockSpec((quarter, slab, model), lambda i, o: (0, 0, 0))
    step = lambda cols: pl.BlockSpec((quarter, slab, cols), lambda i, o: (i, 0, 0))
    shape = lambda n, cols: jax.ShapeDtypeStruct((n * quarter, slab, cols), BF16)
    return pl.pallas_call(
        functools.partial(expert_kernel, dims),
        grid_spec=pltpu.PrefetchScalarGridSpec(
            num_scalar_prefetch=1,
            grid=(2,),
            in_specs=[
                fixed, fixed,
                pl.BlockSpec((quarter, dims.patches, model), lambda i, o: (o[i], 0, 0)),
                pl.BlockSpec((quarter, dims.caption, model), lambda i, o: (o[i], 0, 0)),
                spec_whole(vec), spec_whole(up), spec_whole(up_bias), spec_whole(down),
            ],
            out_specs=[
                step(hidden), step(hidden), step(model),
                first, first, first, first,
                pl.BlockSpec((2, hidden), lambda i, o: (0, 0)),
                pl.BlockSpec((2, 16, model), lambda i, o: (0, 0, 0)),
            ],
            scratch_shapes=[pltpu.VMEM((quarter, slab, model), BF16), pltpu.VMEM((slab, model), F32)],
        ),
        out_shape=[
            shape(2, hidden), shape(2, hidden), shape(2, model),
            shape(1, model), shape(1, model), shape(1, model), shape(1, model),
            jax.ShapeDtypeStruct((2, hidden), F32),
            jax.ShapeDtypeStruct((2, 16, model), F32),
        ],
        compiler_params=params(),
        cost_estimate=pl.CostEstimate(
            flops=16 * quarter * slab * model * hidden, bytes_accessed=20_000_000, transcendentals=0),
        name=name,
    )(seq, peer, own, img, txt, vec, up, up_bias, down)


def expert_grads_kernel(dims, peer, own, act_a, dup_a, ddn_a, act_b, dup_b, ddn_b, ce, ca, cu, cd, out, acc):
    i = pl.program_id(0)

    def add(e, dup, ddn, act):
        for m, lo, hi in ((0, 0, dims.ip), (1, dims.ip, dims.slab)):
            count = dims.quarter * (hi - lo)
            flat = lambda ref: ref[:, lo:hi, :].reshape(count, -1)
            acc[m] += t_dot(flat(e), flat(dup))
            acc[2 + m] += t_dot(flat(ddn), flat(act))

    @pl.when(i == 0)
    def _():
        for m in range(2):
            acc[m] = t_dot(ce[m], cu[m])
            acc[2 + m] = t_dot(cd[m], ca[m])

    for j, refs in enumerate((
        (peer, dup_a, ddn_a, act_a), (own, dup_a, ddn_a, act_a),
        (peer, dup_b, ddn_b, act_b), (own, dup_b, ddn_b, act_b),
    )):
        @pl.when(i == j)
        def _():
            add(*refs)

    @pl.when(i == 3)
    def _():
        out[...] = acc[...].astype(BF16)


def expert_grads(dims, peer, own, act_a, dup_a, ddn_a, act_b, dup_b, ddn_b, ce, ca, cu, cd):
    model = own.shape[-1]
    hidden = act_a.shape[-1]
    slab, quarter = dims.slab, dims.quarter
    assert hidden == model
    half = pl.BlockSpec((quarter, slab, model), lambda i: (jnp.where(i < 2, 1, 0), 0, 0))
    first = pl.BlockSpec((quarter, slab, hidden), lambda i: (jnp.minimum(i, 1), 0, 0))
    last = pl.BlockSpec((quarter, slab, hidden), lambda i: (jnp.maximum(i - 2, 0), 0, 0))
    return pl.pallas_call(
        functools.partial(expert_grads_kernel, dims),
        grid=(4,),
        in_specs=[half, half, first, first, first, last, last, last] + [spec_whole(v) for v in (ce, ca, cu, cd)],
        out_specs=pl.BlockSpec((4, model, hidden), lambda i: (0, 0, 0)),
        scratch_shapes=[pltpu.VMEM((4, model, hidden), F32)],
        out_shape=jax.ShapeDtypeStruct((4, model, hidden), BF16),
        compiler_params=params(),
        cost_estimate=pl.CostEstimate(
            flops=16 * quarter * slab * model * hidden, bytes_accessed=40_000_000, transcendentals=0),
        name="expert_grads",
    )(peer, own, act_a, dup_a, ddn_a, act_b, dup_b, ddn_b, ce, ca, cu, cd)


def own_row(dims, r, p):
    return 8 * (r // 2) + dims.quarter * (r % 2) + p


def class_forward_kernel(dims, near, far, up, up_bias, down, out, rows):
    for m in range(2):
        e = jnp.concatenate([near[2 + m], far[2 + m]], axis=0).astype(BF16)
        rows[m] = e
        u = dot(e, up[m]) + up_bias[m:m + 1]
        out[m] = dot(gelu_low(u), down[m])


def class_forward(dims, near, far, up, up_bias, down):
    shape = (2, 16, near.shape[-1])
    return pl.pallas_call(
        functools.partial(class_forward_kernel, dims),
        out_shape=[jax.ShapeDtypeStruct(shape, F32), jax.ShapeDtypeStruct(shape, BF16)],
        compiler_params=params(),
        cost_estimate=pl.CostEstimate(flops=200_000_000, bytes_accessed=5_000_000, transcendentals=0),
        name="class_forward",
    )(near, far, up, up_bias, down)


def class_final_kernel(dims, order, near, far, d0, d1, d2, d3, vec, out):
    q = dims.quarter
    for m in range(2):
        out[m] = jnp.zeros(out.shape[1:], F32)
        for r in range(4):
            half, at = (near, far)[r // 2], q * (r % 2)
            for p in range(q):
                rows = [d[m, own_row(dims, s, p):own_row(dims, s, p) + 1, :]
                        for d, s in ((d0, r), (d1, r ^ 2), (d2, r ^ 1), (d3, r ^ 3))]
                total = (rows[0] + rows[1]) + (rows[2] + rows[3])
                x = half[m, at + p:at + p + 1, :] + vector(vec, F_SCALE) * (total + vector(vec, F_BIAS + m))
                out[m, pl.ds(4 * order[r] + p, 1), :] = x


def class_final(dims, order, near, far, parts, vec):
    shape = (2, 16, near.shape[-1])
    args = (near, far) + tuple(parts) + (vec,)
    return pl.pallas_call(
        functools.partial(class_final_kernel, dims),
        grid_spec=pltpu.PrefetchScalarGridSpec(
            num_scalar_prefetch=1, grid=(1,),
            in_specs=[spec_whole(v) for v in args],
            out_specs=pl.BlockSpec(shape, lambda i, o: (0, 0, 0)),
        ),
        out_shape=jax.ShapeDtypeStruct(shape, F32),
        compiler_params=params(),
        cost_estimate=pl.CostEstimate(flops=1_000_000, bytes_accessed=1_000_000, transcendentals=0),
        name="class_final",
    )(order, *args)


def class_back_kernel(dims, order, e, cot_a, cot_b, dclass, vec, up, up_bias, down,
                      act, dup, ddown, dexp, bias_grad, dcls, rows):
    q = dims.quarter
    rows[...] = jnp.zeros_like(rows)
    dcls[...] = jnp.zeros_like(dcls)
    for m in range(2):
        for r in range(4):
            cot, base = (cot_b, cot_a)[r % 2], 8 * (1 - r // 2)
            for p in range(q):
                d = dclass[m, pl.ds(4 * order[r] + p, 1), :]
                at = own_row(dims, r, p)
                rows[m, at:at + 1, :] = cot[m, base + p:base + p + 1, :] + d
                if r == 0:
                    dcls[p, m:m + 1, :] = d
        u = dot(e[m], up[m]) + up_bias[m:m + 1]
        big, small = gelu_parts(u)
        act[m] = (u * big).astype(BF16)
        g = (rows[m] * vector(vec, F_SCALE)).astype(BF16)
        ddown[m] = g
        du = dot_t(g, down[m]) * (big + u * small)
        bias_grad[m:m + 1, :] = jnp.sum(du, axis=0, keepdims=True)
        low = du.astype(BF16)
        dup[m] = low
        dexp[m] = dot_t(low, up[m])


def class_back(dims, order, e, cot_a, cot_b, dclass, vec, up, up_bias, down):
    hidden, model = up.shape[-1], e.shape[-1]
    args = (e, cot_a, cot_b, dclass, vec, up, up_bias, down)
    shapes = [((2, 16, hidden), BF16), ((2, 16, hidden), BF16), ((2, 16, model), BF16), ((2, 16, model), F32),
              ((2, hidden), F32), ((dims.quarter, 8, model), F32)]
    return pl.pallas_call(
        functools.partial(class_back_kernel, dims),
        grid_spec=pltpu.PrefetchScalarGridSpec(
            num_scalar_prefetch=1, grid=(1,),
            in_specs=[spec_whole(v) for v in args],
            out_specs=[pl.BlockSpec(s, lambda i, o, n=len(s): (0,) * n) for s, _ in shapes],
            scratch_shapes=[pltpu.VMEM((2, 16, model), F32)],
        ),
        out_shape=[jax.ShapeDtypeStruct(s, t) for s, t in shapes],
        compiler_params=params(),
        cost_estimate=pl.CostEstimate(flops=300_000_000, bytes_accessed=5_000_000, transcendentals=0),
        name="class_back",
    )(order, *args)


def contrast_kernel(dims, total, at, blocks, vec, weight, scale,
                    head_in, dproj, dcls, gains, shifts, scalars, cls, back):
    me = at[0]
    span = blocks[0].shape[0]
    for k, block in enumerate(blocks):
        for j in range(span):
            for m in range(2):
                cls[m, pl.ds(pl.multiple_of(16 * (me ^ (k * span + j)), 16), 16), :] = block[j, m]
    n_rows = cls.shape[1]
    sharp = jnp.exp(scale[...])
    col_at = lax.broadcasted_iota(jnp.int32, (1, n_rows), 1)
    row_at = lax.broadcasted_iota(jnp.int32, (n_rows, 1), 0)
    col_ok = (col_at % 4) < dims.quarter
    row_ok = (row_at % 4) < dims.quarter
    normal, inverse, proj, unit, embed = [], [], [], [], []
    for m in range(2):
        n, r = normalise(cls[m])
        h = (n * vector(vec, H_GAIN + m) + vector(vec, H_SHIFT + m)).astype(BF16)
        head_in[m] = h
        y = dot(h, weight[m])
        u = lax.rsqrt(jnp.sum(y * y, axis=-1, keepdims=True) + 1e-6)
        normal.append(n)
        inverse.append(r)
        proj.append(y)
        unit.append(u)
        embed.append((y * u).astype(BF16))
    ok = row_ok & col_ok
    logits = sharp * dot_t(embed[0], embed[1])
    masked = jnp.where(ok, logits, -1e30)
    row_max = jnp.max(masked, axis=1, keepdims=True)
    row_lse = row_max + jnp.log(jnp.sum(jnp.exp(masked - row_max), axis=1, keepdims=True))
    col_max = jnp.max(masked, axis=0, keepdims=True)
    col_lse = col_max + jnp.log(jnp.sum(jnp.exp(masked - col_max), axis=0, keepdims=True))
    same = (row_at == col_at) & ok
    both = jnp.exp(masked - row_lse) + jnp.exp(masked - col_lse)
    dlogits = jnp.where(ok, jnp.where(same, both - 2.0, both) * (1.0 / (2 * total)), 0.0)
    diagonal = jnp.sum(jnp.where(same, logits, 0.0), axis=1, keepdims=True)
    rows = jnp.where(row_ok, row_lse - 2.0 * diagonal, 0.0)
    cols = jnp.where(col_ok, col_lse, 0.0)
    loss = (jnp.sum(rows, axis=0, keepdims=True) + jnp.sum(cols, axis=1, keepdims=True)) * (1.0 / (2 * total))
    slope = jnp.sum(jnp.sum(dlogits * logits, axis=1, keepdims=True), axis=0, keepdims=True)
    scalars[0:1, :] = jnp.broadcast_to(loss, (1, 128))
    scalars[1:2, :] = jnp.broadcast_to(slope, (1, 128))
    high = lax.Precision.HIGHEST
    wide = [e.astype(F32) for e in embed]
    dembed = [
        sharp * jnp.dot(dlogits, wide[1], precision=high, preferred_element_type=F32),
        sharp * lax.dot_general(dlogits, wide[0], (((0,), (0,)), ((), ())), precision=high,
                                preferred_element_type=F32),
    ]
    for m in range(2):
        u, y, d = unit[m], proj[m], dembed[m]
        dp = (u * d - u * u * u * y * jnp.sum(y * d, axis=-1, keepdims=True)).astype(BF16)
        dproj[m] = dp
        dh = dot_t(dp, weight[m])
        gains[m:m + 1, :] = jnp.sum(dh * normal[m], axis=0, keepdims=True)
        shifts[m:m + 1, :] = jnp.sum(dh, axis=0, keepdims=True)
        back[m] = norm_back(normal[m], inverse[m], dh * vector(vec, H_GAIN + m))
        dcls[m] = back[m, pl.ds(pl.multiple_of(16 * me, 16), 16), :]


def contrast(dims, total, at, blocks, vec, weight, scale):
    model = weight.shape[1]
    rows = 16 * len(blocks) * blocks[0].shape[0]
    args = tuple(blocks) + (vec, weight, scale)
    shapes = [((2, rows, model), BF16), ((2, rows, weight.shape[2]), BF16), ((2, 16, model), F32),
              ((2, model), F32), ((2, model), F32), ((2, 128), F32)]

    def kernel(at, *refs):
        contrast_kernel(dims, total, at, refs[:len(blocks)], *refs[len(blocks):])

    return pl.pallas_call(
        kernel,
        grid_spec=pltpu.PrefetchScalarGridSpec(
            num_scalar_prefetch=1, grid=(1,),
            in_specs=[spec_whole(v) for v in args],
            out_specs=[pl.BlockSpec(s, lambda i, o, n=len(s): (0,) * n) for s, _ in shapes],
            scratch_shapes=[pltpu.VMEM((2, rows, model), F32)] * 2,
        ),
        out_shape=[jax.ShapeDtypeStruct(s, t) for s, t in shapes],
        compiler_params=params(),
        cost_estimate=pl.CostEstimate(flops=1_000_000_000, bytes_accessed=5_000_000, transcendentals=0),
        name="contrast",
    )(at, *args)


def contrast_large(dims, total, at, blocks, vec, weight, scale):
    model = weight.shape[1]
    held = jnp.concatenate(blocks)
    held = held[jnp.arange(held.shape[0]) ^ at[0]]
    rows = jnp.asarray([r for r in range(16) if r % 4 < dims.quarter])
    cls = jnp.transpose(held[:, :, rows], (1, 0, 2, 3)).reshape(2, -1, model)
    gain, shift = vec[H_GAIN:H_GAIN + 2, None], vec[H_SHIFT:H_SHIFT + 2, None]
    n, r = normalise(cls)
    head_in = (n * gain + shift).astype(BF16)
    proj = jnp.einsum("mrc,mce->mre", head_in, weight, preferred_element_type=F32)
    unit = lax.rsqrt(jnp.sum(proj * proj, axis=-1, keepdims=True) + 1e-6)
    embed = (proj * unit).astype(BF16)
    sharp = jnp.exp(scale[0, 0])
    logits = sharp * dot_t(embed[0], embed[1])
    row_lse = jax.nn.logsumexp(logits, axis=1, keepdims=True)
    col_lse = jax.nn.logsumexp(logits, axis=0, keepdims=True)
    dlogits = jnp.exp(logits - row_lse) + jnp.exp(logits - col_lse) - 2.0 * jnp.eye(total, dtype=F32)
    dlogits = dlogits / (2 * total)
    loss = (jnp.sum(row_lse) + jnp.sum(col_lse) - 2.0 * jnp.trace(logits)) / (2 * total)
    slope = jnp.sum(dlogits * logits)
    high = lax.Precision.HIGHEST
    wide = embed.astype(F32)
    dembed = sharp * jnp.stack([
        jnp.dot(dlogits, wide[1], precision=high, preferred_element_type=F32),
        jnp.dot(dlogits.T, wide[0], precision=high, preferred_element_type=F32)])
    dproj = (unit * dembed - unit ** 3 * proj * jnp.sum(proj * dembed, axis=-1, keepdims=True)).astype(BF16)
    dh = jnp.einsum("mre,mce->mrc", dproj, weight, preferred_element_type=F32)
    back = norm_back(n, r, dh * gain)
    pairs = 4 * dims.quarter
    own = lax.dynamic_slice_in_dim(back, at[0] * pairs, pairs, axis=1)
    dcls = jnp.zeros((2, 16, model), F32).at[:, rows].set(own)
    scalars = jnp.broadcast_to(jnp.stack([loss, slope])[:, None], (2, 128))
    return head_in, dproj, dcls, jnp.sum(dh * n, axis=1), jnp.sum(dh, axis=1), scalars


def own_pair(rows_of):
    return lambda i, o: (o[0] * rows_of + i, 0, 0)


def own_call(kernel, dims, name, order, blocks, img, txt, others, outs, scratch):
    model = img.shape[-1]
    block = pl.BlockSpec((1, dims.slab, model), lambda i, o: (i, 0, 0))
    specs = {
        "slab": (block, (dims.quarter, dims.slab, model)),
        "img": (pl.BlockSpec((1, dims.patches, model), lambda i, o: (i, 0, 0)), (dims.quarter, dims.patches, model)),
        "txt": (pl.BlockSpec((1, dims.caption, model), lambda i, o: (i, 0, 0)), (dims.quarter, dims.caption, model)),
        "sums": (pl.BlockSpec((8, model), lambda i, o: (0, 0)), (8, model)),
    }
    return pl.pallas_call(
        functools.partial(kernel, dims),
        grid_spec=pltpu.PrefetchScalarGridSpec(
            num_scalar_prefetch=1,
            grid=(dims.quarter,),
            in_specs=[block] * len(blocks) + [
                pl.BlockSpec((1, dims.patches, model), own_pair(dims.quarter)),
                pl.BlockSpec((1, dims.caption, model), own_pair(dims.quarter)),
            ] + [spec_whole(v) for v in others],
            out_specs=[specs[kind][0] for kind, _ in outs],
            scratch_shapes=[pltpu.VMEM((dims.slab, model), F32)] * scratch,
        ),
        out_shape=[jax.ShapeDtypeStruct(specs[kind][1], dtype) for kind, dtype in outs],
        compiler_params=params(),
        cost_estimate=pl.CostEstimate(flops=40_000_000, bytes_accessed=15_000_000, transcendentals=0),
        name=name,
    )(order, *blocks, img, txt, *others)


def start_own(rows, sums):
    @pl.when(pl.program_id(0) == 0)
    def _():
        rows[...] = jnp.zeros_like(rows)
        sums[...] = jnp.zeros_like(sums)


def add_class(dims, dcls, rows):
    i = pl.program_id(0)
    rows[0:1, :] += dcls[i, 0:1, :]
    rows[dims.ip:dims.ip + 1, :] += dcls[i, 1:2, :]


def final_kernel(dims, order, keep, recv, far, attended, img, txt, dcls, vec, fin_img, fin_txt, sums, rows):
    start_own(rows, sums)
    load_rows(dims, 0, img, txt, rows)
    add_class(dims, dcls, rows)
    for m, lo, hi in ((0, 0, dims.ip), (1, dims.ip, dims.slab)):
        b = keep[0, lo:hi].astype(F32) + recv[0, lo:hi].astype(F32) + far[0, lo:hi].astype(F32)
        b = b + vector(vec, F_BIAS + m)
        f = attended[0, lo:hi, :] + vector(vec, F_SCALE) * b
        if m == 0:
            fin_img[0] = f[0:dims.patches].astype(BF16)
        else:
            fin_txt[0] = f[0:dims.caption].astype(BF16)
        g = rows[lo:hi, :]
        sums[0:1, :] += jnp.sum(g * b, axis=0, keepdims=True)
        sums[1 + m:2 + m, :] += jnp.sum(g, axis=0, keepdims=True) * vector(vec, F_SCALE)


def final_rows(dims, order, keep, recv, far, attended, img, txt, dcls, vec):
    return own_call(final_kernel, dims, "final_rows", order, (keep, recv, far, attended), img, txt,
                    (dcls, vec), (("img", BF16), ("txt", BF16), ("sums", F32)), 1)


def norm_two_kernel(dims, order, keep, recv, far, attended, a_keep, a_recv, img, txt, dcls, x0, x1, x2, x3,
                    vec, dattended, dattn, sums, rows, ups):
    i = pl.program_id(0)
    start_own(rows, sums)
    load_rows(dims, 0, img, txt, rows)
    add_class(dims, dcls, rows)
    ups[...] = keep[0].astype(F32) + recv[0].astype(F32) + far[0].astype(F32)
    for m, at in ((0, 0), (1, dims.ip)):
        extra = [x[m, pl.ds(own_row(dims, r, 0) + i, 1), :] for x, r in ((x0, 0), (x1, 2), (x2, 1), (x3, 3))]
        ups[at:at + 1, :] += (extra[0] + extra[1]) + (extra[2] + extra[3])
    for m, lo, hi in ((0, 0, dims.ip), (1, dims.ip, dims.slab)):
        n, r = normalise(attended[0, lo:hi, :])
        dy = ups[lo:hi, :]
        sums[m:m + 1, :] += jnp.sum(dy * n, axis=0, keepdims=True)
        sums[2 + m:3 + m, :] += jnp.sum(dy, axis=0, keepdims=True)
        d = rows[lo:hi, :] + norm_back(n, r, dy * vector(vec, GAIN2 + m))
        dattended[0, lo:hi, :] = d
        sd = d * vector(vec, A_SCALE)
        dattn[0, lo:hi, :] = sd.astype(BF16)
        a = a_keep[0, lo:hi, :].astype(F32) + a_recv[0, lo:hi, :].astype(F32) + vector(vec, A_BIAS)
        sums[4:5, :] += jnp.sum(d * a, axis=0, keepdims=True)
        sums[5:6, :] += jnp.sum(sd, axis=0, keepdims=True)


def norm_two(dims, order, keep, recv, far, attended, a_keep, a_recv, img, txt, dcls, parts, vec):
    return own_call(norm_two_kernel, dims, "norm_two", order, (keep, recv, far, attended, a_keep, a_recv), img, txt,
                    (dcls,) + tuple(parts) + (vec,), (("slab", F32), ("slab", BF16), ("sums", F32)), 2)


def norm_one_kernel(dims, order, keep, recv, dattended, img, txt, vec, d_img, d_txt, sums, rows):
    start_own(rows, sums)
    load_rows(dims, 0, img, txt, rows)
    n, r = normalise(rows[...])
    dy = keep[0].astype(F32) + recv[0].astype(F32)
    sums[0:1, :] += jnp.sum(dy * n, axis=0, keepdims=True)
    sums[1:2, :] += jnp.sum(dy, axis=0, keepdims=True)
    d = dattended[0] + norm_back(n, r, dy * vector(vec, GAIN1))
    d_img[0] = d[0:dims.patches].astype(BF16)
    d_txt[0] = d[dims.ip:dims.ip + dims.caption].astype(BF16)


def norm_one(dims, order, keep, recv, dattended, img, txt, vec):
    return own_call(norm_one_kernel, dims, "norm_one", order, (keep, recv, dattended), img, txt,
                    (vec,), (("img", BF16), ("txt", BF16), ("sums", F32)), 1)


def back_step(dims, tiles, lens, whose, dattn, normed, qkv, mixed, dmixed, dqkv, acc, col_sums, w, ow):
    quarter, slab = dims.quarter, dims.slab
    count, width = quarter * slab, tiles * 128
    model = normed.shape[-1]
    d_rows = dattn[...].reshape(count, model)
    dmixed[...] = dot_t(d_rows, ow[...]).astype(BF16).reshape(quarter, slab, width)

    def one_pair(p, c):
        length = lens[whose * quarter + p]
        for lo, hi, start, limit in key_tail(dims, length):
            for g in range(tiles):
                at = [slice((t * tiles + g) * 128, (t * tiles + g + 1) * 128) for t in range(3)]
                q, k, v = [qkv[p, lo:hi, c] for c in at]
                q = scaled(q)
                qq = split_pair(q)
                dd = split_pair(dmixed[p, lo:hi, g * 128:(g + 1) * 128])
                w_ = softmax_keys(hide(dot_t(k, qq), start, limit))
                dw = dot_t(v, dd)
                dqkv[p, lo:hi, at[2]] = dot(w_.astype(BF16), dd).astype(BF16)
                ds = (w_ * (dw - jnp.sum(w_ * dw, axis=0, keepdims=True))).astype(BF16)
                dqkv[p, lo:hi, at[1]] = dot(ds, qq).astype(BF16)
                dqkv[p, lo:hi, at[0]] = (join_pair(t_dot(ds, k)) * HEAD_DIM ** -0.5).astype(BF16)
        return c

    lax.fori_loop(0, quarter, one_pair, 0)
    dp = dqkv[...].reshape(count, 3 * width)
    part = dot(dp, w[...])
    acc[:, 0:3 * width] += t_dot(normed[...].reshape(count, model), dp)
    acc[:, 3 * width:] += t_dot(d_rows, mixed[...].reshape(count, width))
    col_sums[...] += jnp.sum(dp.astype(F32), axis=0, keepdims=True)
    return part


def attend_back_kernel(dims, far, order, lens, d_own, d_peer, normed, qkv, mixed, wq, wo, wf, *refs):
    if not far:
        prior_keep, prior_send, *refs = refs
    keep, send, grad, *refs = refs
    if far:
        grad_rest, *refs = refs
    col_sums, dattn, dmixed, dqkv, acc, w, ow = refs
    i = pl.program_id(0)
    slab, quarter, local = dims.slab, dims.quarter, dims.local
    two, one_head = parts_of(dims)
    tiles = 2 if far else 1
    width = tiles * two
    count = quarter * slab
    model = normed.shape[-1]

    @pl.when(i == 0)
    def _():
        dattn[...] = d_own[...]
        acc[...] = jnp.zeros_like(acc)
        col_sums[...] = jnp.zeros_like(col_sums)
        for t in range(4):
            dst, at = (w, t * width) if t < 3 else (ow, 0)
            own, start = (wq, t * local) if t < 3 else (wo, 0)
            if far:
                copy_rows(dst, at, wf, t * local, two)
                copy_rows(dst, at + two, own, start + two, one_head)
                copy_rows(dst, at + two + one_head, wf, t * local + two, one_head)
            else:
                copy_rows(dst, at, own, start, two)

    @pl.when(i == 1)
    def _():
        dattn[...] = d_peer[...]

    part = back_step(dims, tiles, lens, order[2 * i], dattn, normed, qkv, mixed,
                     dmixed, dqkv, acc, col_sums, w, ow)

    @pl.when(i == 0)
    def _():
        prior = 0.0 if far else prior_keep[...].reshape(count, model).astype(F32)
        keep[...] = (part + prior).astype(BF16).reshape(quarter, slab, model)

    @pl.when(i == 1)
    def _():
        prior = 0.0 if far else prior_send[...].reshape(count, model).astype(F32)
        send[...] = (part + prior).astype(BF16).reshape(quarter, slab, model)
        for t in range(4):
            grad[:, t * two:(t + 1) * two] = acc[:, t * width:t * width + two].astype(BF16)
            if far:
                at = t * width + two
                to = 4 * two + t * one_head
                grad[:, to:to + one_head] = acc[:, at + one_head:at + two].astype(BF16)
                grad_rest[:, t * one_head:(t + 1) * one_head] = acc[:, at:at + one_head].astype(BF16)


def attend_back(dims, far, order, lens, d_own, d_peer, normed, qkv, mixed, wq, wo, wf, prior=()):
    model = normed.shape[-1]
    slab, quarter = dims.slab, dims.quarter
    width = 256 if far else 128
    one = pl.BlockSpec((quarter, slab, model), lambda i, o, n: (0, 0, 0))
    stride = normed.shape[0] // (2 * quarter)
    step = lambda cols: pl.BlockSpec((quarter, slab, cols), lambda i, o, n: (stride * i, 0, 0))
    grads = (768, 256) if far else (512,)
    specs = [one, one] + [pl.BlockSpec((model, n), lambda i, o, n_: (0, 0)) for n in grads]
    specs += [pl.BlockSpec((1, 3 * width), lambda i, o, n: (0, 0))]
    shapes = [
        jax.ShapeDtypeStruct((quarter, slab, model), BF16),
        jax.ShapeDtypeStruct((quarter, slab, model), BF16),
    ] + [jax.ShapeDtypeStruct((model, n), BF16) for n in grads] + [jax.ShapeDtypeStruct((1, 3 * width), F32)]
    scratch = [
        pltpu.VMEM((quarter, slab, model), BF16),
        pltpu.VMEM((quarter, slab, width), BF16),
        pltpu.VMEM((quarter, slab, 3 * width), BF16),
        pltpu.VMEM((model, 4 * width), F32),
        pltpu.VMEM((3 * width, model), BF16),
        pltpu.VMEM((width, model), BF16),
    ]
    return pl.pallas_call(
        functools.partial(attend_back_kernel, dims, far),
        grid_spec=pltpu.PrefetchScalarGridSpec(
            num_scalar_prefetch=2,
            grid=(2,),
            in_specs=[one, one, step(model), step(3 * width), step(width), spec_whole(wq), spec_whole(wo),
                      spec_whole(wf)] + [one] * len(prior),
            out_specs=specs,
            scratch_shapes=scratch,
        ),
        out_shape=shapes,
        compiler_params=params(),
        cost_estimate=pl.CostEstimate(
            flops=32 * quarter * slab * model * width, bytes_accessed=20_000_000, transcendentals=0),
        name="attend_back_far" if far else "attend_back_own",
    )(order, lens, d_own, d_peer, normed, qkv, mixed, wq, wo, wf, *prior)


def swap(value, axis, bit):
    size = lax.axis_size(axis)
    return lax.ppermute(value, axis, [(j, j ^ bit) for j in range(size)])


def to_core(value):
    return swap(value, "mp", 1)


def to_y(value):
    return swap(value, "mp", 2)


def from_others(value, axis, first, count):
    return [value] + [swap(value, axis, k * first) for k in range(1, count)]


def add_tree(parts):
    while len(parts) > 1:
        parts = [a + b for a, b in zip(parts[::2], parts[1::2])]
    return parts[0]


def sum_over(value, axis):
    first = 1
    while first < lax.axis_size(axis):
        count = min(8, lax.axis_size(axis) // first)
        value = add_tree(from_others(value, axis, first, count))
        first *= count
    return value


def gather_batch(value):
    parts = [value]
    first = 1
    size = lax.axis_size("batch")
    while first < size:
        count = min(8, size // first)
        whole = jnp.concatenate(parts) if len(parts) > 1 else parts[0]
        parts = from_others(whole, "batch", first, count)
        first *= count
    return parts


def gather_rows(own, me):
    near = jnp.stack([own, to_y(own)])
    far = to_core(near)
    out = jnp.zeros((4,) + own.shape, own.dtype)
    for r, value in enumerate((near[0], near[1], far[0], far[1])):
        out = lax.dynamic_update_slice(out, value[None], (me ^ ORDER[r],) + (0,) * own.ndim)
    return out.reshape((4 * own.shape[0],) + own.shape[1:])


def add_low(a, b):
    return (a.astype(F32) + b.astype(F32)).astype(BF16)


MESH = pl.DeviceIdType.MESH


class Place:
    def __init__(self):
        self.b, self.m = lax.axis_index("batch"), lax.axis_index("mp")
        self.z, self.x = self.b // 2, self.b % 2
        self.y, self.c = self.m // 2, self.m % 2
        self.core = (self.b, 2 * self.y + 1 - self.c)
        self.near = (self.b, 2 * (1 - self.y) + self.c)
        self.across = (self.b, 2 * (1 - self.y) + 1 - self.c)
        self.side = (2 * self.z + 1 - self.x, self.m)
        self.along = [(2 * ((self.z + k) % 4) + self.x, self.m) for k in range(1, 4)]
        self.batch = [((self.b + k) % 8, self.m) for k in range(1, 8)]

    def quarter(self, far_y, far_core):
        return 2 * ((self.y + far_y) % 2) + (self.c + far_core) % 2


def meet(peers):
    barrier = pltpu.get_barrier_semaphore()
    for peer in peers:
        pl.semaphore_signal(barrier, inc=1, device_id=peer, device_id_type=MESH)
    pl.semaphore_wait(barrier, len(peers))


def remote(src, dst, send_sem, recv_sem, at, device):
    return pltpu.make_async_remote_copy(
        src_ref=src, dst_ref=dst, send_sem=send_sem.at[at], recv_sem=recv_sem.at[at],
        device_id=device, device_id_type=MESH)


def front_kernel(dims, lens, img, txt, vectors, bias, own_w, own_o,
                 vec, normed, qkv, mixed, qkv_far, mixed_far, far_w, attended, attn, expert, expert_peer, cls, cls_peer,
                 rows, w, w2, ow, b, wf, far_bias, n_all, rest, m_all, m_far, q_own, q_far, a_send, a_recv, e_send, c_recv,
                 local_sem, send_sem, recv_sem):
    here = Place()
    i = pl.program_id(0)
    local, quarter, slab, ip = dims.local, dims.quarter, dims.slab, dims.ip
    two, one_head = parts_of(dims)
    count = quarter * slab
    model = img.shape[-1]
    at = i % 4
    whose = here.quarter(at % 2, 1 - at // 2)
    sent_w = [remote(own_w, wf.at[pl.ds(0, 3 * local)], send_sem, recv_sem, 0, here.near),
              remote(own_o, wf.at[pl.ds(3 * local, local)], send_sem, recv_sem, 1, here.near),
              remote(bias, far_bias, send_sem, recv_sem, 2, here.near)]
    sent_a = [remote(a_send.at[j], a_recv.at[j], send_sem, recv_sem, 3 + j, here.core) for j in range(2)]

    def e_over(j):
        return remote(e_send.at[j], expert_peer.at[j], send_sem, recv_sem, 5 + j, here.core)

    def e_here(j):
        return pltpu.make_async_copy(e_send.at[j], expert.at[j], local_sem.at[1 + j])

    sent_c = remote(cls, c_recv, send_sem, recv_sem, 5 + 2 * quarter, here.core)
    keep_w = pltpu.make_async_copy(wf, far_w, local_sem.at[0])
    sent_e = [e_over(j) for j in range(2 * quarter)]
    keep_e = [e_here(j) for j in range(2 * quarter)]

    @pl.when(i == 0)
    def _():
        meet([here.core, here.near])
        for copy in sent_w:
            copy.start()
        fill(vec, vectors)
        rows[...] = jnp.zeros_like(rows)
        b[...] = jnp.zeros_like(b)
        w[...] = jnp.zeros_like(w)
        cls[...] = jnp.zeros_like(cls)
        for t in range(3):
            copy_rows(w, t * 2 * two, own_w, t * local, local)
        b[0:1, 0:local] = bias[0:1, :]
        b[0:1, 4 * two:4 * two + local] = bias[1:2, :]

    def project(weights):
        proj = dot_t(n_all[at].reshape(count, model), weights[...]) + b[0:1, :]
        return proj.astype(BF16).reshape(quarter, slab, 6 * two)

    @pl.when(i < 4)
    def _():
        def one_norm(p, c):
            load_rows(dims, p, img, txt, rows)
            n, _ = normalise(rows[...])
            n_all[at, p] = (n * vector(vec, GAIN1) + vector(vec, SHIFT1)).astype(BF16)
            return c

        lax.fori_loop(0, quarter, one_norm, 0)
        proj = project(w)
        for t in range(3):
            q_own[:, :, t * two:(t + 1) * two] = proj[:, :, 2 * t * two:(2 * t + 1) * two]
            rest[at, :, :, t * two:(t + 1) * two] = proj[:, :, (2 * t + 1) * two:(2 * t + 2) * two]
        attend_tiles(dims, lens, whose, q_own, m_all.at[at])

        @pl.when(i % 2 == 0)
        def _():
            normed[...] = n_all[at]
            qkv[...] = q_own[...]
            mixed[...] = m_all[at]

    @pl.when(i == 4)
    def _():
        for copy in sent_w:
            copy.wait_recv()
        keep_w.start()
        w2[...] = jnp.zeros_like(w2)
        b[...] = jnp.zeros_like(b)
        for t in range(3):
            copy_rows(w2, t * 2 * two, wf, t * local, two)
            copy_rows(w2, t * 2 * two + two + one_head, wf, t * local + two, one_head)
        for t, to in ((0, 0), (1, 4 * two)):
            b[0:1, to:to + two] = far_bias[t:t + 1, 0:two]
            b[0:1, to + two + one_head:to + 2 * two] = far_bias[t:t + 1, two:]
        copy_rows(ow, 0, own_o, 0, two)
        copy_rows(ow, two, wf, 3 * local, two)
        copy_rows(ow, 2 * two, own_o, two, one_head)
        copy_rows(ow, 2 * two + one_head, wf, 3 * local + two, one_head)

    @pl.when(i >= 4)
    def _():
        proj = project(w2)
        for t in range(3):
            to = 2 * t * two
            q_far[:, :, to:to + two] = proj[:, :, to:to + two]
            q_far[:, :, to + two:to + 2 * two] = (
                proj[:, :, to + two:to + 2 * two] + rest[at, :, :, t * two:(t + 1) * two])
        attend_tiles(dims, lens, whose, q_far, m_far)

        @pl.when(i % 2 == 0)
        def _():
            qkv_far[...] = q_far[...]
            mixed_far[...] = m_far[...]

        part = dot(m_all[at].reshape(count, two), ow[0:two, :])
        part = part + dot(m_far[...].reshape(count, 2 * two), ow[two:, :])
        part = part.reshape(quarter, slab, model)

        @pl.when(i < 6)
        def _():
            a_send[at] = part.astype(BF16)

        for j in range(2):
            @pl.when(i == 4 + j)
            def _():
                sent_a[j].start()

        for j in range(2):
            @pl.when(i == 6 + j)
            def _():
                sent_a[j].wait_recv()

        @pl.when(i >= 6)
        def _():
            j = i - 6
            for p in range(quarter):
                load_rows(dims, p, img, txt, rows)
                a = part[p] + a_recv[j, p].astype(F32)
                x = rows[...] + vector(vec, A_SCALE) * (a + vector(vec, A_BIAS))
                n, _ = normalise(x)
                e_img = n[0:ip] * vector(vec, GAIN2) + vector(vec, SHIFT2)
                e_txt = n[ip:] * vector(vec, GAIN2 + 1) + vector(vec, SHIFT2 + 1)
                r = j * quarter + p
                e_send[r, 0:ip, :] = e_img.astype(BF16)
                e_send[r, ip:, :] = e_txt.astype(BF16)
                e_over(r).start()
                e_here(r).start()
                for k, v in enumerate((x[0:1], x[ip:ip + 1], e_img[0:1], e_txt[0:1])):
                    cls[k, pl.ds(r, 1), :] = v

                @pl.when(j == 0)
                def _():
                    attended[p] = x
                    attn[p] = a


    @pl.when(i == 7)
    def _():
        sent_c.start()
        keep_w.wait()
        for copy in keep_e:
            copy.wait()
        sent_c.wait()
        cls_peer[...] = c_recv[...]
        for copy in sent_e:
            copy.wait()
        for copy in sent_w + sent_a:
            copy.wait_send()


def fill(table, vectors):
    table[...] = jnp.zeros_like(table)
    at = 0
    for v in vectors:
        n = v.shape[0] if len(v.shape) == 2 else 1
        table[at:at + n, :] = v[...].reshape(n, table.shape[1])
        at += n


def front(dims, lens, img, txt, vectors, bias, own_w, own_o):
    model = img.shape[-1]
    quarter, slab, local = dims.quarter, dims.slab, dims.local
    held = pl.BlockSpec(memory_space=pltpu.VMEM)
    away = pl.BlockSpec(memory_space=pl.ANY)

    def states_at(i):
        return Place().quarter(i % 2, 1 - i % 4 // 2), 0, 0

    own_block = lambda cols: pl.BlockSpec((quarter, slab, cols), lambda i: (jnp.where(i < 2, 1, 0), 0, 0))
    far_block = lambda cols: pl.BlockSpec((quarter, slab, cols), lambda i: (jnp.where(i < 6, 1, 0), 0, 0))
    six = lambda cols: jax.ShapeDtypeStruct((2 * quarter, slab, cols), BF16)
    block = lambda cols: (quarter, slab, cols)
    n_remote = 6 + 2 * quarter
    return pl.pallas_call(
        lambda lens, img, txt, *refs: front_kernel(
            dims, lens, img, txt, refs[:len(vectors)], *refs[len(vectors):]),
        grid=(8,),
        in_specs=[pl.BlockSpec(memory_space=pltpu.SMEM),
                  pl.BlockSpec((quarter, dims.patches, model), states_at),
                  pl.BlockSpec((quarter, dims.caption, model), states_at)] + [held] * (3 + len(vectors)),
        out_specs=[held, own_block(model), own_block(384), own_block(128), far_block(768), far_block(256),
                   away, held, held, away, away, held, held],
        out_shape=[jax.ShapeDtypeStruct((16, model), F32), six(model), six(384), six(128), six(768), six(256),
                   jax.ShapeDtypeStruct((4 * local, model), BF16),
                   jax.ShapeDtypeStruct(block(model), F32), jax.ShapeDtypeStruct(block(model), F32),
                   six(model), six(model),
                   jax.ShapeDtypeStruct((4, 8, model), F32), jax.ShapeDtypeStruct((4, 8, model), F32)],
        scratch_shapes=[
            pltpu.VMEM((slab, model), F32), pltpu.VMEM((768, model), BF16), pltpu.VMEM((768, model), BF16),
            pltpu.VMEM((384, model), BF16), pltpu.VMEM((8, 768), F32), pltpu.VMEM((4 * local, model), BF16),
            pltpu.VMEM((2, local), F32),
            pltpu.VMEM((4,) + block(model), BF16), pltpu.VMEM((4,) + block(384), BF16),
            pltpu.VMEM((4,) + block(128), BF16), pltpu.VMEM(block(256), BF16),
            pltpu.VMEM(block(384), BF16), pltpu.VMEM(block(768), BF16),
            pltpu.VMEM((2,) + block(model), BF16), pltpu.VMEM((2,) + block(model), BF16),
            pltpu.VMEM((2 * quarter, slab, model), BF16), pltpu.VMEM((4, 8, model), F32),
            pltpu.SemaphoreType.DMA((1 + 2 * quarter,)),
            pltpu.SemaphoreType.DMA((n_remote,)), pltpu.SemaphoreType.DMA((n_remote,)),
        ],
        compiler_params=params(collective_id=6, has_side_effects=True),
        cost_estimate=pl.CostEstimate(
            flops=16 * quarter * slab * model * 1152, bytes_accessed=40_000_000, transcendentals=0),
        name="front",
    )(lens, img, txt, *vectors, bias, own_w, own_o)


def middle_kernel(dims, total, img, txt, own, peer, cls_own, cls_peer, vec, up, up_bias, down, weight, scale,
                  act, dup, ddn, dexp, d_own, d_near, bias_grad, class_e, c_act, c_dup, c_ddn, dcls,
                  head_in, dproj, gains, shifts, scalars,
                  bx, bd, rx, rd, x_near, x_far, ins, rows, part, parts, cls, back, cot, c_rows, extra, extras,
                  send_sem, recv_sem):
    here = Place()
    ip, slab, quarter = dims.ip, dims.slab, dims.quarter
    i = pl.program_id(0)
    model = own.shape[-1]
    mp_peers = [here.core, here.near, here.across]
    of = [here.quarter(0, 0), here.quarter(1, 0), here.quarter(0, 1), here.quarter(1, 1)]

    sent_x = [remote(bx.at[2 * j], rx.at[j], send_sem, recv_sem, j, here.core) for j in range(2)]
    sent_d = [remote(bd.at[2 * j], rd.at[j], send_sem, recv_sem, 2 + j, here.core) for j in range(2)]
    sent_near = remote(x_near, x_far, send_sem, recv_sem, 4, here.near)
    sent_part = [remote(part, parts.at[k], send_sem, recv_sem, 5 + k, mp_peers[k]) for k in range(3)]
    sent_extra = [remote(extra, extras.at[k], send_sem, recv_sem, 8 + k, mp_peers[k]) for k in range(3)]
    sent_cls = [remote(cls.at[here.b], cls.at[here.b], send_sem, recv_sem, 11 + k, here.batch[k]) for k in range(7)]

    @pl.when(i == 0)
    def _():
        rows[...] = jnp.zeros_like(rows)
        bias_grad[...] = jnp.zeros_like(bias_grad)
        for m in range(2):
            e = jnp.concatenate([cls_own[2 + m], cls_peer[2 + m]], axis=0).astype(BF16)
            class_e[m] = e
            u = dot(e, up[m]) + up_bias[m:m + 1]
            part[m] = dot(gelu_low(u), down[m])
        meet(mp_peers + here.batch)
        for copy in sent_part:
            copy.start()
        ins[...] = peer[quarter:, :, :]

    @pl.when(i == 1)
    def _():
        for copy in sent_part:
            copy.wait_recv()
        for m in range(2):
            cls[here.b, m] = jnp.zeros(cls.shape[2:], F32)
            for r in range(4):
                half, at = (cls_own, cls_peer)[r // 2], quarter * (r % 2)
                for p in range(quarter):
                    line = [d[m, own_row(dims, s, p):own_row(dims, s, p) + 1, :]
                            for d, s in ((part, r), (parts.at[0], r ^ 2), (parts.at[1], r ^ 1), (parts.at[2], r ^ 3))]
                    x = (line[0] + line[1]) + (line[2] + line[3]) + vector(vec, F_BIAS + m)
                    x = half[m, at + p:at + p + 1, :] + vector(vec, F_SCALE) * x
                    cls[here.b, m, pl.ds(4 * of[r] + p, 1), :] = x
        for copy in sent_cls:
            copy.start()
        ins[...] = own[quarter:, :, :]

    @pl.when(i == 2)
    def _():
        ins[...] = peer[:quarter, :, :]

    @pl.when(i == 3)
    def _():
        ins[...] = own[:quarter, :, :]
        for copy in sent_cls:
            copy.wait_recv()
        n_rows = 16 * cls.shape[0]
        sharp = jnp.exp(scale[...])
        col_at = lax.broadcasted_iota(jnp.int32, (1, n_rows), 1)
        row_at = lax.broadcasted_iota(jnp.int32, (n_rows, 1), 0)
        col_ok = (col_at % 4) < quarter
        row_ok = (row_at % 4) < quarter
        normal, inverse, proj, unit, embed = [], [], [], [], []
        for m in range(2):
            n, r = normalise(cls[:, m].reshape(n_rows, model))
            h = (n * vector(vec, H_GAIN + m) + vector(vec, H_SHIFT + m)).astype(BF16)
            head_in[m] = h
            y = dot(h, weight[m])
            u = lax.rsqrt(jnp.sum(y * y, axis=-1, keepdims=True) + 1e-6)
            normal.append(n)
            inverse.append(r)
            proj.append(y)
            unit.append(u)
            embed.append((y * u).astype(BF16))
        ok = row_ok & col_ok
        logits = sharp * dot_t(embed[0], embed[1])
        masked = jnp.where(ok, logits, -1e30)
        row_max = jnp.max(masked, axis=1, keepdims=True)
        row_lse = row_max + jnp.log(jnp.sum(jnp.exp(masked - row_max), axis=1, keepdims=True))
        col_max = jnp.max(masked, axis=0, keepdims=True)
        col_lse = col_max + jnp.log(jnp.sum(jnp.exp(masked - col_max), axis=0, keepdims=True))
        same = (row_at == col_at) & ok
        both = jnp.exp(masked - row_lse) + jnp.exp(masked - col_lse)
        dlogits = jnp.where(ok, jnp.where(same, both - 2.0, both) * (1.0 / (2 * total)), 0.0)
        diagonal = jnp.sum(jnp.where(same, logits, 0.0), axis=1, keepdims=True)
        lines = jnp.sum(jnp.where(row_ok, row_lse - 2.0 * diagonal, 0.0), axis=0, keepdims=True)
        lines = lines + jnp.sum(jnp.where(col_ok, col_lse, 0.0), axis=1, keepdims=True)
        slope = jnp.sum(jnp.sum(dlogits * logits, axis=1, keepdims=True), axis=0, keepdims=True)
        scalars[0:1, :] = jnp.broadcast_to(lines * (1.0 / (2 * total)), (1, 128))
        scalars[1:2, :] = jnp.broadcast_to(slope, (1, 128))
        high = lax.Precision.HIGHEST
        wide = [e.astype(F32) for e in embed]
        dembed = [
            sharp * jnp.dot(dlogits, wide[1], precision=high, preferred_element_type=F32),
            sharp * lax.dot_general(dlogits, wide[0], (((0,), (0,)), ((), ())), precision=high,
                                    preferred_element_type=F32),
        ]
        c_rows[...] = jnp.zeros_like(c_rows)
        dcls[...] = jnp.zeros_like(dcls)
        for m in range(2):
            for p in range(quarter):
                src = (img, txt)[m]
                cot[m, 8 * 3 + p:8 * 3 + p + 1, :] = src[p, 0:1, :].astype(F32)
        for m in range(2):
            u, y, d = unit[m], proj[m], dembed[m]
            dp = (u * d - u * u * u * y * jnp.sum(y * d, axis=-1, keepdims=True)).astype(BF16)
            dproj[m] = dp
            dh = dot_t(dp, weight[m])
            gains[m:m + 1, :] = jnp.sum(dh * normal[m], axis=0, keepdims=True)
            shifts[m:m + 1, :] = jnp.sum(dh, axis=0, keepdims=True)
            back[m] = norm_back(normal[m], inverse[m], dh * vector(vec, H_GAIN + m))
            for r in range(4):
                step = (3, 1, 2, 0)[r]
                for p in range(quarter):
                    g = back[m, pl.ds(16 * here.b + 4 * of[r] + p, 1), :]
                    at = own_row(dims, r, p)
                    c_rows[m, at:at + 1, :] = cot[m, 8 * step + p:8 * step + p + 1, :] + g
                    if r == 0:
                        dcls[p, m:m + 1, :] = g
            u = dot(class_e[m], up[m]) + up_bias[m:m + 1]
            big, small = gelu_parts(u)
            c_act[m] = (u * big).astype(BF16)
            g = (c_rows[m] * vector(vec, F_SCALE)).astype(BF16)
            c_ddn[m] = g
            du = dot_t(g, down[m]) * (big + u * small)
            bias_grad[m:m + 1, :] += jnp.sum(du, axis=0, keepdims=True)
            low = du.astype(BF16)
            c_dup[m] = low
            extra[m] = dot_t(low, up[m])
        for copy in sent_extra:
            copy.start()

    at = lax.broadcasted_iota(jnp.int32, (slab, 1), 0)
    inner = (at != 0) & (at != ip)

    def one(p, c):
        load_rows(dims, p, img, txt, rows)
        cot[0, pl.ds(8 * i + p, 1), :] = rows[0:1, :]
        cot[1, pl.ds(8 * i + p, 1), :] = rows[ip:ip + 1, :]
        ddn[p] = jnp.where(inner, rows[...] * vector(vec, F_SCALE), 0.0).astype(BF16)
        return c

    lax.fori_loop(0, quarter, one, 0)
    for m, lo, hi in ((0, 0, ip), (1, ip, slab)):
        count = quarter * (hi - lo)
        e = ins[:, lo:hi, :].reshape(count, model)
        u = dot(e, up[m]) + up_bias[m:m + 1]
        big, small = gelu_parts(u)
        a = (u * big).astype(BF16)
        act[:, lo:hi, :] = a.reshape(quarter, hi - lo, -1)
        slope = big + u * small
        bd[i, :, lo:hi, :] = dot(a, down[m]).astype(BF16).reshape(quarter, hi - lo, model)
        g = ddn[:, lo:hi, :].reshape(count, model)
        du = dot_t(g, down[m]) * slope
        bias_grad[m:m + 1, :] += jnp.sum(du, axis=0, keepdims=True)
        low = du.astype(BF16)
        dup[:, lo:hi, :] = low.reshape(quarter, hi - lo, -1)
        bx[i, :, lo:hi, :] = dot_t(low, up[m]).astype(BF16).reshape(quarter, hi - lo, model)

    for j in range(2):
        @pl.when(i == 2 * j)
        def _():
            sent_x[j].start()
            sent_d[j].start()

    @pl.when(i == 1)
    def _():
        sent_x[0].wait_recv()

        def add_x(p, c):
            x_near[p] = (bx[1, p].astype(F32) + rx[0, p].astype(F32)).astype(BF16)
            return c

        lax.fori_loop(0, quarter, add_x, 0)
        sent_near.start()
        sent_d[0].wait_recv()

        def add_d(p, c):
            d_near[p] = (bd[1, p].astype(F32) + rd[0, p].astype(F32)).astype(BF16)
            return c

        lax.fori_loop(0, quarter, add_d, 0)

    @pl.when(i == 3)
    def _():
        sent_d[1].wait_recv()

        def add_d(p, c):
            d_own[p] = bd[3, p].astype(F32) + rd[1, p].astype(F32)
            return c

        lax.fori_loop(0, quarter, add_d, 0)
        sent_x[1].wait_recv()
        sent_near.wait_recv()

        def add_x(p, c):
            dexp[p] = bx[3, p].astype(F32) + rx[1, p].astype(F32) + x_far[p].astype(F32)
            return c

        lax.fori_loop(0, quarter, add_x, 0)
        for copy in sent_extra:
            copy.wait_recv()
        for m in range(2):
            for p in range(quarter):
                line = [x[m, own_row(dims, r, p):own_row(dims, r, p) + 1, :]
                        for x, r in ((extra, 0), (extras.at[0], 2), (extras.at[1], 1), (extras.at[2], 3))]
                dexp[p, m * ip:m * ip + 1, :] += (line[0] + line[1]) + (line[2] + line[3])
        for copy in sent_x + sent_d + [sent_near] + sent_part + sent_extra + sent_cls:
            copy.wait_send()


def middle(dims, total, img, txt, own, peer, cls_own, cls_peer, vec, up, up_bias, down, weight, scale):
    model = own.shape[-1]
    hidden = up.shape[-1]
    slab, quarter = dims.slab, dims.quarter
    batch = 8

    def cot_at(i):
        here = Place()
        return here.quarter(1 - i // 2, 1 - i % 2), 0, 0

    held = pl.BlockSpec(memory_space=pltpu.VMEM)
    step = lambda cols: pl.BlockSpec((quarter, slab, cols), lambda i: (i, 0, 0))
    rows_of = lambda n, t: jax.ShapeDtypeStruct((n, slab, model), t)
    small = [((quarter, slab, model), F32), ((quarter, slab, model), F32), ((quarter, slab, model), BF16),
             ((2, hidden), F32), ((2, 16, model), BF16), ((2, 16, hidden), BF16), ((2, 16, hidden), BF16),
             ((2, 16, model), BF16), ((quarter, 8, model), F32), ((2, 16 * batch, model), BF16),
             ((2, 16 * batch, weight.shape[2]), BF16), ((2, model), F32), ((2, model), F32), ((2, 128), F32)]
    block = (quarter, slab, model)
    return pl.pallas_call(
        functools.partial(middle_kernel, dims, total),
        grid=(4,),
        in_specs=[pl.BlockSpec((quarter, dims.patches, model), cot_at),
                  pl.BlockSpec((quarter, dims.caption, model), cot_at)] + [held] * 10,
        out_specs=[step(hidden), step(hidden), step(model)] + [held] * len(small),
        out_shape=[rows_of(4 * quarter, BF16)] * 3 + [jax.ShapeDtypeStruct(v, t) for v, t in small],
        scratch_shapes=[
            pltpu.VMEM((4,) + block, BF16), pltpu.VMEM((4,) + block, BF16),
            pltpu.VMEM((2,) + block, BF16), pltpu.VMEM((2,) + block, BF16),
            pltpu.VMEM(block, BF16), pltpu.VMEM(block, BF16), pltpu.VMEM(block, BF16),
            pltpu.VMEM((slab, model), F32),
            pltpu.VMEM((2, 16, model), F32), pltpu.VMEM((3, 2, 16, model), F32),
            pltpu.VMEM((batch, 2, 16, model), F32), pltpu.VMEM((2, 16 * batch, model), F32),
            pltpu.VMEM((2, 32, model), F32), pltpu.VMEM((2, 16, model), F32),
            pltpu.VMEM((2, 16, model), F32), pltpu.VMEM((3, 2, 16, model), F32),
            pltpu.SemaphoreType.DMA((18,)), pltpu.SemaphoreType.DMA((18,)),
        ],
        compiler_params=params(collective_id=2, has_side_effects=True),
        cost_estimate=pl.CostEstimate(
            flops=32 * quarter * slab * model * hidden, bytes_accessed=40_000_000, transcendentals=0),
        name="middle",
    )(img, txt, own, peer, cls_own, cls_peer, vec, up, up_bias, down, weight, scale)


def turn_kernel(dims, img, txt, peer, own, act, dup, ddn, ce, ca, cu, cd, dexp, attended, attn, d_own, d_near, dcls, vec,
                down_sum, up_keep, up_send, dattended, dattn, dattn_peer, fin_img, fin_txt, sums,
                acc, d_far, n_peer, rows, side_send, side_recv, e_in, dexp_in, attended_in, attn_in, d_own_in,
                local_sem, send_sem, recv_sem):
    here = Place()
    quarter, ip = dims.quarter, dims.ip
    i = pl.program_id(0)
    piece = side_send.shape[2]
    sent_near = remote(d_near, d_far, send_sem, recv_sem, 0, here.near)
    sent_core = [remote(dattn.at[p], n_peer.at[p], send_sem, recv_sem, 1 + p, here.core) for p in range(quarter)]
    sent_side = [remote(side_send.at[j], side_recv.at[j], send_sem, recv_sem, 1 + quarter + j, here.side)
                 for j in range(4)]
    loaded = [pltpu.make_async_copy(src, dst, local_sem.at[j]) for j, (src, dst) in enumerate((
        (dexp, dexp_in), (attended, attended_in), (attn, attn_in), (d_own, d_own_in)))]
    dexp, attended, attn, d_own = dexp_in, attended_in, attn_in, d_own_in
    spans = ((0, 0, ip), (1, ip, dims.slab))
    flat = lambda v: v.reshape(-1, v.shape[-1])
    block = lambda j: pl.ds(pl.multiple_of(j * piece, piece), piece)

    @pl.when(i == 0)
    def _():
        meet([here.core, here.near, here.side])
        sent_near.start()
        for copy in loaded:
            copy.start()
        for m in range(2):
            acc[m] = t_dot(cd[m], ca[m])

    @pl.when(i < 4)
    def _():
        for m, lo, hi in spans:
            acc[m] += t_dot(flat(ddn[:, lo:hi, :]), flat(act[:, lo:hi, :]))

    @pl.when(i == 3)
    def _():
        for j in range(4):
            for m in range(2):
                side_send[j, m] = acc[m, block(2 * j + 1 - here.x), :].astype(BF16)
                down_sum[j, m] = acc[m, block(2 * j + here.x), :].astype(BF16)
            sent_side[j].start()

    @pl.when(i == 4)
    def _():
        for m in range(2):
            acc[m] = t_dot(ce[m], cu[m])

    @pl.when((i >= 4) & (i % 2 == 0))
    def _():
        e_in[...] = peer[...]

    @pl.when((i >= 4) & (i % 2 == 1))
    def _():
        e_in[...] = own[...]

    @pl.when(i >= 4)
    def _():
        for m, lo, hi in spans:
            acc[m] += t_dot(flat(e_in[:, lo:hi, :]), flat(dup[:, lo:hi, :]))

    @pl.when(i == 7)
    def _():
        for j in range(4):
            for m in range(2):
                up_keep[j, m] = acc[m, block(2 * j + here.x), :].astype(BF16)
                up_send[j, m] = acc[m, block(2 * j + 1 - here.x), :].astype(BF16)
        for copy in loaded:
            copy.wait()
        rows[...] = jnp.zeros_like(rows)
        sums[...] = jnp.zeros_like(sums)

        def load(p):
            load_rows(dims, p, img, txt, rows)
            rows[0:1, :] += dcls[p, 0:1, :]
            rows[ip:ip + 1, :] += dcls[p, 1:2, :]

        for p in range(quarter):
            load(p)
            for m, lo, hi in ((0, 0, ip), (1, ip, dims.slab)):
                n, r = normalise(attended[p, lo:hi, :])
                dy = dexp[p, lo:hi, :]
                sums[m:m + 1, :] += jnp.sum(dy * n, axis=0, keepdims=True)
                sums[2 + m:3 + m, :] += jnp.sum(dy, axis=0, keepdims=True)
                d = rows[lo:hi, :] + norm_back(n, r, dy * vector(vec, GAIN2 + m))
                dattended[p, lo:hi, :] = d
                sd = d * vector(vec, A_SCALE)
                dattn[p, lo:hi, :] = sd.astype(BF16)
                a = attn[p, lo:hi, :] + vector(vec, A_BIAS)
                sums[4:5, :] += jnp.sum(d * a, axis=0, keepdims=True)
                sums[5:6, :] += jnp.sum(sd, axis=0, keepdims=True)
            sent_core[p].start()
        sent_near.wait_recv()

        def final(p, c):
            load(p)
            for m, lo, hi in ((0, 0, ip), (1, ip, dims.slab)):
                b = d_own[p, lo:hi, :] + d_far[p, lo:hi, :].astype(F32) + vector(vec, F_BIAS + m)
                f = attended[p, lo:hi, :] + vector(vec, F_SCALE) * b
                if m == 0:
                    fin_img[p] = f[0:dims.patches].astype(BF16)
                else:
                    fin_txt[p] = f[0:dims.caption].astype(BF16)
                g = rows[lo:hi, :]
                sums[6:7, :] += jnp.sum(g * b, axis=0, keepdims=True)
                sums[7 + m:8 + m, :] += jnp.sum(g, axis=0, keepdims=True) * vector(vec, F_SCALE)
            return c

        lax.fori_loop(0, quarter, final, 0)
        for p in range(quarter):
            sent_core[p].wait()
            dattn_peer[p] = n_peer[p]
        for j in range(4):
            sent_side[j].wait()
            down_sum[j] = (down_sum[j].astype(F32) + side_recv[j].astype(F32)).astype(BF16)
        sent_near.wait_send()


def turn(dims, img, txt, peer, own, act, dup, ddn, ce, ca, cu, cd, dexp, attended, attn, d_own, d_near, dcls, vec):
    model = own.shape[-1]
    hidden = act.shape[-1]
    slab, quarter = dims.slab, dims.quarter
    held = pl.BlockSpec(memory_space=pltpu.VMEM)

    def own_at(i):
        return Place().quarter(0, 0), 0, 0

    away = pl.BlockSpec(memory_space=pl.ANY)
    half = pl.BlockSpec((quarter, slab, model), lambda i: (jnp.where(i < 6, 1, 0), 0, 0))
    first = pl.BlockSpec((quarter, slab, hidden), lambda i: (jnp.minimum(i, 3), 0, 0))
    last = pl.BlockSpec((quarter, slab, hidden), lambda i: (jnp.maximum(i - 4, 0), 0, 0))
    block = (quarter, slab, model)
    part = (4, 2, model // 8, hidden)
    outs = [(part, BF16), (part, BF16), (part, BF16), (block, F32), (block, BF16), (block, BF16),
            ((quarter, dims.patches, model), BF16), ((quarter, dims.caption, model), BF16), ((16, model), F32)]
    return pl.pallas_call(
        functools.partial(turn_kernel, dims),
        grid=(8,),
        in_specs=[pl.BlockSpec((quarter, dims.patches, model), own_at),
                  pl.BlockSpec((quarter, dims.caption, model), own_at)] + [half] * 2 + [first, last, first]
        + [held] * 4 + [away] * 4 + [held] * 3,
        out_specs=[held] * len(outs),
        out_shape=[jax.ShapeDtypeStruct(v, t) for v, t in outs],
        scratch_shapes=[
            pltpu.VMEM((2, model, hidden), F32), pltpu.VMEM(block, BF16), pltpu.VMEM(block, BF16),
            pltpu.VMEM((slab, model), F32), pltpu.VMEM(part, BF16), pltpu.VMEM(part, BF16),
            pltpu.VMEM(block, BF16),
        ] + [pltpu.VMEM(block, F32)] * 4 + [
            pltpu.SemaphoreType.DMA((4,)),
            pltpu.SemaphoreType.DMA((5 + quarter,)), pltpu.SemaphoreType.DMA((5 + quarter,)),
        ],
        compiler_params=params(collective_id=3, has_side_effects=True),
        cost_estimate=pl.CostEstimate(
            flops=16 * quarter * slab * model * hidden, bytes_accessed=40_000_000, transcendentals=0),
        name="turn",
    )(img, txt, peer, own, act, dup, ddn, ce, ca, cu, cd, dexp, attended, attn, d_own, d_near, dcls, vec)


def back_kernel(dims, lens, d_own, d_peer, normed, qkv_far, mixed_far, qkv_own, mixed_own, wq, wo, wf,
                fin_img, fin_txt, up_keep, up_send, down_sum,
                keep, send, grad_pair, grad_single, cols_far, cols_own, near_img, near_txt, far_sum, up_one, down_out, up_out,
                dattn, dm_far, dm_own, dq_far, dq_own, acc_far, acc_own, w_far, w_own, o_far, o_own, dn, grad_f,
                up_mine, up_side, up_low, up_z, down_mine, down_z, from_side, local_sem, send_sem, recv_sem):
    here = Place()
    i = pl.program_id(0)
    slab, quarter, local = dims.slab, dims.quarter, dims.local
    two, one_head = parts_of(dims)
    count = quarter * slab
    model = normed.shape[-1]
    piece = from_side.shape[1]
    block = lambda j: pl.ds(pl.multiple_of(j * piece, piece), piece)
    used = [0]

    def make(src, dst, device):
        at = used[0]
        used[0] += 1
        return remote(src, dst, send_sem, recv_sem, at, device)

    sent_near = [make(fin_img, near_img, here.near), make(fin_txt, near_txt, here.near)]
    sent_up = [make(up_send.at[j, m], up_side.at[m, j], here.side) for m in range(2) for j in range(4)]
    sent_down = [make(down_sum.at[(here.z + k) % 4], down_z.at[k - 1], here.along[k - 1]) for k in range(1, 4)]
    sent_far = [make(grad_f.at[block(2 * j + 1 - here.x)], from_side.at[j], here.side) for j in range(4)]
    sent_low = [make(up_low.at[(here.z + k) % 4], up_z.at[k - 1], here.along[k - 1]) for k in range(1, 4)]
    loaded = [pltpu.make_async_copy(up_keep, up_mine, local_sem.at[0]),
              pltpu.make_async_copy(down_sum.at[here.z], down_mine, local_sem.at[1])]

    @pl.when(i == 0)
    def _():
        meet([here.near, here.side] + here.along)
        for copy in loaded + sent_near + sent_up + sent_down:
            copy.start()
        for acc, cols in ((acc_far, cols_far), (acc_own, cols_own)):
            acc[...] = jnp.zeros_like(acc)
            cols[...] = jnp.zeros_like(cols)
        for t in range(4):
            own, start = (wq, t * local) if t < 3 else (wo, 0)
            dst, at = (w_far, t * 2 * two) if t < 3 else (o_far, 0)
            copy_rows(dst, at, wf, t * local, two)
            copy_rows(dst, at + two, own, start + two, one_head)
            copy_rows(dst, at + two + one_head, wf, t * local + two, one_head)
            dst, at = (w_own, t * two) if t < 3 else (o_own, 0)
            copy_rows(dst, at, own, start, two)

    @pl.when(i % 2 == 0)
    def _():
        dattn[...] = d_own[...]

    @pl.when(i % 2 == 1)
    def _():
        dattn[...] = d_peer[...]

    whose = here.quarter(0, i % 2)

    @pl.when(i < 2)
    def _():
        part = back_step(dims, 2, lens, whose, dattn, normed, qkv_far, mixed_far, dm_far, dq_far, acc_far, cols_far,
                         w_far, o_far)
        dn[i] = part.reshape(quarter, slab, model)

    @pl.when(i == 1)
    def _():
        for t in range(4):
            at = t * 2 * two
            to = 4 * two + t * one_head
            grad_f[:, t * two:(t + 1) * two] = acc_far[:, at:at + two].astype(BF16)
            grad_f[:, to:to + one_head] = acc_far[:, at + two + one_head:at + 2 * two].astype(BF16)
            grad_single[:, t * one_head:(t + 1) * one_head] = acc_far[:, at + two:at + two + one_head].astype(BF16)
        for copy in sent_far:
            copy.start()
        loaded[0].wait()
        for j in range(4):
            sent_up[j].wait_recv()
            up_low[j] = (up_mine[j, 0].astype(F32) + up_side[0, j].astype(F32)).astype(BF16)
        for copy in sent_low:
            copy.start()

    @pl.when(i >= 2)
    def _():
        part = back_step(dims, 1, lens, whose, dattn, normed, qkv_own, mixed_own, dm_own, dq_own, acc_own, cols_own,
                         w_own, o_own)
        total = (part.reshape(quarter, slab, model) + dn[i - 2]).astype(BF16)

        @pl.when(i == 2)
        def _():
            keep[...] = total

        @pl.when(i == 3)
        def _():
            send[...] = total

    @pl.when(i == 3)
    def _():
        grad_pair[...] = acc_own[...].astype(BF16)
        for j in range(4):
            sent_up[4 + j].wait_recv()
            up_one[j] = (up_mine[j, 1].astype(F32) + up_side[1, j].astype(F32)).astype(BF16)
        loaded[1].wait()
        for copy in sent_down:
            copy.wait_recv()
        down_out[...] = (down_mine[...].astype(F32) + down_z[0].astype(F32)) + (
            down_z[1].astype(F32) + down_z[2].astype(F32))
        for j in range(4):
            sent_far[j].wait_recv()
            far_sum[j] = (grad_f[block(2 * j + here.x), :].astype(F32) + from_side[j].astype(F32)).astype(BF16)
        for copy in sent_low:
            copy.wait_recv()
        up_out[...] = (up_low[here.z].astype(F32) + up_z[0].astype(F32)) + (
            up_z[1].astype(F32) + up_z[2].astype(F32))
        for copy in sent_near:
            copy.wait_recv()
        for copy in sent_near + sent_up + sent_down + sent_far + sent_low:
            copy.wait_send()


def back(dims, lens, d_own, d_peer, normed, qkv_far, mixed_far, qkv_own, mixed_own, wq, wo, wf,
         fin_img, fin_txt, up_keep, up_send, down_sum):
    model = normed.shape[-1]
    slab, quarter = dims.slab, dims.quarter
    hidden = up_keep.shape[-1]
    piece = model // 8
    held = pl.BlockSpec(memory_space=pltpu.VMEM)
    away = pl.BlockSpec(memory_space=pl.ANY)
    spec = lambda cols, at: pl.BlockSpec((quarter, slab, cols), lambda i: (at(i), 0, 0))
    early, late = lambda i: jnp.minimum(i, 1), lambda i: jnp.maximum(i - 2, 0)
    rows = (quarter, slab, model)
    outs = [(held, rows, BF16), (held, rows, BF16), (held, (model, 512), BF16), (held, (model, 256), BF16),
            (held, (1, 768), F32), (held, (1, 384), F32),
            (away, fin_img.shape, BF16), (away, fin_txt.shape, BF16),
            (held, (4, piece, model), BF16), (held, (4, piece, hidden), BF16),
            (held, (2, piece, hidden), F32), (held, (piece, hidden), F32)]
    slabs = lambda cols: pltpu.VMEM((quarter, slab, cols), BF16)
    return pl.pallas_call(
        functools.partial(back_kernel, dims),
        grid=(4,),
        in_specs=[pl.BlockSpec(memory_space=pltpu.SMEM), held, held, spec(model, lambda i: i % 2),
                  spec(768, early), spec(256, early), spec(384, late), spec(128, late), held, held, held]
        + [away] * 5,
        out_specs=[v[0] for v in outs],
        out_shape=[jax.ShapeDtypeStruct(v[1], v[2]) for v in outs],
        scratch_shapes=[
            slabs(model), slabs(256), slabs(128), slabs(768), slabs(384),
            pltpu.VMEM((model, 1024), F32), pltpu.VMEM((model, 512), F32),
            pltpu.VMEM((768, model), BF16), pltpu.VMEM((384, model), BF16),
            pltpu.VMEM((256, model), BF16), pltpu.VMEM((128, model), BF16),
            pltpu.VMEM((2,) + rows, F32), pltpu.VMEM((model, model), BF16),
            pltpu.VMEM((4, 2, piece, hidden), BF16), pltpu.VMEM((2, 4, piece, hidden), BF16),
            pltpu.VMEM((4, piece, hidden), BF16), pltpu.VMEM((3, piece, hidden), BF16),
            pltpu.VMEM((2, piece, hidden), BF16), pltpu.VMEM((3, 2, piece, hidden), BF16),
            pltpu.VMEM((4, piece, model), BF16),
            pltpu.SemaphoreType.DMA((2,)), pltpu.SemaphoreType.DMA((20,)), pltpu.SemaphoreType.DMA((20,)),
        ],
        compiler_params=params(collective_id=4, has_side_effects=True),
        cost_estimate=pl.CostEstimate(
            flops=24 * quarter * slab * model * 1152, bytes_accessed=30_000_000, transcendentals=0),
        name="back",
    )(lens, d_own, d_peer, normed, qkv_far, mixed_far, qkv_own, mixed_own, wq, wo, wf,
      fin_img, fin_txt, up_keep, up_send, down_sum)


V_ROWS, V_MP, V_HEADS, V_FAR = 24, 11, 13, 15


def finish_kernel(dims, n_keep, n_send, dattended, states_img, states_txt, vec, fin_img, fin_txt,
                  near_img, near_txt, grad_pair, grad_single, grad_far, up_one, own_sums, up_sums, cols_own, cols_far,
                  out_img, out_txt, back_img, back_txt, grad_out, v_out, up_out,
                  n_recv, s_img, s_txt, d_img, d_txt, rows, xr, zs, zr, zr_far, zr_up, far_sum, far_recv, vs, vr,
                  local_sem, send_sem, recv_sem):
    quarter = dims.quarter
    here = Place()
    z, x, m = here.z, here.x, here.m
    near_quarter = here.quarter(1, 0)
    used = [0]

    def send(src, dst, device):
        at = used[0]
        used[0] += 1
        return remote(src, dst, send_sem, recv_sem, at, device)

    loaded = [pltpu.make_async_copy(states_img.at[pl.ds(m * quarter, quarter)], s_img, local_sem.at[0]),
              pltpu.make_async_copy(states_txt.at[pl.ds(m * quarter, quarter)], s_txt, local_sem.at[1])]
    for copy in loaded:
        copy.start()
    meet([here.core, here.near, here.side] + here.along)

    n_copies = [send(n_send.at[p], n_recv.at[p], here.core) for p in range(quarter)]
    for copy in n_copies:
        copy.start()
    piece = xr.shape[1]
    wide = grad_pair.shape[1]
    spans = ((grad_pair, 0, wide), (grad_single, wide, xr.shape[2]))
    block = lambda j: pl.ds(pl.multiple_of(j * piece, piece), piece)
    x_copies = []
    for j in range(4):
        for src, lo, hi in spans:
            x_copies.append(send(src.at[block(2 * j + 1 - x)], xr.at[j, :, pl.ds(lo, hi - lo)], here.side))
            x_copies[-1].start()
    far_copies = [send(grad_far.at[(z + k) % 4], zr_far.at[k - 1], here.along[k - 1]) for k in range(1, 4)]
    for copy in far_copies:
        copy.start()

    fin_local, fin_remote = [], []
    for j, (src, dst, q) in enumerate((
        (fin_img, out_img, m), (fin_txt, out_txt, m), (near_img, out_img, near_quarter), (near_txt, out_txt, near_quarter),
    )):
        at = pl.ds(q * quarter, quarter)
        fin_local.append(pltpu.make_async_copy(src, dst.at[at], local_sem.at[2 + j]))
        fin_remote.append(send(src, dst.at[at], here.core))

    rows[...] = jnp.zeros_like(rows)
    for copy in loaded:
        copy.wait()
    total = [jnp.zeros((1, rows.shape[1]), F32)] * 2
    back_local, to_near, to_other = [], [], []
    for p in range(quarter):
        load_rows(dims, p, s_img, s_txt, rows)
        n, r = normalise(rows[...])
        n_copies[p].wait_recv()
        dy = n_keep[p].astype(F32) + n_recv[p].astype(F32)
        total[0] = total[0] + jnp.sum(dy * n, axis=0, keepdims=True)
        total[1] = total[1] + jnp.sum(dy, axis=0, keepdims=True)
        d = dattended[p] + norm_back(n, r, dy * vector(vec, GAIN1))
        d_img[p] = d[0:dims.patches].astype(BF16)
        d_txt[p] = d[dims.ip:dims.ip + dims.caption].astype(BF16)
        for j, (src, dst) in enumerate(((d_img, back_img), (d_txt, back_txt))):
            at = dst.at[m * quarter + p]
            to_near.append(send(src.at[p], at, here.near))
            to_near[-1].start()
            to_other.append(send(src.at[p], at, here.core))
            to_other[-1].start()
            back_local.append(pltpu.make_async_copy(src.at[p], at, local_sem.at[6 + 2 * p + j]))
            back_local[-1].start()
    for copy in fin_local + fin_remote:
        copy.start()

    at = lax.broadcasted_iota(jnp.int32, (V_ROWS, 1), 0)
    two, one_head = parts_of(dims)
    vs[0] = jnp.zeros(vs.shape[1:], F32)
    vs[0, 0:1, :] = total[0]
    vs[0, 1:2, :] = total[1]
    vs[0, 2:V_MP, :] = own_sums[0:V_MP - 2, :]
    vs[0, V_MP:V_HEADS, :] = up_sums[...]
    for j in range(2):
        own_at, far_at = 2 * j * two, 4 * j * two
        vs[0, V_HEADS + j:V_HEADS + j + 1, 0:two] = cols_own[0:1, own_at:own_at + two]
        vs[0, V_HEADS + j:V_HEADS + j + 1, two:two + one_head] = cols_far[0:1, far_at + two:far_at + two + one_head]
        vs[0, V_FAR + j:V_FAR + j + 1, 0:two] = cols_far[0:1, far_at:far_at + two]
        vs[0, V_FAR + j:V_FAR + j + 1, two:two + one_head] = cols_far[0:1, far_at + two + one_head:far_at + 2 * two]
    v = vs[0]
    v_copies = []

    def exchange(step, value, device):
        vs[step] = value
        copy = send(vs.at[step], vr.at[step], device)
        copy.start()
        copy.wait_recv()
        v_copies.append(copy)
        return vr[step]

    v = v + jnp.where(at < V_MP, exchange(0, v, here.core), 0.0)
    v = v + exchange(1, v, here.side)
    vs[2] = v
    vr[3 + z] = v
    around = [send(vs.at[2], vr.at[3 + z], here.along[k - 1]) for k in range(1, 4)]
    for copy in around:
        copy.start()
    up_copies = [send(up_one.at[(z + k) % 4], zr_up.at[k - 1], here.along[k - 1]) for k in range(1, 4)]
    for copy in up_copies:
        copy.start()

    def own_sum(j, k):
        src, lo, hi = spans[k]
        return src[block(2 * j + x), :].astype(F32) + xr[j, :, lo:hi].astype(F32)

    for copy in x_copies:
        copy.wait_recv()
    for j in range(4):
        for k, (src, lo, hi) in enumerate(spans):
            zs[j, :, lo:hi] = own_sum(j, k).astype(BF16)
    z_copies = [send(zs.at[(z + k) % 4], zr.at[k - 1], here.along[k - 1]) for k in range(1, 4)]
    for copy in z_copies:
        copy.start()

    for copy in around:
        copy.wait_recv()
    v = (vr[3] + vr[4]) + (vr[5] + vr[6])
    for copy in far_copies:
        copy.wait_recv()
    far = grad_far[z].astype(F32)
    for k in range(3):
        far = far + zr_far[k].astype(F32)
    far_sum[...] = far.astype(BF16)
    far_copy = send(far_sum, far_recv, here.near)
    far_copy.start()
    vs[3] = v
    v_near = send(vs.at[3], vr.at[2], here.near)
    v_near.start()
    for copy in up_copies:
        copy.wait_recv()
    up_out[...] = (up_one[z].astype(F32) + zr_up[0].astype(F32)) + (zr_up[1].astype(F32) + zr_up[2].astype(F32))
    for copy in fin_local + back_local:
        copy.wait()
    onward = []
    for p in range(quarter):
        for j, dst in enumerate((back_img, back_txt)):
            to_near[2 * p + j].wait_recv()
            at_near = dst.at[near_quarter * quarter + p]
            onward.append(send(at_near, at_near, here.core))
            onward[-1].start()
    far_copy.wait_recv()
    for copy in z_copies:
        copy.wait_recv()
    for k, (src, lo, hi) in enumerate(spans):
        g = own_sum(z, k) + far_recv[:, lo:hi].astype(F32)
        for j in range(3):
            g = g + zr[j, :, lo:hi].astype(F32)
        grad_out[:, lo:hi] = g
    v_near.wait_recv()
    there = vr[2]
    v_out[...] = v + jnp.where(at < V_MP, there, 0.0)
    v_out[V_HEADS:V_HEADS + 2, :] = v[V_HEADS:V_HEADS + 2, :] + there[V_FAR:V_FAR + 2, :]
    for copy in to_other + fin_remote + onward:
        copy.wait()
    for copy in n_copies + x_copies + far_copies + to_near + z_copies + v_copies + around + up_copies + [far_copy, v_near]:
        copy.wait_send()


def finish(dims, n_keep, n_send, dattended, states_img, states_txt, vec, fin_img, fin_txt,
           near_img, near_txt, grad_pair, grad_single, grad_far, up_one, *tables):
    pairs, patches, model = states_img.shape
    caption = states_txt.shape[1]
    quarter, slab = dims.quarter, dims.slab
    piece, cols = grad_far.shape[1:]
    held = pl.BlockSpec(memory_space=pltpu.VMEM)
    away = pl.BlockSpec(memory_space=pl.ANY)
    n_remote = 7 * quarter + 28
    return pl.pallas_call(
        functools.partial(finish_kernel, dims),
        in_specs=[held] * 3 + [away] * 2 + [held] * 13,
        out_specs=[away] * 4 + [held] * 3,
        out_shape=[
            jax.ShapeDtypeStruct((pairs, patches, model), BF16),
            jax.ShapeDtypeStruct((pairs, caption, model), BF16),
            jax.ShapeDtypeStruct((pairs, patches, model), BF16),
            jax.ShapeDtypeStruct((pairs, caption, model), BF16),
            jax.ShapeDtypeStruct((piece, cols), F32),
            jax.ShapeDtypeStruct((V_ROWS, model), F32),
            jax.ShapeDtypeStruct(up_one.shape[1:], F32),
        ],
        scratch_shapes=[
            pltpu.VMEM((quarter, slab, model), BF16),
            pltpu.VMEM((quarter, patches, model), BF16),
            pltpu.VMEM((quarter, caption, model), BF16),
            pltpu.VMEM((quarter, patches, model), BF16),
            pltpu.VMEM((quarter, caption, model), BF16),
            pltpu.VMEM((slab, model), F32),
            pltpu.VMEM((4, piece, cols), BF16), pltpu.VMEM((4, piece, cols), BF16),
            pltpu.VMEM((3, piece, cols), BF16), pltpu.VMEM((3, piece, cols), BF16),
            pltpu.VMEM((3,) + up_one.shape[1:], BF16),
            pltpu.VMEM((piece, cols), BF16), pltpu.VMEM((piece, cols), BF16),
            pltpu.VMEM((4, V_ROWS, model), F32),
            pltpu.VMEM((7, V_ROWS, model), F32),
            pltpu.SemaphoreType.DMA((6 + 2 * quarter,)),
            pltpu.SemaphoreType.DMA((n_remote,)),
            pltpu.SemaphoreType.DMA((n_remote,)),
        ],
        compiler_params=params(collective_id=1, has_side_effects=True),
        name="finish",
    )(n_keep, n_send, dattended, states_img, states_txt, vec, fin_img, fin_txt,
      near_img, near_txt, grad_pair, grad_single, grad_far, up_one, *tables)


def spread_kernel(cols, at, sums, grad, gains, shifts, *refs):
    *outs, qkv, out_w, turned = refs
    back = sums.shape[1] - at[0] * cols

    def slice_of(value):
        return pltpu.roll(value, back, 1)[:, 0:cols]

    mine = slice_of(sums[...])
    for out, (lo, count) in zip(outs[:8], ((0, 1), (1, 1), (7, 1), (6, 1), (2, 2), (4, 2), (9, 2), (8, 1))):
        out[...] = mine[lo:lo + count, :]
    wide = jnp.concatenate([gains[...], shifts[...], jnp.zeros((4, sums.shape[1]), F32)], axis=0)
    heads = slice_of(wide)
    outs[8][...] = heads[0:2, :]
    outs[9][...] = heads[2:4, :]
    outs[10][...] = sums[V_MP:V_MP + 2, :]
    outs[11][...] = sums[V_HEADS:V_HEADS + 2, 0:outs[11].shape[1]]
    two, one = 2 * HEAD_DIM, HEAD_DIM
    for t in range(3):
        qkv[t, :, 0:two] = grad[:, t * two:(t + 1) * two]
        qkv[t, :, two:two + one] = grad[:, 4 * two + t * one:4 * two + (t + 1) * one]
    turned[...] = jnp.zeros_like(turned)
    turned[0:cols, 0:two] = grad[:, 3 * two:4 * two]
    turned[0:cols, two:two + one] = grad[:, 4 * two + 3 * one:4 * two + 4 * one]
    out_w[...] = turned[...].T[0:two + one, 0:cols]


def spread(local, at, sums, grad, gains, shifts):
    cols, model = grad.shape[0], sums.shape[1]
    assert cols <= 128
    shapes = [(1, cols)] * 4 + [(2, cols)] * 3 + [(1, cols)] + [(2, cols)] * 2 + [(2, model), (2, local)]
    shapes += [(3, cols, local), (local, cols)]
    args = (sums, grad, gains, shifts)
    return pl.pallas_call(
        functools.partial(spread_kernel, cols),
        grid_spec=pltpu.PrefetchScalarGridSpec(
            num_scalar_prefetch=1, grid=(1,),
            in_specs=[spec_whole(v) for v in args],
            out_specs=[pl.BlockSpec(v, lambda i, o, n=len(v): (0,) * n) for v in shapes],
            scratch_shapes=[pltpu.VMEM((128, 256), F32)],
        ),
        out_shape=[jax.ShapeDtypeStruct(v, F32) for v in shapes],
        compiler_params=params(),
        cost_estimate=pl.CostEstimate(flops=1_000_000, bytes_accessed=1_000_000, transcendentals=0),
        name="spread",
    )(at, *args)


def per_device(
    image_states, text_states, caption_lengths, image_cotangent, text_cotangent,
    first_gain, first_shift, query_key_value, query_value_bias, output_weight, output_bias,
    attention_scale, expert_gain, expert_shift, expert_up, expert_up_bias, expert_down,
    expert_down_bias, feedforward_scale, head_gain, head_shift, head_weight, logit_scale,
):
    pairs, patches, model = image_states.shape
    caption = text_states.shape[1]
    local = query_key_value.shape[2]
    quarter = pairs // 4
    batch_size = lax.axis_size("batch")
    assert lax.axis_size("mp") == 4 and pairs == 4 * quarter and quarter <= 3
    assert batch_size & (batch_size - 1) == 0
    assert local == 3 * HEAD_DIM
    ip, tp = up16(patches), up16(caption)
    dims = Dims(patches, caption, ip, tp, ip + tp, quarter, local)
    me = lax.axis_index("mp")
    batch_at = lax.axis_index("batch")
    order = me ^ jnp.asarray(ORDER, jnp.int32)
    vectors = (first_gain, first_shift, attention_scale, output_bias, expert_gain, expert_shift,
               feedforward_scale, expert_down_bias, head_gain, head_shift)
    own_w = jnp.transpose(query_key_value, (1, 2, 0)).reshape(3 * local, model)
    one_kernel = batch_size == 8 and model // batch_size % 32 == 0 and expert_up.shape[2] == model
    if one_kernel:
        (vec, normed, qkv_own, mixed_own, qkv_far, mixed_far, wf, attended, attn, e_own, e_peer, cls_own, cls_peer) = front(
            dims, caption_lengths, image_states, text_states, vectors, query_value_bias, own_w, output_weight)
    else:
        vec = jnp.concatenate([v.reshape(-1, model) for v in vectors] + [jnp.zeros((1, model), F32)])
        wo = jnp.concatenate([own_w, output_weight])
        wf = to_y(wo)
        far_bias = to_y(query_value_bias)
        normed, qkv_own, rest, mixed_own = attend_own(
            dims, order, caption_lengths, image_states, text_states, vec, query_value_bias, wo)
        qkv_far, mixed_far, a_keep, a_send = attend_far(
            dims, order, caption_lengths, normed, rest, mixed_own, far_bias, wo, wf)
        a_recv = to_core(a_send)
        attended, attn, e_own, cls_own = residual(
            dims, order, a_keep, a_recv, image_states, text_states, vec)
        e_peer = to_core(e_own)
        cls_peer = to_core(cls_own)
    if one_kernel:
        (act, dup, ddn, dexp, d_own, d_near, up_sums, class_e, c_act, c_dup, c_ddn, dcls, head_in, dproj,
         grad_head_gain, grad_head_shift, scalars) = middle(
            dims, pairs * batch_size, image_cotangent, text_cotangent, e_own, e_peer, cls_own, cls_peer, vec,
            expert_up, expert_up_bias, expert_down, head_weight, logit_scale.reshape(1, 1))
        down_sum, up_keep, up_send, dattended, dattn, dattn_peer, fin_img, fin_txt, own_sums = turn(
            dims, image_cotangent, text_cotangent, e_peer, e_own, act, dup, ddn, class_e, c_act, c_dup, c_ddn,
            dexp, attended, attn, d_own, d_near, dcls, vec)
    else:
        class_part, class_e = class_forward(dims, cls_own, cls_peer, expert_up, expert_up_bias, expert_down)
        class_parts = from_others(class_part, "mp", 1, 4)

        act_a, dup_a, ddn_a, d_send3, d_keep1, x_send3, x_keep1, bias_a, cot_a = experts(
            dims, "experts_a", 1, order[jnp.asarray([3, 1])], e_peer, e_own, image_cotangent, text_cotangent,
            tie(vec, class_part), expert_up, expert_up_bias, expert_down)
        x_recv1 = to_core(x_send3)
        d_recv1 = to_core(d_send3)
        final_class = class_final(
            dims, order, cls_own, cls_peer, class_parts, tie(vec, bias_a))
        class_blocks = gather_batch(final_class[None])
        x_near = add_low(x_keep1, x_recv1)
        x_far = to_y(x_near)
        act_b, dup_b, ddn_b, d_send2, d_keep0, x_send2, x_keep0, bias_b, cot_b = experts(
            dims, "experts_b", 0, order[jnp.asarray([2, 0])], e_peer, e_own, image_cotangent, text_cotangent,
            tie(vec, final_class, x_near), expert_up, expert_up_bias, expert_down)
        x_recv0 = to_core(x_send2)
        d_recv0 = to_core(d_send2)

        head_in, dproj, dclass, grad_head_gain, grad_head_shift, scalars = (contrast if batch_size <= 8 else contrast_large)(
            dims, pairs * batch_size, batch_at.reshape(1), class_blocks, tie(vec, bias_b), head_weight,
             logit_scale.reshape(1, 1))
        c_act, c_dup, c_ddn, c_dexp, c_bias, dcls = class_back(
            dims, order, class_e, cot_a, cot_b, dclass, vec, expert_up, expert_up_bias, expert_down)
        extras = from_others(c_dexp, "mp", 1, 4)
        d_far = to_y(add_low(d_keep1, tie(d_recv1, c_dexp)))
        expert_grad = expert_grads(
            dims, e_peer, e_own, act_a, dup_a, ddn_a, act_b, dup_b, ddn_b, class_e, c_act, c_dup, c_ddn)
        expert_sum = lax.psum_scatter(expert_grad, "batch", scatter_dimension=1, tiled=True)

        dattended, dattn, sums_two = norm_two(
            dims, order, x_keep0, x_recv0, x_far, attended, a_keep, a_recv, image_cotangent, text_cotangent,
            dcls, extras, tie(vec, expert_grad))
        dattn_peer = to_core(dattn)
        fin_img, fin_txt, sums_fin = final_rows(
            dims, order, d_keep0, d_recv0, d_far, attended, image_cotangent, text_cotangent, dcls,
            tie(vec, sums_two))
        own_sums = jnp.concatenate([sums_two[:6], sums_fin[:3]])
        up_sums = bias_a + bias_b + c_bias
    contrast_loss = scalars[0, :1]
    grad_logit_scale = scalars[1, :1]
    if one_kernel:
        (n_keep, n_send, grad_o01, grad_o2, cols_far, cols_own, near_img, near_txt, far_sum, up_one, grad_down,
         up_low) = back(
            dims, caption_lengths, dattn, dattn_peer, normed, qkv_far, mixed_far, qkv_own, mixed_own,
            own_w, output_weight, wf, fin_img, fin_txt, up_keep, up_send, down_sum)
    else:
        n_keep, n_send, grad_far, grad_o2, cols_far = attend_back(
            dims, True, order, caption_lengths, dattn, dattn_peer, normed, qkv_far, mixed_far, own_w, output_weight, wf)
        n_keep, n_send, grad_o01, cols_own = attend_back(
            dims, False, order, caption_lengths, dattn, dattn_peer, normed, qkv_own, mixed_own, own_w, output_weight, wf,
            prior=(n_keep, n_send))
    cols = model // batch_size
    mine = lambda v, axis: lax.dynamic_slice_in_dim(v, batch_at * cols, cols, axis=axis)
    grad_head_weight = jnp.einsum("mnc,mne->mce", mine(head_in, 2), dproj, preferred_element_type=F32)
    pair, single = 2 * HEAD_DIM, HEAD_DIM
    if one_kernel:
        image_output, text_output, image_grad, text_grad, attn_grad, sums, up_high = finish(
            dims, n_keep, n_send, dattended, image_states, text_states, vec, fin_img, fin_txt,
            near_img, near_txt, grad_o01, grad_o2, far_sum, up_one, own_sums, up_sums, cols_own, cols_far)
        *vectors, grad_qkv, grad_output_weight = spread(
            local, batch_at.reshape(1), sums, attn_grad, grad_head_gain, grad_head_shift)
        flat = lambda v: v.reshape(-1)
        return (
            image_output,
            text_output,
            contrast_loss,
            image_grad,
            text_grad,
            flat(vectors[0]),
            flat(vectors[1]),
            jnp.transpose(grad_qkv, (1, 0, 2)),
            vectors[11],
            grad_output_weight,
            flat(vectors[2]),
            flat(vectors[3]),
            vectors[4],
            vectors[5],
            jnp.stack([up_low, up_high]),
            vectors[10],
            jnp.transpose(grad_down, (0, 2, 1)),
            vectors[6],
            flat(vectors[7]),
            vectors[8],
            vectors[9],
            grad_head_weight,
            grad_logit_scale,
        )
    else:
        grad_expert_up = expert_sum[:2].astype(F32)
        grad_expert_down = jnp.transpose(expert_sum[2:].astype(F32), (0, 2, 1))
        cols_own = cols_own.reshape(3, pair)[::2]
        cols_far = cols_far.reshape(3, 2 * pair)[::2]
        heads = jnp.concatenate([cols_own, cols_far[:, pair:pair + single]], axis=1)
        heads_far = jnp.concatenate([cols_far[:, :pair], cols_far[:, pair + single:]], axis=1)
        n_recv = to_core(n_send)
        d_img, d_txt, sums_one = norm_one(
            dims, order, n_keep, n_recv, dattended, image_states, text_states, vec)
        image_output = gather_rows(fin_img, me)
        text_output = gather_rows(fin_txt, me)
        image_grad = gather_rows(d_img, me)
        text_grad = gather_rows(d_txt, me)
        grad_own = jnp.concatenate([grad_o01, grad_o2], axis=1)
        grad_far = lax.psum_scatter(grad_far, "batch", scatter_dimension=0, tiled=True)
        grad_own = lax.psum_scatter(grad_own, "batch", scatter_dimension=0, tiled=True)
        attn_grad = grad_own.astype(F32) + to_y(grad_far).astype(F32)
        heads = heads + to_y(heads_far)
        own_sums = sum_over(jnp.concatenate([sums_one[:2], own_sums]), "mp")
        flat = jnp.concatenate([own_sums.reshape(-1), heads.reshape(-1), up_sums.reshape(-1)])
        count = flat.shape[0]
        flat = jnp.pad(flat, (0, -count % 1024)).reshape(-1, 128)
        flat = sum_over(flat, "batch").reshape(-1)[:count]
        done = own_sums.shape[0]
        own_sums = mine(flat[:done * model].reshape(done, model), 1)
        heads = flat[done * model:done * model + 2 * local].reshape(2, local)
        grad_expert_up_bias = flat[done * model + 2 * local:].reshape(up_sums.shape)
    attn_grad = jnp.concatenate(
        [attn_grad[:, :4 * pair].reshape(cols, 4, pair), attn_grad[:, 4 * pair:].reshape(cols, 4, single)], axis=2)
    grad_query_key_value = attn_grad[:, :3]
    grad_output_weight = jnp.transpose(attn_grad[:, 3])
    return (
        image_output,
        text_output,
        contrast_loss,
        image_grad,
        text_grad,
        own_sums[0],
        own_sums[1],
        grad_query_key_value,
        heads,
        grad_output_weight,
        own_sums[7],
        own_sums[6],
        own_sums[2:4],
        own_sums[4:6],
        grad_expert_up,
        grad_expert_up_bias,
        grad_expert_down,
        own_sums[9:11],
        own_sums[8],
        mine(grad_head_gain, 1),
        mine(grad_head_shift, 1),
        grad_head_weight,
        grad_logit_scale,
    )


def solution(mesh):
    return jax.shard_map(
        per_device,
        mesh=mesh,
        in_specs=(
            P("batch", None, None),
            P("batch", None, None),
            P("batch"),
            P("batch", None, None),
            P("batch", None, None),
            P(),
            P(),
            P(None, None, "mp"),
            P(None, "mp"),
            P("mp", None),
            P(),
            P(),
            P(),
            P(),
            P(None, None, "mp"),
            P(None, "mp"),
            P(None, "mp", None),
            P(),
            P(),
            P(),
            P(),
            P(),
            P(),
        ),
        out_specs=(
            P("batch", None, None),
            P("batch", None, None),
            P(),
            P("batch", None, None),
            P("batch", None, None),
            P("batch"),
            P("batch"),
            P("batch", None, "mp"),
            P(None, "mp"),
            P("mp", "batch"),
            P("batch"),
            P("batch"),
            P(None, "batch"),
            P(None, "batch"),
            P(None, "batch", "mp"),
            P(None, "mp"),
            P(None, "mp", "batch"),
            P(None, "batch"),
            P("batch"),
            P(None, "batch"),
            P(None, "batch"),
            P(None, "batch", None),
            P(),
        ),
        check_vma=False,
    )
```

profile of v0, /device:TPU:0, one launch (start us, length us, event | category | flops | bytes accessed | tf_op | source)
XLA Modules:
  0.0 281.6 jit_solution(6844076604941716468)
XLA Ops:
  0.7 62.9 %front.1 = (f32[16,768]{1,0:T(8,128)}, bf16[6,256,768]{2,1,0:T(8,128)(2,1)}, bf16[6,256,384]{2,1,0:T(8,128)(2,1)}, bf16[6,256,128]{2,1,0:T(8,128)(2,1)}, bf16[6,...) custom-call(s32[12]{0:T(128)} %lens.3, ...), custom_call_target="tpu_custom_call" | custom-call | flops 10871635968 | bytes 40000000 | tf_op jit(solution)/shard_map/front/pallas_call | solution.py:1234
  64.2 57.8 %middle.1 = (bf16[12,256,768]{2,1,0:T(8,128)(2,1)}, bf16[12,256,768]{2,1,0:T(8,128)(2,1)}, bf16[12,256,768]{2,1,0:T(8,128)(2,1)}, f32[3,256,768]{2,1,0:T(8,128)}...) custom-call(bf16[12,197,768]{2,1,0:T(8,128)(2,1)} %img.5, ...), custom_call_target="tpu_custom_call" | custom-call | flops 14495514624 | bytes 40000000 | tf_op jit(solution)/shard_map/middle/pallas_call | solution.py:1500
  122.0 2.2 fusion
  124.2 43.3 %turn.1 = (bf16[4,2,96,768]{3,2,1,0:T(8,128)(2,1)}, bf16[4,2,96,768]{3,2,1,0:T(8,128)(2,1)}, bf16[4,2,96,768]{3,2,1,0:T(8,128)(2,1)}, f32[3,256,768]{2,1,0:T(8,1...) custom-call(bf16[12,197,768]{2,1,0:T(8,128)(2,1)} %img.5, ...), custom_call_target="tpu_custom_call" | custom-call | flops 7247757312 | bytes 40000000 | tf_op jit(solution)/shard_map/turn/pallas_call | solution.py:1658
  167.5 47.3 %back.1 = (bf16[3,256,768]{2,1,0:T(8,128)(2,1)}, bf16[3,256,768]{2,1,0:T(8,128)(2,1)}, bf16[768,512]{1,0:T(8,128)(2,1)}, bf16[768,256]{1,0:T(8,128)(2,1)}, f32[1...) custom-call(s32[12]{0:T(128)} %lens.3, ...), custom_call_target="tpu_custom_call" | custom-call | flops 16307453952 | bytes 30000000 | tf_op jit(solution)/shard_map/back/pallas_call | solution.py:1814
  214.8 0.0 copy-start.4
  214.8 0.0 copy-start.5
  214.8 53.6 %finish.1 = (bf16[12,197,768]{2,1,0:T(8,128)(2,1)}, bf16[12,40,768]{2,1,0:T(8,128)(2,1)}, bf16[12,197,768]{2,1,0:T(8,128)(2,1)}, bf16[12,40,768]{2,1,0:T(8,128)(...) custom-call(bf16[3,256,768]{2,1,0:T(8,128)(2,1)} %get-tuple-element.126.n_keep, ...), custom_call_target="tpu_custom_call" | custom-call | tf_op jit(solution)/shard_map/finish/pallas_call | solution.py:2018
  268.4 0.0 copy-done.4
  268.4 1.8 pad_maximum_fusion
  270.2 1.9 spread.1
  272.1 0.0 copy-done.5
  272.1 0.5 fusion.3
  272.6 0.0 copy-start.2
  272.6 0.0 copy-start
  272.6 4.3 %copy.54 = bf16[12,197,768]{2,1,0:T(8,128)(2,1)} copy(bf16[12,197,768]{2,1,0:T(8,128)(2,1)} %get-tuple-element.192) | data formatting | bytes 7262208
  276.9 0.0 copy-done.2
  276.9 0.9 copy.55
  277.8 0.0 copy-done
  277.8 0.0 copy-start.1
  277.8 0.0 copy-start.3
  277.8 1.8 copy.56
  279.6 0.0 copy-done.1
  279.6 0.9 copy.57
  280.5 0.0 copy-done.3
  280.5 0.8 copy.58
Async XLA Ops:
  214.8 53.6 %copy-start.4 = (f32[96,768]{1,0:T(8,128)S(1)}, f32[96,768]{1,0:T(8,128)}, u32[]{:S(2)}) copy-start(f32[96,768]{1,0:T(8,128)} %get-tuple-element.157) | copy-start | bytes 884740
  214.8 57.3 %copy-start.5 = (f32[2,128]{1,0:T(2,128)S(1)}, f32[2,128]{1,0:T(2,128)}, u32[]{:S(2)}) copy-start(f32[2,128]{1,0:T(2,128)} %get-tuple-element.141) | copy-start | bytes 3076
  272.6 4.3 %copy-start.2 = (bf16[12,40,768]{2,1,0:T(8,128)(2,1)S(1)}, bf16[12,40,768]{2,1,0:T(8,128)(2,1)}, u32[]{:S(2)}) copy-start(bf16[12,40,768]{2,1,0:T(8,128)(2,1)} %get-tuple-element.193) | copy-start | bytes 2211844
  272.6 5.1 %copy-start = (bf16[12,197,768]{2,1,0:T(8,128)(2,1)S(1)}, bf16[12,197,768]{2,1,0:T(8,128)(2,1)}, u32[]{:S(2)}) copy-start(bf16[12,197,768]{2,1,0:T(8,128)(2,1)} %get-tuple-element.195) | copy-start | bytes 10893316
  277.8 1.8 copy-start.1
  277.8 2.7 copy-start.3
where the time goes:
time: 287 us; the launch traced here: 282 us
  Pallas kernels  267 us (93%)
  local copies, waits for them, and re-layouts  9.2 us (3%)
    pallas_call x1, Pallas kernels, front(): pl.pallas_call(lambda lens, img, txt, *refs: front_kernel(dims, lens, img...  62.9 us
    pallas_call x1, Pallas kernels, middle(): pl.pallas_call(functools.partial(middle_kernel, dims, total), grid=(4,),...  57.8 us
    pallas_call x1, Pallas kernels, finish(): pl.pallas_call(functools.partial(finish_kernel, dims), in_specs=[held] *...  53.6 us
    pallas_call x1, Pallas kernels, back(): pl.pallas_call(functools.partial(back_kernel, dims), grid=(4,), in_specs=...  47.3 us
    pallas_call x1, Pallas kernels, turn(): pl.pallas_call(functools.partial(turn_kernel, dims), grid=(8,), in_specs=...  43.3 us
    unnamed x17, local copies, waits for them, and re-layouts  8.68 us

commit v1 on v0

--- a/solution.py
+++ b/solution.py
@@ -1031,7 +1031,11 @@
         self.near = (self.b, 2 * (1 - self.y) + self.c)
         self.across = (self.b, 2 * (1 - self.y) + 1 - self.c)
         self.side = (2 * self.z + 1 - self.x, self.m)
-        self.along = [(2 * ((self.z + k) % 4) + self.x, self.m) for k in range(1, 4)]
+        self.z_pair = self.z + 1 - 2 * (self.z % 2)
+        self.z_far = (self.z + 2) % 4
+        self.z_rest = (self.z_pair + 2) % 4
+        self.paired = (2 * self.z_pair + self.x, self.m)
+        self.opposite = (2 * self.z_far + self.x, self.m)
         self.batch = [((self.b + k) % 8, self.m) for k in range(1, 8)]
 
     def quarter(self, far_y, far_core):
@@ -1680,9 +1684,10 @@
 
 def back_kernel(dims, lens, d_own, d_peer, normed, qkv_far, mixed_far, qkv_own, mixed_own, wq, wo, wf,
                 fin_img, fin_txt, up_keep, up_send, down_sum,
-                keep, send, grad_pair, grad_single, cols_far, cols_own, near_img, near_txt, far_sum, up_one, down_out, up_out,
+                keep, send, grad_pair, grad_single, cols_far, cols_own, near_img, near_txt, far_sum, up_half, down_out, up_out,
                 dattn, dm_far, dm_own, dq_far, dq_own, acc_far, acc_own, w_far, w_own, o_far, o_own, dn, grad_f,
-                up_mine, up_side, up_low, up_z, down_mine, down_z, from_side, local_sem, send_sem, recv_sem):
+                up_mine, up_side, up_low, up_one, up_in, one_in, up_pass, up_last, down_mine, down_in, down_pass, down_last,
+                from_side, local_sem, send_sem, recv_sem):
     here = Place()
     i = pl.program_id(0)
     slab, quarter, local = dims.slab, dims.quarter, dims.local
@@ -1700,15 +1705,21 @@
 
     sent_near = [make(fin_img, near_img, here.near), make(fin_txt, near_txt, here.near)]
     sent_up = [make(up_send.at[j, m], up_side.at[m, j], here.side) for m in range(2) for j in range(4)]
-    sent_down = [make(down_sum.at[(here.z + k) % 4], down_z.at[k - 1], here.along[k - 1]) for k in range(1, 4)]
+    in_pair = lambda src, dst: [make(src.at[here.z_pair], dst.at[0], here.paired), make(src.at[here.z_rest], dst.at[1], here.paired)]
+    sent_down = in_pair(down_sum, down_in)
+    pass_down = make(down_pass, down_last, here.opposite)
     sent_far = [make(grad_f.at[block(2 * j + 1 - here.x)], from_side.at[j], here.side) for j in range(4)]
-    sent_low = [make(up_low.at[(here.z + k) % 4], up_z.at[k - 1], here.along[k - 1]) for k in range(1, 4)]
+    sent_low = in_pair(up_low, up_in)
+    pass_low = make(up_pass, up_last, here.opposite)
+    sent_one = in_pair(up_one, one_in)
     loaded = [pltpu.make_async_copy(up_keep, up_mine, local_sem.at[0]),
-              pltpu.make_async_copy(down_sum.at[here.z], down_mine, local_sem.at[1])]
+              pltpu.make_async_copy(down_sum.at[here.z], down_mine.at[0], local_sem.at[1]),
+              pltpu.make_async_copy(down_sum.at[here.z_far], down_mine.at[1], local_sem.at[2])]
+    add = lambda *parts: functools.reduce(lambda p, q: p + q, [v.astype(F32) for v in parts])
 
     @pl.when(i == 0)
     def _():
-        meet([here.near, here.side] + here.along)
+        meet([here.near, here.side, here.paired, here.opposite])
         for copy in loaded + sent_near + sent_up + sent_down:
             copy.start()
         for acc, cols in ((acc_far, cols_far), (acc_own, cols_own)):
@@ -1739,6 +1750,15 @@
                          w_far, o_far)
         dn[i] = part.reshape(quarter, slab, model)
 
+    @pl.when(i == 0)
+    def _():
+        for copy in loaded[1:]:
+            copy.wait()
+        for copy in sent_down:
+            copy.wait_recv()
+        down_pass[...] = add(down_mine[1], down_in[1]).astype(BF16)
+        pass_down.start()
+
     @pl.when(i == 1)
     def _():
         for t in range(4):
@@ -1752,7 +1772,7 @@
         loaded[0].wait()
         for j in range(4):
             sent_up[j].wait_recv()
-            up_low[j] = (up_mine[j, 0].astype(F32) + up_side[0, j].astype(F32)).astype(BF16)
+            up_low[j] = add(up_mine[j, 0], up_side[0, j]).astype(BF16)
         for copy in sent_low:
             copy.start()
 
@@ -1765,6 +1785,15 @@
         @pl.when(i == 2)
         def _():
             keep[...] = total
+            for copy in sent_low:
+                copy.wait_recv()
+            up_pass[...] = add(up_low[here.z_far], up_in[1]).astype(BF16)
+            pass_low.start()
+            for j in range(4):
+                sent_up[4 + j].wait_recv()
+                up_one[j] = add(up_mine[j, 1], up_side[1, j]).astype(BF16)
+            for copy in sent_one:
+                copy.start()
 
         @pl.when(i == 3)
         def _():
@@ -1773,24 +1802,21 @@
     @pl.when(i == 3)
     def _():
         grad_pair[...] = acc_own[...].astype(BF16)
-        for j in range(4):
-            sent_up[4 + j].wait_recv()
-            up_one[j] = (up_mine[j, 1].astype(F32) + up_side[1, j].astype(F32)).astype(BF16)
-        loaded[1].wait()
-        for copy in sent_down:
-            copy.wait_recv()
-        down_out[...] = (down_mine[...].astype(F32) + down_z[0].astype(F32)) + (
-            down_z[1].astype(F32) + down_z[2].astype(F32))
+        down_out[...] = add(down_mine[0], down_in[0])
         for j in range(4):
             sent_far[j].wait_recv()
-            far_sum[j] = (grad_f[block(2 * j + here.x), :].astype(F32) + from_side[j].astype(F32)).astype(BF16)
-        for copy in sent_low:
+            far_sum[j] = add(grad_f[block(2 * j + here.x), :], from_side[j]).astype(BF16)
+        pass_down.wait_recv()
+        down_out[...] += down_last[...].astype(F32)
+        for copy in sent_one:
             copy.wait_recv()
-        up_out[...] = (up_low[here.z].astype(F32) + up_z[0].astype(F32)) + (
-            up_z[1].astype(F32) + up_z[2].astype(F32))
+        up_half[0] = add(up_one[here.z], one_in[0]).astype(BF16)
+        up_half[1] = add(up_one[here.z_far], one_in[1]).astype(BF16)
+        pass_low.wait_recv()
+        up_out[...] = add(up_low[here.z], up_in[0], up_last[...])
         for copy in sent_near:
             copy.wait_recv()
-        for copy in sent_near + sent_up + sent_down + sent_far + sent_low:
+        for copy in sent_near + sent_up + sent_down + sent_far + sent_low + sent_one + [pass_down, pass_low]:
             copy.wait_send()
 
 
@@ -1808,7 +1834,7 @@
     outs = [(held, rows, BF16), (held, rows, BF16), (held, (model, 512), BF16), (held, (model, 256), BF16),
             (held, (1, 768), F32), (held, (1, 384), F32),
             (away, fin_img.shape, BF16), (away, fin_txt.shape, BF16),
-            (held, (4, piece, model), BF16), (held, (4, piece, hidden), BF16),
+            (held, (4, piece, model), BF16), (held, (2, piece, hidden), BF16),
             (held, (2, piece, hidden), F32), (held, (piece, hidden), F32)]
     slabs = lambda cols: pltpu.VMEM((quarter, slab, cols), BF16)
     return pl.pallas_call(
@@ -1826,10 +1852,13 @@
             pltpu.VMEM((256, model), BF16), pltpu.VMEM((128, model), BF16),
             pltpu.VMEM((2,) + rows, F32), pltpu.VMEM((model, model), BF16),
             pltpu.VMEM((4, 2, piece, hidden), BF16), pltpu.VMEM((2, 4, piece, hidden), BF16),
-            pltpu.VMEM((4, piece, hidden), BF16), pltpu.VMEM((3, piece, hidden), BF16),
-            pltpu.VMEM((2, piece, hidden), BF16), pltpu.VMEM((3, 2, piece, hidden), BF16),
+            pltpu.VMEM((4, piece, hidden), BF16), pltpu.VMEM((4, piece, hidden), BF16),
+            pltpu.VMEM((2, piece, hidden), BF16), pltpu.VMEM((2, piece, hidden), BF16),
+            pltpu.VMEM((piece, hidden), BF16), pltpu.VMEM((piece, hidden), BF16),
+            pltpu.VMEM((2, 2, piece, hidden), BF16), pltpu.VMEM((2, 2, piece, hidden), BF16),
+            pltpu.VMEM((2, piece, hidden), BF16), pltpu.VMEM((2, piece, hidden), BF16),
             pltpu.VMEM((4, piece, model), BF16),
-            pltpu.SemaphoreType.DMA((2,)), pltpu.SemaphoreType.DMA((20,)), pltpu.SemaphoreType.DMA((20,)),
+            pltpu.SemaphoreType.DMA((3,)), pltpu.SemaphoreType.DMA((22,)), pltpu.SemaphoreType.DMA((22,)),
         ],
         compiler_params=params(collective_id=4, has_side_effects=True),
         cost_estimate=pl.CostEstimate(
@@ -1843,9 +1872,9 @@
 
 
 def finish_kernel(dims, n_keep, n_send, dattended, states_img, states_txt, vec, fin_img, fin_txt,
-                  near_img, near_txt, grad_pair, grad_single, grad_far, up_one, own_sums, up_sums, cols_own, cols_far,
+                  near_img, near_txt, grad_pair, grad_single, grad_far, up_half, own_sums, up_sums, cols_own, cols_far,
                   out_img, out_txt, back_img, back_txt, grad_out, v_out, up_out,
-                  n_recv, s_img, s_txt, d_img, d_txt, rows, xr, zs, zr, zr_far, zr_up, far_sum, far_recv, vs, vr,
+                  n_recv, s_img, s_txt, d_img, d_txt, rows, xr, zs, z_in, z_pass, z_last, f_in, f_pass, f_last, up_last, far_sum, far_recv, vs, vr,
                   local_sem, send_sem, recv_sem):
     quarter = dims.quarter
     here = Place()
@@ -1862,7 +1891,7 @@
               pltpu.make_async_copy(states_txt.at[pl.ds(m * quarter, quarter)], s_txt, local_sem.at[1])]
     for copy in loaded:
         copy.start()
-    meet([here.core, here.near, here.side] + here.along)
+    meet([here.core, here.near, here.side, here.paired, here.opposite])
 
     n_copies = [send(n_send.at[p], n_recv.at[p], here.core) for p in range(quarter)]
     for copy in n_copies:
@@ -1876,8 +1905,12 @@
         for src, lo, hi in spans:
             x_copies.append(send(src.at[block(2 * j + 1 - x)], xr.at[j, :, pl.ds(lo, hi - lo)], here.side))
             x_copies[-1].start()
-    far_copies = [send(grad_far.at[(z + k) % 4], zr_far.at[k - 1], here.along[k - 1]) for k in range(1, 4)]
-    for copy in far_copies:
+    add = lambda *parts: functools.reduce(lambda p, q: p + q, [v.astype(F32) for v in parts])
+    in_pair = lambda src, dst: [send(src.at[here.z_pair], dst.at[0], here.paired),
+                                send(src.at[here.z_rest], dst.at[1], here.paired)]
+    up_copy = send(up_half.at[1], up_last, here.opposite)
+    far_copies = in_pair(grad_far, f_in)
+    for copy in [up_copy] + far_copies:
         copy.start()
 
     fin_local, fin_remote = [], []
@@ -1939,15 +1972,16 @@
         return vr[step]
 
     v = v + jnp.where(at < V_MP, exchange(0, v, here.core), 0.0)
+    for copy in far_copies:
+        copy.wait_recv()
+    f_pass[...] = add(grad_far[here.z_far], f_in[1]).astype(BF16)
+    far_copies.append(send(f_pass, f_last, here.opposite))
+    far_copies[-1].start()
     v = v + exchange(1, v, here.side)
-    vs[2] = v
-    vr[3 + z] = v
-    around = [send(vs.at[2], vr.at[3 + z], here.along[k - 1]) for k in range(1, 4)]
-    for copy in around:
-        copy.start()
-    up_copies = [send(up_one.at[(z + k) % 4], zr_up.at[k - 1], here.along[k - 1]) for k in range(1, 4)]
-    for copy in up_copies:
-        copy.start()
+    v = v + exchange(2, v, here.paired)
+    vs[3] = v
+    v_far = send(vs.at[3], vr.at[3], here.opposite)
+    v_far.start()
 
     def own_sum(j, k):
         src, lo, hi = spans[k]
@@ -1958,27 +1992,26 @@
     for j in range(4):
         for k, (src, lo, hi) in enumerate(spans):
             zs[j, :, lo:hi] = own_sum(j, k).astype(BF16)
-    z_copies = [send(zs.at[(z + k) % 4], zr.at[k - 1], here.along[k - 1]) for k in range(1, 4)]
+    z_copies = in_pair(zs, z_in)
     for copy in z_copies:
         copy.start()
 
-    for copy in around:
-        copy.wait_recv()
-    v = (vr[3] + vr[4]) + (vr[5] + vr[6])
-    for copy in far_copies:
-        copy.wait_recv()
-    far = grad_far[z].astype(F32)
-    for k in range(3):
-        far = far + zr_far[k].astype(F32)
-    far_sum[...] = far.astype(BF16)
+    far_copies[-1].wait_recv()
+    far_sum[...] = add(grad_far[z], f_in[0], f_last[...]).astype(BF16)
     far_copy = send(far_sum, far_recv, here.near)
     far_copy.start()
-    vs[3] = v
-    v_near = send(vs.at[3], vr.at[2], here.near)
+    v_far.wait_recv()
+    v = v + vr[3]
+    up_copy.wait_recv()
+    up_out[...] = add(up_half[0], up_last[...])
+    for copy in z_copies:
+        copy.wait_recv()
+    z_pass[...] = add(zs[here.z_far], z_in[1]).astype(BF16)
+    z_copies.append(send(z_pass, z_last, here.opposite))
+    z_copies[-1].start()
+    vs[4] = v
+    v_near = send(vs.at[4], vr.at[4], here.near)
     v_near.start()
-    for copy in up_copies:
-        copy.wait_recv()
-    up_out[...] = (up_one[z].astype(F32) + zr_up[0].astype(F32)) + (zr_up[1].astype(F32) + zr_up[2].astype(F32))
     for copy in fin_local + back_local:
         copy.wait()
     onward = []
@@ -1989,25 +2022,22 @@
             onward.append(send(at_near, at_near, here.core))
             onward[-1].start()
     far_copy.wait_recv()
-    for copy in z_copies:
-        copy.wait_recv()
+    z_copies[-1].wait_recv()
     for k, (src, lo, hi) in enumerate(spans):
-        g = own_sum(z, k) + far_recv[:, lo:hi].astype(F32)
-        for j in range(3):
-            g = g + zr[j, :, lo:hi].astype(F32)
-        grad_out[:, lo:hi] = g
+        grad_out[:, lo:hi] = own_sum(z, k) + add(
+            far_recv[:, lo:hi], z_in[0, :, lo:hi], z_last[:, lo:hi])
     v_near.wait_recv()
-    there = vr[2]
+    there = vr[4]
     v_out[...] = v + jnp.where(at < V_MP, there, 0.0)
     v_out[V_HEADS:V_HEADS + 2, :] = v[V_HEADS:V_HEADS + 2, :] + there[V_FAR:V_FAR + 2, :]
     for copy in to_other + fin_remote + onward:
         copy.wait()
-    for copy in n_copies + x_copies + far_copies + to_near + z_copies + v_copies + around + up_copies + [far_copy, v_near]:
+    for copy in n_copies + x_copies + far_copies + to_near + z_copies + v_copies + [far_copy, v_near, v_far, up_copy]:
         copy.wait_send()
 
 
 def finish(dims, n_keep, n_send, dattended, states_img, states_txt, vec, fin_img, fin_txt,
-           near_img, near_txt, grad_pair, grad_single, grad_far, up_one, *tables):
+           near_img, near_txt, grad_pair, grad_single, grad_far, up_half, *tables):
     pairs, patches, model = states_img.shape
     caption = states_txt.shape[1]
     quarter, slab = dims.quarter, dims.slab
@@ -2026,7 +2056,7 @@
             jax.ShapeDtypeStruct((pairs, caption, model), BF16),
             jax.ShapeDtypeStruct((piece, cols), F32),
             jax.ShapeDtypeStruct((V_ROWS, model), F32),
-            jax.ShapeDtypeStruct(up_one.shape[1:], F32),
+            jax.ShapeDtypeStruct(up_half.shape[1:], F32),
         ],
         scratch_shapes=[
             pltpu.VMEM((quarter, slab, model), BF16),
@@ -2036,11 +2066,11 @@
             pltpu.VMEM((quarter, caption, model), BF16),
             pltpu.VMEM((slab, model), F32),
             pltpu.VMEM((4, piece, cols), BF16), pltpu.VMEM((4, piece, cols), BF16),
-            pltpu.VMEM((3, piece, cols), BF16), pltpu.VMEM((3, piece, cols), BF16),
-            pltpu.VMEM((3,) + up_one.shape[1:], BF16),
+        ] + [pltpu.VMEM((2, piece, cols), BF16), pltpu.VMEM((piece, cols), BF16), pltpu.VMEM((piece, cols), BF16)] * 2 + [
+            pltpu.VMEM(up_half.shape[1:], BF16),
             pltpu.VMEM((piece, cols), BF16), pltpu.VMEM((piece, cols), BF16),
-            pltpu.VMEM((4, V_ROWS, model), F32),
-            pltpu.VMEM((7, V_ROWS, model), F32),
+            pltpu.VMEM((5, V_ROWS, model), F32),
+            pltpu.VMEM((5, V_ROWS, model), F32),
             pltpu.SemaphoreType.DMA((6 + 2 * quarter,)),
             pltpu.SemaphoreType.DMA((n_remote,)),
             pltpu.SemaphoreType.DMA((n_remote,)),
@@ -2048,7 +2078,7 @@
         compiler_params=params(collective_id=1, has_side_effects=True),
         name="finish",
     )(n_keep, n_send, dattended, states_img, states_txt, vec, fin_img, fin_txt,
-      near_img, near_txt, grad_pair, grad_single, grad_far, up_one, *tables)
+      near_img, near_txt, grad_pair, grad_single, grad_far, up_half, *tables)
 
 
 def spread_kernel(cols, at, sums, grad, gains, shifts, *refs):
@@ -2189,7 +2219,7 @@
     contrast_loss = scalars[0, :1]
     grad_logit_scale = scalars[1, :1]
     if one_kernel:
-        (n_keep, n_send, grad_o01, grad_o2, cols_far, cols_own, near_img, near_txt, far_sum, up_one, grad_down,
+        (n_keep, n_send, grad_o01, grad_o2, cols_far, cols_own, near_img, near_txt, far_sum, up_half, grad_down,
          up_low) = back(
             dims, caption_lengths, dattn, dattn_peer, normed, qkv_far, mixed_far, qkv_own, mixed_own,
             own_w, output_weight, wf, fin_img, fin_txt, up_keep, up_send, down_sum)
@@ -2206,7 +2236,7 @@
     if one_kernel:
         image_output, text_output, image_grad, text_grad, attn_grad, sums, up_high = finish(
             dims, n_keep, n_send, dattended, image_states, text_states, vec, fin_img, fin_txt,
-            near_img, near_txt, grad_o01, grad_o2, far_sum, up_one, own_sums, up_sums, cols_own, cols_far)
+            near_img, near_txt, grad_o01, grad_o2, far_sum, up_half, own_sums, up_sums, cols_own, cols_far)
         *vectors, grad_qkv, grad_output_weight = spread(
             local, batch_at.reshape(1), sums, attn_grad, grad_head_gain, grad_head_shift)
         flat = lambda v: v.reshape(-1)

time: 287 us -> 285 us (level)
    pallas_call x1, Pallas kernels: 53.6 us -> 44.4 us  [finish(): pl.pallas_call(functools.partial(finish_kernel, dims), in_specs=[held] *...]
    pallas_call x1, Pallas kernels: 47.3 us -> 54.8 us  [back(): pl.pallas_call(functools.partial(back_kernel, dims), grid=(4,), in_specs=...]
where the time goes in v1:
time: 285 us; the launch traced here: 280 us
  Pallas kernels  265 us (93%)
  local copies, waits for them, and re-layouts  9.2 us (3%)
    pallas_call x1, Pallas kernels, front(): pl.pallas_call(lambda lens, img, txt, *refs: front_kernel(dims, lens, img...  62.9 us
    pallas_call x1, Pallas kernels, middle(): pl.pallas_call(functools.partial(middle_kernel, dims, total), grid=(4,),...  57.8 us
    pallas_call x1, Pallas kernels, back(): pl.pallas_call(functools.partial(back_kernel, dims), grid=(4,), in_specs=...  54.8 us
    pallas_call x1, Pallas kernels, finish(): pl.pallas_call(functools.partial(finish_kernel, dims), in_specs=[held] *...  44.4 us
    pallas_call x1, Pallas kernels, turn(): pl.pallas_call(functools.partial(turn_kernel, dims), grid=(8,), in_specs=...  43.3 us
    unnamed x17, local copies, waits for them, and re-layouts  8.68 us

profile of v1, /device:TPU:0, one launch (start us, length us, event | category | flops | bytes accessed | tf_op | source)
XLA Modules:
  0.0 279.9 jit_solution(1782673348863062251)
XLA Ops:
  0.7 62.9 %front.1 = (f32[16,768]{1,0:T(8,128)}, bf16[6,256,768]{2,1,0:T(8,128)(2,1)}, bf16[6,256,384]{2,1,0:T(8,128)(2,1)}, bf16[6,256,128]{2,1,0:T(8,128)(2,1)}, bf16[6,...) custom-call(s32[12]{0:T(128)} %lens.3, ...), custom_call_target="tpu_custom_call" | custom-call | flops 10871635968 | bytes 40000000 | tf_op jit(solution)/shard_map/front/pallas_call | solution.py:1238
  64.2 57.8 %middle.1 = (bf16[12,256,768]{2,1,0:T(8,128)(2,1)}, bf16[12,256,768]{2,1,0:T(8,128)(2,1)}, bf16[12,256,768]{2,1,0:T(8,128)(2,1)}, f32[3,256,768]{2,1,0:T(8,128)}...) custom-call(bf16[12,197,768]{2,1,0:T(8,128)(2,1)} %img.5, ...), custom_call_target="tpu_custom_call" | custom-call | flops 14495514624 | bytes 40000000 | tf_op jit(solution)/shard_map/middle/pallas_call | solution.py:1504
  122.0 2.2 fusion
  124.2 43.3 %turn.1 = (bf16[4,2,96,768]{3,2,1,0:T(8,128)(2,1)}, bf16[4,2,96,768]{3,2,1,0:T(8,128)(2,1)}, bf16[4,2,96,768]{3,2,1,0:T(8,128)(2,1)}, f32[3,256,768]{2,1,0:T(8,1...) custom-call(bf16[12,197,768]{2,1,0:T(8,128)(2,1)} %img.5, ...), custom_call_target="tpu_custom_call" | custom-call | flops 7247757312 | bytes 40000000 | tf_op jit(solution)/shard_map/turn/pallas_call | solution.py:1662
  167.5 54.8 %back.1 = (bf16[3,256,768]{2,1,0:T(8,128)(2,1)}, bf16[3,256,768]{2,1,0:T(8,128)(2,1)}, bf16[768,512]{1,0:T(8,128)(2,1)}, bf16[768,256]{1,0:T(8,128)(2,1)}, f32[1...) custom-call(s32[12]{0:T(128)} %lens.3, ...), custom_call_target="tpu_custom_call" | custom-call | flops 16307453952 | bytes 30000000 | tf_op jit(solution)/shard_map/back/pallas_call | solution.py:1840
  222.3 0.0 copy-start.4
  222.3 0.0 copy-start.5
  222.3 44.4 %finish.1 = (bf16[12,197,768]{2,1,0:T(8,128)(2,1)}, bf16[12,40,768]{2,1,0:T(8,128)(2,1)}, bf16[12,197,768]{2,1,0:T(8,128)(2,1)}, bf16[12,40,768]{2,1,0:T(8,128)(...) custom-call(bf16[3,256,768]{2,1,0:T(8,128)(2,1)} %get-tuple-element.126.n_keep, ...), custom_call_target="tpu_custom_call" | custom-call | tf_op jit(solution)/shard_map/finish/pallas_call | solution.py:2048
  266.7 0.0 copy-done.4
  266.7 1.8 pad_maximum_fusion
  268.5 1.9 spread.1
  270.4 0.0 copy-done.5
  270.4 0.5 fusion.3
  270.9 0.0 copy-start.2
  270.9 0.0 copy-start
  270.9 4.3 %copy.54 = bf16[12,197,768]{2,1,0:T(8,128)(2,1)} copy(bf16[12,197,768]{2,1,0:T(8,128)(2,1)} %get-tuple-element.192) | data formatting | bytes 7262208
  275.2 0.0 copy-done.2
  275.2 0.9 copy.55
  276.1 0.0 copy-done
  276.1 0.0 copy-start.1
  276.1 0.0 copy-start.3
  276.1 1.8 copy.56
  277.9 0.0 copy-done.1
  277.9 0.9 copy.57
  278.8 0.0 copy-done.3
  278.8 0.8 copy.58
Async XLA Ops:
  222.3 44.4 %copy-start.4 = (f32[96,768]{1,0:T(8,128)S(1)}, f32[96,768]{1,0:T(8,128)}, u32[]{:S(2)}) copy-start(f32[96,768]{1,0:T(8,128)} %get-tuple-element.157) | copy-start | bytes 884740
  222.3 48.1 %copy-start.5 = (f32[2,128]{1,0:T(2,128)S(1)}, f32[2,128]{1,0:T(2,128)}, u32[]{:S(2)}) copy-start(f32[2,128]{1,0:T(2,128)} %get-tuple-element.141) | copy-start | bytes 3076
  270.9 4.3 %copy-start.2 = (bf16[12,40,768]{2,1,0:T(8,128)(2,1)S(1)}, bf16[12,40,768]{2,1,0:T(8,128)(2,1)}, u32[]{:S(2)}) copy-start(bf16[12,40,768]{2,1,0:T(8,128)(2,1)} %get-tuple-element.193) | copy-start | bytes 2211844
  270.9 5.1 %copy-start = (bf16[12,197,768]{2,1,0:T(8,128)(2,1)S(1)}, bf16[12,197,768]{2,1,0:T(8,128)(2,1)}, u32[]{:S(2)}) copy-start(bf16[12,197,768]{2,1,0:T(8,128)(2,1)} %get-tuple-element.195) | copy-start | bytes 10893316
  276.1 1.8 copy-start.1
  276.1 2.7 copy-start.3

commit v2 on v1

--- a/solution.py
+++ b/solution.py
@@ -1057,7 +1057,7 @@
 
 def front_kernel(dims, lens, img, txt, vectors, bias, own_w, own_o,
                  vec, normed, qkv, mixed, qkv_far, mixed_far, far_w, attended, attn, expert, expert_peer, cls, cls_peer,
-                 rows, w, w2, ow, b, wf, far_bias, n_all, rest, m_all, m_far, q_own, q_far, a_send, a_recv, e_send, c_recv,
+                 rows, w, w2, ow, b, wf, far_bias, n_all, rest, m_all, m_far, q_own, q_far, a_send, a_recv, e_send, c_recv, held,
                  local_sem, send_sem, recv_sem):
     here = Place()
     i = pl.program_id(0)
@@ -1177,9 +1177,11 @@
         @pl.when(i >= 6)
         def _():
             j = i - 6
-            for p in range(quarter):
+            held[...] = part
+
+            def one_residual(p, c):
                 load_rows(dims, p, img, txt, rows)
-                a = part[p] + a_recv[j, p].astype(F32)
+                a = held[p] + a_recv[j, p].astype(F32)
                 x = rows[...] + vector(vec, A_SCALE) * (a + vector(vec, A_BIAS))
                 n, _ = normalise(x)
                 e_img = n[0:ip] * vector(vec, GAIN2) + vector(vec, SHIFT2)
@@ -1197,6 +1199,9 @@
                     attended[p] = x
                     attn[p] = a
 
+                return c
+
+            lax.fori_loop(0, quarter, one_residual, 0)
 
     @pl.when(i == 7)
     def _():
@@ -1258,6 +1263,7 @@
             pltpu.VMEM(block(384), BF16), pltpu.VMEM(block(768), BF16),
             pltpu.VMEM((2,) + block(model), BF16), pltpu.VMEM((2,) + block(model), BF16),
             pltpu.VMEM((2 * quarter, slab, model), BF16), pltpu.VMEM((4, 8, model), F32),
+            pltpu.VMEM(block(model), F32),
             pltpu.SemaphoreType.DMA((1 + 2 * quarter,)),
             pltpu.SemaphoreType.DMA((n_remote,)), pltpu.SemaphoreType.DMA((n_remote,)),
         ],
@@ -1535,7 +1541,11 @@
     i = pl.program_id(0)
     piece = side_send.shape[2]
     sent_near = remote(d_near, d_far, send_sem, recv_sem, 0, here.near)
-    sent_core = [remote(dattn.at[p], n_peer.at[p], send_sem, recv_sem, 1 + p, here.core) for p in range(quarter)]
+
+    def over(p):
+        return remote(dattn.at[p], n_peer.at[p], send_sem, recv_sem, 1 + p, here.core)
+
+    sent_core = [over(p) for p in range(quarter)]
     sent_side = [remote(side_send.at[j], side_recv.at[j], send_sem, recv_sem, 1 + quarter + j, here.side)
                  for j in range(4)]
     loaded = [pltpu.make_async_copy(src, dst, local_sem.at[j]) for j, (src, dst) in enumerate((
@@ -1601,7 +1611,7 @@
             rows[0:1, :] += dcls[p, 0:1, :]
             rows[ip:ip + 1, :] += dcls[p, 1:2, :]
 
-        for p in range(quarter):
+        def norm(p, c):
             load(p)
             for m, lo, hi in ((0, 0, ip), (1, ip, dims.slab)):
                 n, r = normalise(attended[p, lo:hi, :])
@@ -1615,7 +1625,10 @@
                 a = attn[p, lo:hi, :] + vector(vec, A_BIAS)
                 sums[4:5, :] += jnp.sum(d * a, axis=0, keepdims=True)
                 sums[5:6, :] += jnp.sum(sd, axis=0, keepdims=True)
-            sent_core[p].start()
+            over(p).start()
+            return c
+
+        lax.fori_loop(0, quarter, norm, 0)
         sent_near.wait_recv()
 
         def final(p, c):
@@ -1684,9 +1697,9 @@
 
 def back_kernel(dims, lens, d_own, d_peer, normed, qkv_far, mixed_far, qkv_own, mixed_own, wq, wo, wf,
                 fin_img, fin_txt, up_keep, up_send, down_sum,
-                keep, send, grad_pair, grad_single, cols_far, cols_own, near_img, near_txt, far_sum, up_half, down_out, up_out,
+                keep, send, grad_pair, grad_single, cols_far, cols_own, near_img, near_txt, far_sum, up_one, down_out, up_out,
                 dattn, dm_far, dm_own, dq_far, dq_own, acc_far, acc_own, w_far, w_own, o_far, o_own, dn, grad_f,
-                up_mine, up_side, up_low, up_one, up_in, one_in, up_pass, up_last, down_mine, down_in, down_pass, down_last,
+                up_mine, up_side, up_low, up_in, up_pass, up_last, down_mine, down_in, down_pass, down_last,
                 from_side, local_sem, send_sem, recv_sem):
     here = Place()
     i = pl.program_id(0)
@@ -1711,7 +1724,6 @@
     sent_far = [make(grad_f.at[block(2 * j + 1 - here.x)], from_side.at[j], here.side) for j in range(4)]
     sent_low = in_pair(up_low, up_in)
     pass_low = make(up_pass, up_last, here.opposite)
-    sent_one = in_pair(up_one, one_in)
     loaded = [pltpu.make_async_copy(up_keep, up_mine, local_sem.at[0]),
               pltpu.make_async_copy(down_sum.at[here.z], down_mine.at[0], local_sem.at[1]),
               pltpu.make_async_copy(down_sum.at[here.z_far], down_mine.at[1], local_sem.at[2])]
@@ -1789,11 +1801,6 @@
                 copy.wait_recv()
             up_pass[...] = add(up_low[here.z_far], up_in[1]).astype(BF16)
             pass_low.start()
-            for j in range(4):
-                sent_up[4 + j].wait_recv()
-                up_one[j] = add(up_mine[j, 1], up_side[1, j]).astype(BF16)
-            for copy in sent_one:
-                copy.start()
 
         @pl.when(i == 3)
         def _():
@@ -1808,15 +1815,14 @@
             far_sum[j] = add(grad_f[block(2 * j + here.x), :], from_side[j]).astype(BF16)
         pass_down.wait_recv()
         down_out[...] += down_last[...].astype(F32)
-        for copy in sent_one:
-            copy.wait_recv()
-        up_half[0] = add(up_one[here.z], one_in[0]).astype(BF16)
-        up_half[1] = add(up_one[here.z_far], one_in[1]).astype(BF16)
+        for j in range(4):
+            sent_up[4 + j].wait_recv()
+            up_one[j] = add(up_mine[j, 1], up_side[1, j]).astype(BF16)
         pass_low.wait_recv()
         up_out[...] = add(up_low[here.z], up_in[0], up_last[...])
         for copy in sent_near:
             copy.wait_recv()
-        for copy in sent_near + sent_up + sent_down + sent_far + sent_low + sent_one + [pass_down, pass_low]:
+        for copy in sent_near + sent_up + sent_down + sent_far + sent_low + [pass_down, pass_low]:
             copy.wait_send()
 
 
@@ -1834,7 +1840,7 @@
     outs = [(held, rows, BF16), (held, rows, BF16), (held, (model, 512), BF16), (held, (model, 256), BF16),
             (held, (1, 768), F32), (held, (1, 384), F32),
             (away, fin_img.shape, BF16), (away, fin_txt.shape, BF16),
-            (held, (4, piece, model), BF16), (held, (2, piece, hidden), BF16),
+            (held, (4, piece, model), BF16), (held, (4, piece, hidden), BF16),
             (held, (2, piece, hidden), F32), (held, (piece, hidden), F32)]
     slabs = lambda cols: pltpu.VMEM((quarter, slab, cols), BF16)
     return pl.pallas_call(
@@ -1852,13 +1858,12 @@
             pltpu.VMEM((256, model), BF16), pltpu.VMEM((128, model), BF16),
             pltpu.VMEM((2,) + rows, F32), pltpu.VMEM((model, model), BF16),
             pltpu.VMEM((4, 2, piece, hidden), BF16), pltpu.VMEM((2, 4, piece, hidden), BF16),
-            pltpu.VMEM((4, piece, hidden), BF16), pltpu.VMEM((4, piece, hidden), BF16),
-            pltpu.VMEM((2, piece, hidden), BF16), pltpu.VMEM((2, piece, hidden), BF16),
+            pltpu.VMEM((4, piece, hidden), BF16), pltpu.VMEM((2, piece, hidden), BF16),
             pltpu.VMEM((piece, hidden), BF16), pltpu.VMEM((piece, hidden), BF16),
             pltpu.VMEM((2, 2, piece, hidden), BF16), pltpu.VMEM((2, 2, piece, hidden), BF16),
             pltpu.VMEM((2, piece, hidden), BF16), pltpu.VMEM((2, piece, hidden), BF16),
             pltpu.VMEM((4, piece, model), BF16),
-            pltpu.SemaphoreType.DMA((3,)), pltpu.SemaphoreType.DMA((22,)), pltpu.SemaphoreType.DMA((22,)),
+            pltpu.SemaphoreType.DMA((3,)), pltpu.SemaphoreType.DMA((20,)), pltpu.SemaphoreType.DMA((20,)),
         ],
         compiler_params=params(collective_id=4, has_side_effects=True),
         cost_estimate=pl.CostEstimate(
@@ -1872,9 +1877,9 @@
 
 
 def finish_kernel(dims, n_keep, n_send, dattended, states_img, states_txt, vec, fin_img, fin_txt,
-                  near_img, near_txt, grad_pair, grad_single, grad_far, up_half, own_sums, up_sums, cols_own, cols_far,
-                  out_img, out_txt, back_img, back_txt, grad_out, v_out, up_out,
-                  n_recv, s_img, s_txt, d_img, d_txt, rows, xr, zs, z_in, z_pass, z_last, f_in, f_pass, f_last, up_last, far_sum, far_recv, vs, vr,
+                  near_img, near_txt, grad_pair, grad_single, grad_far, up_one, own_sums, up_sums, cols_own, cols_far,
+                  core_img, core_txt, across_img, across_txt, back_img, back_txt, grad_out, v_out, up_out,
+                  n_recv, s_img, s_txt, d_img, d_txt, rows, xr, zs, z_in, z_pass, z_last, f_in, f_pass, f_last, u_in, u_pass, u_last, far_sum, far_recv, vs, vr,
                   local_sem, send_sem, recv_sem):
     quarter = dims.quarter
     here = Place()
@@ -1908,18 +1913,13 @@
     add = lambda *parts: functools.reduce(lambda p, q: p + q, [v.astype(F32) for v in parts])
     in_pair = lambda src, dst: [send(src.at[here.z_pair], dst.at[0], here.paired),
                                 send(src.at[here.z_rest], dst.at[1], here.paired)]
-    up_copy = send(up_half.at[1], up_last, here.opposite)
     far_copies = in_pair(grad_far, f_in)
-    for copy in [up_copy] + far_copies:
+    up_copies = in_pair(up_one, u_in)
+    for copy in far_copies + up_copies:
         copy.start()
 
-    fin_local, fin_remote = [], []
-    for j, (src, dst, q) in enumerate((
-        (fin_img, out_img, m), (fin_txt, out_txt, m), (near_img, out_img, near_quarter), (near_txt, out_txt, near_quarter),
-    )):
-        at = pl.ds(q * quarter, quarter)
-        fin_local.append(pltpu.make_async_copy(src, dst.at[at], local_sem.at[2 + j]))
-        fin_remote.append(send(src, dst.at[at], here.core))
+    fin_remote = [send(src, dst, here.core) for src, dst in (
+        (fin_img, core_img), (fin_txt, core_txt), (near_img, across_img), (near_txt, across_txt))]
 
     rows[...] = jnp.zeros_like(rows)
     for copy in loaded:
@@ -1942,9 +1942,9 @@
             to_near[-1].start()
             to_other.append(send(src.at[p], at, here.core))
             to_other[-1].start()
-            back_local.append(pltpu.make_async_copy(src.at[p], at, local_sem.at[6 + 2 * p + j]))
+            back_local.append(pltpu.make_async_copy(src.at[p], at, local_sem.at[2 + 2 * p + j]))
             back_local[-1].start()
-    for copy in fin_local + fin_remote:
+    for copy in fin_remote:
         copy.start()
 
     at = lax.broadcasted_iota(jnp.int32, (V_ROWS, 1), 0)
@@ -1978,10 +1978,15 @@
     far_copies.append(send(f_pass, f_last, here.opposite))
     far_copies[-1].start()
     v = v + exchange(1, v, here.side)
+    for copy in up_copies:
+        copy.wait_recv()
+    u_pass[...] = add(up_one[here.z_far], u_in[1]).astype(BF16)
     v = v + exchange(2, v, here.paired)
     vs[3] = v
     v_far = send(vs.at[3], vr.at[3], here.opposite)
     v_far.start()
+    up_copies.append(send(u_pass, u_last, here.opposite))
+    up_copies[-1].start()
 
     def own_sum(j, k):
         src, lo, hi = spans[k]
@@ -2002,8 +2007,8 @@
     far_copy.start()
     v_far.wait_recv()
     v = v + vr[3]
-    up_copy.wait_recv()
-    up_out[...] = add(up_half[0], up_last[...])
+    up_copies[-1].wait_recv()
+    up_out[...] = add(up_one[z], u_in[0], u_last[...])
     for copy in z_copies:
         copy.wait_recv()
     z_pass[...] = add(zs[here.z_far], z_in[1]).astype(BF16)
@@ -2012,7 +2017,7 @@
     vs[4] = v
     v_near = send(vs.at[4], vr.at[4], here.near)
     v_near.start()
-    for copy in fin_local + back_local:
+    for copy in back_local:
         copy.wait()
     onward = []
     for p in range(quarter):
@@ -2032,12 +2037,12 @@
     v_out[V_HEADS:V_HEADS + 2, :] = v[V_HEADS:V_HEADS + 2, :] + there[V_FAR:V_FAR + 2, :]
     for copy in to_other + fin_remote + onward:
         copy.wait()
-    for copy in n_copies + x_copies + far_copies + to_near + z_copies + v_copies + [far_copy, v_near, v_far, up_copy]:
+    for copy in n_copies + x_copies + far_copies + to_near + z_copies + v_copies + up_copies + [far_copy, v_near, v_far]:
         copy.wait_send()
 
 
 def finish(dims, n_keep, n_send, dattended, states_img, states_txt, vec, fin_img, fin_txt,
-           near_img, near_txt, grad_pair, grad_single, grad_far, up_half, *tables):
+           near_img, near_txt, grad_pair, grad_single, grad_far, up_one, *tables):
     pairs, patches, model = states_img.shape
     caption = states_txt.shape[1]
     quarter, slab = dims.quarter, dims.slab
@@ -2047,16 +2052,14 @@
     n_remote = 7 * quarter + 28
     return pl.pallas_call(
         functools.partial(finish_kernel, dims),
-        in_specs=[held] * 3 + [away] * 2 + [held] * 13,
-        out_specs=[away] * 4 + [held] * 3,
-        out_shape=[
-            jax.ShapeDtypeStruct((pairs, patches, model), BF16),
-            jax.ShapeDtypeStruct((pairs, caption, model), BF16),
+        in_specs=[held, away, held] + [away] * 2 + [held] + [away] * 4 + [held] * 8,
+        out_specs=[away] * 6 + [held] * 3,
+        out_shape=[jax.ShapeDtypeStruct(v.shape, BF16) for v in (fin_img, fin_txt) * 2] + [
             jax.ShapeDtypeStruct((pairs, patches, model), BF16),
             jax.ShapeDtypeStruct((pairs, caption, model), BF16),
             jax.ShapeDtypeStruct((piece, cols), F32),
             jax.ShapeDtypeStruct((V_ROWS, model), F32),
-            jax.ShapeDtypeStruct(up_half.shape[1:], F32),
+            jax.ShapeDtypeStruct(up_one.shape[1:], F32),
         ],
         scratch_shapes=[
             pltpu.VMEM((quarter, slab, model), BF16),
@@ -2067,26 +2070,45 @@
             pltpu.VMEM((slab, model), F32),
             pltpu.VMEM((4, piece, cols), BF16), pltpu.VMEM((4, piece, cols), BF16),
         ] + [pltpu.VMEM((2, piece, cols), BF16), pltpu.VMEM((piece, cols), BF16), pltpu.VMEM((piece, cols), BF16)] * 2 + [
-            pltpu.VMEM(up_half.shape[1:], BF16),
+            pltpu.VMEM((2,) + up_one.shape[1:], BF16), pltpu.VMEM(up_one.shape[1:], BF16), pltpu.VMEM(up_one.shape[1:], BF16),
             pltpu.VMEM((piece, cols), BF16), pltpu.VMEM((piece, cols), BF16),
             pltpu.VMEM((5, V_ROWS, model), F32),
             pltpu.VMEM((5, V_ROWS, model), F32),
-            pltpu.SemaphoreType.DMA((6 + 2 * quarter,)),
+            pltpu.SemaphoreType.DMA((2 + 2 * quarter,)),
             pltpu.SemaphoreType.DMA((n_remote,)),
             pltpu.SemaphoreType.DMA((n_remote,)),
         ],
         compiler_params=params(collective_id=1, has_side_effects=True),
         name="finish",
     )(n_keep, n_send, dattended, states_img, states_txt, vec, fin_img, fin_txt,
-      near_img, near_txt, grad_pair, grad_single, grad_far, up_half, *tables)
-
-
-def spread_kernel(cols, at, sums, grad, gains, shifts, *refs):
-    *outs, qkv, out_w, turned = refs
-    back = sums.shape[1] - at[0] * cols
+      near_img, near_txt, grad_pair, grad_single, grad_far, up_one, *tables)
+
+
+def spread_kernel(dims, cols, sums, grad, gains, shifts, up_low, up_high, down, head_in, dproj, *refs):
+    forward, refs = refs[:8], refs[8:]
+    back_img, back_txt, *refs = refs
+    outs, refs = refs[:12], refs[12:]
+    (qkv, out_w, up_out, down_out, head_out, out_img, out_txt, grad_img, grad_txt,
+     turned, held_img, held_txt, in_sem, out_sem) = refs
+    here = Place()
+    quarter = dims.quarter
+    whose = [here.quarter(0, 0), here.quarter(1, 0), here.quarter(0, 1), here.quarter(1, 1)]
+    place = lambda q: pl.ds(q * quarter, quarter)
+    comes, goes = [], []
+    for r in range(4):
+        for j, (held, src, dst, back, to) in enumerate((
+            (held_img, forward[2 * r], out_img, back_img, grad_img), (held_txt, forward[2 * r + 1], out_txt, back_txt, grad_txt),
+        )):
+            for k, (source, target, q) in enumerate(((src, dst, whose[r]), (back.at[place(r)], to, r))):
+                at = 4 * r + 2 * j + k
+                comes.append(pltpu.make_async_copy(source, held.at[2 * r + k], in_sem.at[at]))
+                goes.append(pltpu.make_async_copy(held.at[2 * r + k], target.at[place(q)], out_sem.at[at]))
+    for copy in comes:
+        copy.start()
+    turn_by = sums.shape[1] - here.b * cols
 
     def slice_of(value):
-        return pltpu.roll(value, back, 1)[:, 0:cols]
+        return pltpu.roll(value, turn_by, 1)[:, 0:cols]
 
     mine = slice_of(sums[...])
     for out, (lo, count) in zip(outs[:8], ((0, 1), (1, 1), (7, 1), (6, 1), (2, 2), (4, 2), (9, 2), (8, 1))):
@@ -2105,27 +2127,43 @@
     turned[0:cols, 0:two] = grad[:, 3 * two:4 * two]
     turned[0:cols, two:two + one] = grad[:, 4 * two + 3 * one:4 * two + 4 * one]
     out_w[...] = turned[...].T[0:two + one, 0:cols]
-
-
-def spread(local, at, sums, grad, gains, shifts):
+    up_out[0] = up_low[...]
+    up_out[1] = up_high[...]
+    down_out[...] = down[...]
+    for come, go in zip(comes, goes):
+        come.wait()
+        go.start()
+    for m in range(2):
+        part = pltpu.roll(head_in[m].astype(F32), turn_by, 1)[:, 0:128].astype(BF16)
+        head_out[m] = t_dot(part, dproj[m])[0:cols]
+    for go in goes:
+        go.wait()
+
+
+def spread(dims, sums, grad, gains, shifts, up_low, up_high, down, head_in, dproj, forward, back_img, back_txt):
     cols, model = grad.shape[0], sums.shape[1]
+    local, quarter = dims.local, dims.quarter
     assert cols <= 128
     shapes = [(1, cols)] * 4 + [(2, cols)] * 3 + [(1, cols)] + [(2, cols)] * 2 + [(2, model), (2, local)]
-    shapes += [(3, cols, local), (local, cols)]
-    args = (sums, grad, gains, shifts)
+    shapes += [(3, cols, local), (local, cols), (2,) + up_low.shape, down.shape, (2, cols, dproj.shape[2])]
+    held = pl.BlockSpec(memory_space=pltpu.VMEM)
+    away = pl.BlockSpec(memory_space=pl.ANY)
+    args = (sums, grad, gains, shifts, up_low, up_high, down, head_in, dproj)
     return pl.pallas_call(
-        functools.partial(spread_kernel, cols),
-        grid_spec=pltpu.PrefetchScalarGridSpec(
-            num_scalar_prefetch=1, grid=(1,),
-            in_specs=[spec_whole(v) for v in args],
-            out_specs=[pl.BlockSpec(v, lambda i, o, n=len(v): (0,) * n) for v in shapes],
-            scratch_shapes=[pltpu.VMEM((128, 256), F32)],
-        ),
-        out_shape=[jax.ShapeDtypeStruct(v, F32) for v in shapes],
+        functools.partial(spread_kernel, dims, cols),
+        in_specs=[held] * len(args) + [away] * 10,
+        out_specs=[held] * len(shapes) + [away] * 4,
+        out_shape=[jax.ShapeDtypeStruct(v, F32) for v in shapes]
+        + [jax.ShapeDtypeStruct(v.shape, BF16) for v in (back_img, back_txt) * 2],
+        scratch_shapes=[
+            pltpu.VMEM((128, 256), F32),
+            pltpu.VMEM((8, quarter, dims.patches, model), BF16), pltpu.VMEM((8, quarter, dims.caption, model), BF16),
+            pltpu.SemaphoreType.DMA((16,)), pltpu.SemaphoreType.DMA((16,)),
+        ],
         compiler_params=params(),
-        cost_estimate=pl.CostEstimate(flops=1_000_000, bytes_accessed=1_000_000, transcendentals=0),
+        cost_estimate=pl.CostEstimate(flops=1_000_000, bytes_accessed=20_000_000, transcendentals=0),
         name="spread",
-    )(at, *args)
+    )(*args, *forward, back_img, back_txt)
 
 
 def per_device(
@@ -2219,7 +2257,7 @@
     contrast_loss = scalars[0, :1]
     grad_logit_scale = scalars[1, :1]
     if one_kernel:
-        (n_keep, n_send, grad_o01, grad_o2, cols_far, cols_own, near_img, near_txt, far_sum, up_half, grad_down,
+        (n_keep, n_send, grad_o01, grad_o2, cols_far, cols_own, near_img, near_txt, far_sum, up_one, grad_down,
          up_low) = back(
             dims, caption_lengths, dattn, dattn_peer, normed, qkv_far, mixed_far, qkv_own, mixed_own,
             own_w, output_weight, wf, fin_img, fin_txt, up_keep, up_send, down_sum)
@@ -2231,14 +2269,16 @@
             prior=(n_keep, n_send))
     cols = model // batch_size
     mine = lambda v, axis: lax.dynamic_slice_in_dim(v, batch_at * cols, cols, axis=axis)
-    grad_head_weight = jnp.einsum("mnc,mne->mce", mine(head_in, 2), dproj, preferred_element_type=F32)
     pair, single = 2 * HEAD_DIM, HEAD_DIM
     if one_kernel:
-        image_output, text_output, image_grad, text_grad, attn_grad, sums, up_high = finish(
+        core_img, core_txt, across_img, across_txt, back_img, back_txt, attn_grad, sums, up_high = finish(
             dims, n_keep, n_send, dattended, image_states, text_states, vec, fin_img, fin_txt,
-            near_img, near_txt, grad_o01, grad_o2, far_sum, up_half, own_sums, up_sums, cols_own, cols_far)
-        *vectors, grad_qkv, grad_output_weight = spread(
-            local, batch_at.reshape(1), sums, attn_grad, grad_head_gain, grad_head_shift)
+            near_img, near_txt, grad_o01, grad_o2, far_sum, up_one, own_sums, up_sums, cols_own, cols_far)
+        forward = (fin_img, fin_txt, near_img, near_txt, core_img, core_txt, across_img, across_txt)
+        (*vectors, grad_qkv, grad_output_weight, grad_up, grad_down, grad_head_weight,
+         image_output, text_output, image_grad, text_grad) = spread(
+            dims, sums, attn_grad, grad_head_gain, grad_head_shift, up_low, up_high, grad_down, head_in, dproj,
+            forward, back_img, back_txt)
         flat = lambda v: v.reshape(-1)
         return (
             image_output,
@@ -2255,7 +2295,7 @@
             flat(vectors[3]),
             vectors[4],
             vectors[5],
-            jnp.stack([up_low, up_high]),
+            grad_up,
             vectors[10],
             jnp.transpose(grad_down, (0, 2, 1)),
             vectors[6],
@@ -2266,6 +2306,7 @@
             grad_logit_scale,
         )
     else:
+        grad_head_weight = jnp.einsum("mnc,mne->mce", mine(head_in, 2), dproj, preferred_element_type=F32)
         grad_expert_up = expert_sum[:2].astype(F32)
         grad_expert_down = jnp.transpose(expert_sum[2:].astype(F32), (0, 2, 1))
         cols_own = cols_own.reshape(3, pair)[::2]

time: 285 us -> 272 us (0.954); the launches traced: 280 us -> 272 us
  local copies, waits for them, and re-layouts: 9.2 us -> 0.52 us
  Pallas kernels: 265 us -> 270 us
    pallas_call x2, Pallas kernels: 46.3 us -> 55.7 us  [the longest x1 45.9 us: finish(): pl.pallas_call(functools.partial(finish_kernel, dims), in_specs=[held, aw...]
    unnamed x17 -> x2, local copies, waits for them, and re-layouts: 8.68 us -> 0.01 us
    pallas_call x1, Pallas kernels: 54.8 us -> 50.4 us  [back(): pl.pallas_call(functools.partial(back_kernel, dims), grid=(4,), in_specs=...]
where the time goes in v2:
time: 272 us
  Pallas kernels  270 us (99%)
    pallas_call x1, Pallas kernels, front(): pl.pallas_call(lambda lens, img, txt, *refs: front_kernel(dims, lens, img...  63.2 us
    pallas_call x1, Pallas kernels, middle(): pl.pallas_call(functools.partial(middle_kernel, dims, total), grid=(4,),...  57.4 us
    pallas_call x1, Pallas kernels, back(): pl.pallas_call(functools.partial(back_kernel, dims), grid=(4,), in_specs=...  50.4 us
    pallas_call x1, Pallas kernels, finish(): pl.pallas_call(functools.partial(finish_kernel, dims), in_specs=[held, aw...  45.9 us
    pallas_call x1, Pallas kernels, turn(): pl.pallas_call(functools.partial(turn_kernel, dims), grid=(8,), in_specs=...  43.3 us
    pallas_call x1, Pallas kernels, spread(): pl.pallas_call(functools.partial(spread_kernel, dims, cols), in_specs=[he...  9.83 us

profile of v2, /device:TPU:0, one launch (start us, length us, event | category | flops | bytes accessed | tf_op | source)
XLA Modules:
  0.0 272.2 jit_solution(4815487228615681666)
XLA Ops:
  1.3 63.2 %front.1 = (f32[16,768]{1,0:T(8,128)}, bf16[6,256,768]{2,1,0:T(8,128)(2,1)}, bf16[6,256,384]{2,1,0:T(8,128)(2,1)}, bf16[6,256,128]{2,1,0:T(8,128)(2,1)}, bf16[6,...) custom-call(s32[12]{0:T(128)} %lens.3, ...), custom_call_target="tpu_custom_call" | custom-call | flops 10871635968 | bytes 40000000 | tf_op jit(solution)/shard_map/front/pallas_call | solution.py:1243
  64.6 57.4 %middle.1 = (bf16[12,256,768]{2,1,0:T(8,128)(2,1)}, bf16[12,256,768]{2,1,0:T(8,128)(2,1)}, bf16[12,256,768]{2,1,0:T(8,128)(2,1)}, f32[3,256,768]{2,1,0:T(8,128)}...) custom-call(bf16[12,197,768]{2,1,0:T(8,128)(2,1)} %img.5, ...), custom_call_target="tpu_custom_call" | custom-call | flops 14495514624 | bytes 40000000 | tf_op jit(solution)/shard_map/middle/pallas_call | solution.py:1510
  122.0 43.3 %turn.1 = (bf16[4,2,96,768]{3,2,1,0:T(8,128)(2,1)}, bf16[4,2,96,768]{3,2,1,0:T(8,128)(2,1)}, bf16[4,2,96,768]{3,2,1,0:T(8,128)(2,1)}, f32[3,256,768]{2,1,0:T(8,1...) custom-call(bf16[12,197,768]{2,1,0:T(8,128)(2,1)} %img.5, ...), custom_call_target="tpu_custom_call" | custom-call | flops 7247757312 | bytes 40000000 | tf_op jit(solution)/shard_map/turn/pallas_call | solution.py:1675
  165.3 0.0 copy-start
  165.3 50.4 %back.1 = (bf16[3,256,768]{2,1,0:T(8,128)(2,1)}, bf16[3,256,768]{2,1,0:T(8,128)(2,1)}, bf16[768,512]{1,0:T(8,128)(2,1)}, bf16[768,256]{1,0:T(8,128)(2,1)}, f32[1...) custom-call(s32[12]{0:T(128)} %lens.3, ...), custom_call_target="tpu_custom_call" | custom-call | flops 16307453952 | bytes 30000000 | tf_op jit(solution)/shard_map/back/pallas_call | solution.py:1846
  215.7 0.0 copy-done
  215.7 0.5 fusion
  216.2 45.9 %finish.1 = (bf16[3,197,768]{2,1,0:T(8,128)(2,1)}, bf16[3,40,768]{2,1,0:T(8,128)(2,1)}, bf16[3,197,768]{2,1,0:T(8,128)(2,1)}, bf16[3,40,768]{2,1,0:T(8,128)(2,1)...) custom-call(bf16[3,256,768]{2,1,0:T(8,128)(2,1)} %get-tuple-element., ...), custom_call_target="tpu_custom_call" | custom-call | tf_op jit(solution)/shard_map/finish/pallas_call | solution.py:2053
  262.1 9.8 %spread.1 = (f32[1,96]{1,0:T(1,128)}, f32[1,96]{1,0:T(1,128)}, f32[1,96]{1,0:T(1,128)}, f32[1,96]{1,0:T(1,128)}, f32[2,96]{1,0:T(2,128)}, /*index=5*/f32[2,96]{1...) custom-call(f32[24,768]{1,0:T(8,128)} %get-tuple-element.148.sums, ...), custom_call_target="tpu_custom_call" | custom-call | flops 1000000 | bytes 20000000 | tf_op jit(solution)/shard_map/spread/pallas_call | solution.py:2152
Async XLA Ops:
  165.3 50.4 %copy-start = (f32[2,128]{1,0:T(2,128)S(1)}, f32[2,128]{1,0:T(2,128)}, u32[]{:S(2)}) copy-start(f32[2,128]{1,0:T(2,128)} %get-tuple-element.165) | copy-start | bytes 3076

commit v3 on v2

--- a/solution.py
+++ b/solution.py
@@ -1274,16 +1274,17 @@
     )(lens, img, txt, *vectors, bias, own_w, own_o)
 
 
-def middle_kernel(dims, total, img, txt, own, peer, cls_own, cls_peer, vec, up, up_bias, down, weight, scale,
+def middle_kernel(dims, total, img, txt, own, peer, cls_own, cls_peer, vec, up, up_bias, down, head_weight, scale,
                   act, dup, ddn, dexp, d_own, d_near, bias_grad, class_e, c_act, c_dup, c_ddn, dcls,
                   head_in, dproj, gains, shifts, scalars,
-                  bx, bd, rx, rd, x_near, x_far, ins, rows, part, parts, cls, back, cot, c_rows, extra, extras,
-                  send_sem, recv_sem):
+                  bx, bd, rx, rd, x_near, x_far, ins, rows, part, parts, cls, back, cot, c_rows, extra, extras, hidden_in, weight,
+                  local_sem, send_sem, recv_sem):
     here = Place()
     ip, slab, quarter = dims.ip, dims.slab, dims.quarter
     i = pl.program_id(0)
     model = own.shape[-1]
     mp_peers = [here.core, here.near, here.across]
+    fetch = pltpu.make_async_copy(head_weight, weight, local_sem.at[0])
     of = [here.quarter(0, 0), here.quarter(1, 0), here.quarter(0, 1), here.quarter(1, 1)]
 
     sent_x = [remote(bx.at[2 * j], rx.at[j], send_sem, recv_sem, j, here.core) for j in range(2)]
@@ -1295,17 +1296,19 @@
 
     @pl.when(i == 0)
     def _():
+        fetch.start()
         rows[...] = jnp.zeros_like(rows)
         bias_grad[...] = jnp.zeros_like(bias_grad)
         for m in range(2):
             e = jnp.concatenate([cls_own[2 + m], cls_peer[2 + m]], axis=0).astype(BF16)
             class_e[m] = e
             u = dot(e, up[m]) + up_bias[m:m + 1]
+            hidden_in[m] = u
             part[m] = dot(gelu_low(u), down[m])
         meet(mp_peers + here.batch)
         for copy in sent_part:
             copy.start()
-        ins[...] = peer[quarter:, :, :]
+        ins[...] = peer[...]
 
     @pl.when(i == 1)
     def _():
@@ -1323,15 +1326,16 @@
                     cls[here.b, m, pl.ds(4 * of[r] + p, 1), :] = x
         for copy in sent_cls:
             copy.start()
-        ins[...] = own[quarter:, :, :]
+        ins[...] = own[...]
 
     @pl.when(i == 2)
     def _():
-        ins[...] = peer[:quarter, :, :]
+        ins[...] = peer[...]
 
     @pl.when(i == 3)
     def _():
-        ins[...] = own[:quarter, :, :]
+        ins[...] = own[...]
+        fetch.wait()
         for copy in sent_cls:
             copy.wait_recv()
         n_rows = 16 * cls.shape[0]
@@ -1368,12 +1372,13 @@
         slope = jnp.sum(jnp.sum(dlogits * logits, axis=1, keepdims=True), axis=0, keepdims=True)
         scalars[0:1, :] = jnp.broadcast_to(lines * (1.0 / (2 * total)), (1, 128))
         scalars[1:2, :] = jnp.broadcast_to(slope, (1, 128))
-        high = lax.Precision.HIGHEST
-        wide = [e.astype(F32) for e in embed]
+        pieces, left = [], dlogits
+        for _ in range(3):
+            pieces.append(left.astype(BF16))
+            left = left - pieces[-1].astype(F32)
         dembed = [
-            sharp * jnp.dot(dlogits, wide[1], precision=high, preferred_element_type=F32),
-            sharp * lax.dot_general(dlogits, wide[0], (((0,), (0,)), ((), ())), precision=high,
-                                    preferred_element_type=F32),
+            sharp * (dot(pieces[0], embed[1]) + (dot(pieces[1], embed[1]) + dot(pieces[2], embed[1]))),
+            sharp * (t_dot(pieces[0], embed[0]) + (t_dot(pieces[1], embed[0]) + t_dot(pieces[2], embed[0]))),
         ]
         c_rows[...] = jnp.zeros_like(c_rows)
         dcls[...] = jnp.zeros_like(dcls)
@@ -1397,7 +1402,7 @@
                     c_rows[m, at:at + 1, :] = cot[m, 8 * step + p:8 * step + p + 1, :] + g
                     if r == 0:
                         dcls[p, m:m + 1, :] = g
-            u = dot(class_e[m], up[m]) + up_bias[m:m + 1]
+            u = hidden_in[m]
             big, small = gelu_parts(u)
             c_act[m] = (u * big).astype(BF16)
             g = (c_rows[m] * vector(vec, F_SCALE)).astype(BF16)
@@ -1500,6 +1505,7 @@
         return here.quarter(1 - i // 2, 1 - i % 2), 0, 0
 
     held = pl.BlockSpec(memory_space=pltpu.VMEM)
+    half = pl.BlockSpec((quarter, slab, model), lambda i: (jnp.where(i < 2, 1, 0), 0, 0))
     step = lambda cols: pl.BlockSpec((quarter, slab, cols), lambda i: (i, 0, 0))
     rows_of = lambda n, t: jax.ShapeDtypeStruct((n, slab, model), t)
     small = [((quarter, slab, model), F32), ((quarter, slab, model), F32), ((quarter, slab, model), BF16),
@@ -1511,7 +1517,8 @@
         functools.partial(middle_kernel, dims, total),
         grid=(4,),
         in_specs=[pl.BlockSpec((quarter, dims.patches, model), cot_at),
-                  pl.BlockSpec((quarter, dims.caption, model), cot_at)] + [held] * 10,
+                  pl.BlockSpec((quarter, dims.caption, model), cot_at)] + [half] * 2 + [held] * 6
+        + [pl.BlockSpec(memory_space=pl.ANY), held],
         out_specs=[step(hidden), step(hidden), step(model)] + [held] * len(small),
         out_shape=[rows_of(4 * quarter, BF16)] * 3 + [jax.ShapeDtypeStruct(v, t) for v, t in small],
         scratch_shapes=[
@@ -1523,6 +1530,7 @@
             pltpu.VMEM((batch, 2, 16, model), F32), pltpu.VMEM((2, 16 * batch, model), F32),
             pltpu.VMEM((2, 32, model), F32), pltpu.VMEM((2, 16, model), F32),
             pltpu.VMEM((2, 16, model), F32), pltpu.VMEM((3, 2, 16, model), F32),
+            pltpu.VMEM((2, 16, hidden), F32), pltpu.VMEM(weight.shape, BF16), pltpu.SemaphoreType.DMA((1,)),
             pltpu.SemaphoreType.DMA((18,)), pltpu.SemaphoreType.DMA((18,)),
         ],
         compiler_params=params(collective_id=2, has_side_effects=True),
@@ -1539,15 +1547,16 @@
     here = Place()
     quarter, ip = dims.quarter, dims.ip
     i = pl.program_id(0)
-    piece = side_send.shape[2]
+    piece = side_send.shape[3]
     sent_near = remote(d_near, d_far, send_sem, recv_sem, 0, here.near)
 
     def over(p):
         return remote(dattn.at[p], n_peer.at[p], send_sem, recv_sem, 1 + p, here.core)
 
     sent_core = [over(p) for p in range(quarter)]
-    sent_side = [remote(side_send.at[j], side_recv.at[j], send_sem, recv_sem, 1 + quarter + j, here.side)
-                 for j in range(4)]
+    sent_side = [remote(side_send.at[h], side_recv.at[h], send_sem, recv_sem, 1 + quarter + h, here.side)
+                 for h in range(2)]
+    part = acc.shape[2] // 2
     loaded = [pltpu.make_async_copy(src, dst, local_sem.at[j]) for j, (src, dst) in enumerate((
         (dexp, dexp_in), (attended, attended_in), (attn, attn_in), (d_own, d_own_in)))]
     dexp, attended, attn, d_own = dexp_in, attended_in, attn_in, d_own_in
@@ -1564,38 +1573,40 @@
         for m in range(2):
             acc[m] = t_dot(cd[m], ca[m])
 
-    @pl.when(i < 4)
-    def _():
-        for m, lo, hi in spans:
-            acc[m] += t_dot(flat(ddn[:, lo:hi, :]), flat(act[:, lo:hi, :]))
-
-    @pl.when(i == 3)
-    def _():
-        for j in range(4):
-            for m in range(2):
-                side_send[j, m] = acc[m, block(2 * j + 1 - here.x), :].astype(BF16)
-                down_sum[j, m] = acc[m, block(2 * j + here.x), :].astype(BF16)
-            sent_side[j].start()
-
-    @pl.when(i == 4)
+    for h in range(2):
+        @pl.when(i // 4 == h)
+        def _():
+            for m, lo, hi in spans:
+                acc[m, :, h * part:(h + 1) * part] += t_dot(flat(ddn[:, lo:hi, :]), flat(act[:, lo:hi, :]))
+
+        @pl.when(i == 4 * h + 3)
+        def _():
+            cols = slice(h * part, (h + 1) * part)
+            for j in range(4):
+                for m in range(2):
+                    side_send[h, j, m] = acc[m, block(2 * j + 1 - here.x), cols].astype(BF16)
+                    down_sum[j, m, :, cols] = acc[m, block(2 * j + here.x), cols].astype(BF16)
+            sent_side[h].start()
+
+    @pl.when(i == 8)
     def _():
         for m in range(2):
             acc[m] = t_dot(ce[m], cu[m])
 
-    @pl.when((i >= 4) & (i % 2 == 0))
+    @pl.when((i >= 8) & (i % 2 == 0))
     def _():
         e_in[...] = peer[...]
 
-    @pl.when((i >= 4) & (i % 2 == 1))
+    @pl.when((i >= 8) & (i % 2 == 1))
     def _():
         e_in[...] = own[...]
 
-    @pl.when(i >= 4)
+    @pl.when(i >= 8)
     def _():
         for m, lo, hi in spans:
             acc[m] += t_dot(flat(e_in[:, lo:hi, :]), flat(dup[:, lo:hi, :]))
 
-    @pl.when(i == 7)
+    @pl.when(i == 11)
     def _():
         for j in range(4):
             for m in range(2):
@@ -1649,9 +1660,12 @@
         for p in range(quarter):
             sent_core[p].wait()
             dattn_peer[p] = n_peer[p]
-        for j in range(4):
-            sent_side[j].wait()
-            down_sum[j] = (down_sum[j].astype(F32) + side_recv[j].astype(F32)).astype(BF16)
+        for h in range(2):
+            sent_side[h].wait()
+            cols = slice(h * part, (h + 1) * part)
+            for j in range(4):
+                down_sum[j, :, :, cols] = (
+                    down_sum[j, :, :, cols].astype(F32) + side_recv[h, j].astype(F32)).astype(BF16)
         sent_near.wait_send()
 
 
@@ -1665,28 +1679,31 @@
         return Place().quarter(0, 0), 0, 0
 
     away = pl.BlockSpec(memory_space=pl.ANY)
-    half = pl.BlockSpec((quarter, slab, model), lambda i: (jnp.where(i < 6, 1, 0), 0, 0))
-    first = pl.BlockSpec((quarter, slab, hidden), lambda i: (jnp.minimum(i, 3), 0, 0))
-    last = pl.BlockSpec((quarter, slab, hidden), lambda i: (jnp.maximum(i - 4, 0), 0, 0))
+    half = pl.BlockSpec((quarter, slab, model), lambda i: (jnp.where(i < 10, 1, 0), 0, 0))
+    row = lambda i: jnp.where(i < 8, i % 4, 3)
+    first = pl.BlockSpec((quarter, slab, model), lambda i: (row(i), 0, 0))
+    piece = pl.BlockSpec((quarter, slab, hidden // 2), lambda i: (row(i), 0, jnp.minimum(i // 4, 1)))
+    last = pl.BlockSpec((quarter, slab, hidden), lambda i: (jnp.maximum(i - 8, 0), 0, 0))
     block = (quarter, slab, model)
     part = (4, 2, model // 8, hidden)
+    split = (2, 4, 2, model // 8, hidden // 2)
     outs = [(part, BF16), (part, BF16), (part, BF16), (block, F32), (block, BF16), (block, BF16),
             ((quarter, dims.patches, model), BF16), ((quarter, dims.caption, model), BF16), ((16, model), F32)]
     return pl.pallas_call(
         functools.partial(turn_kernel, dims),
-        grid=(8,),
+        grid=(12,),
         in_specs=[pl.BlockSpec((quarter, dims.patches, model), own_at),
-                  pl.BlockSpec((quarter, dims.caption, model), own_at)] + [half] * 2 + [first, last, first]
+                  pl.BlockSpec((quarter, dims.caption, model), own_at)] + [half] * 2 + [piece, last, first]
         + [held] * 4 + [away] * 4 + [held] * 3,
         out_specs=[held] * len(outs),
         out_shape=[jax.ShapeDtypeStruct(v, t) for v, t in outs],
         scratch_shapes=[
             pltpu.VMEM((2, model, hidden), F32), pltpu.VMEM(block, BF16), pltpu.VMEM(block, BF16),
-            pltpu.VMEM((slab, model), F32), pltpu.VMEM(part, BF16), pltpu.VMEM(part, BF16),
+            pltpu.VMEM((slab, model), F32), pltpu.VMEM(split, BF16), pltpu.VMEM(split, BF16),
             pltpu.VMEM(block, BF16),
         ] + [pltpu.VMEM(block, F32)] * 4 + [
             pltpu.SemaphoreType.DMA((4,)),
-            pltpu.SemaphoreType.DMA((5 + quarter,)), pltpu.SemaphoreType.DMA((5 + quarter,)),
+            pltpu.SemaphoreType.DMA((3 + quarter,)), pltpu.SemaphoreType.DMA((3 + quarter,)),
         ],
         compiler_params=params(collective_id=3, has_side_effects=True),
         cost_estimate=pl.CostEstimate(
@@ -1697,10 +1714,10 @@
 
 def back_kernel(dims, lens, d_own, d_peer, normed, qkv_far, mixed_far, qkv_own, mixed_own, wq, wo, wf,
                 fin_img, fin_txt, up_keep, up_send, down_sum,
-                keep, send, grad_pair, grad_single, cols_far, cols_own, near_img, near_txt, far_sum, up_one, down_out, up_out,
+                whole, grad_pair, grad_single, cols_far, cols_own, near_img, near_txt, far_sum, up_one, down_out, up_out,
                 dattn, dm_far, dm_own, dq_far, dq_own, acc_far, acc_own, w_far, w_own, o_far, o_own, dn, grad_f,
                 up_mine, up_side, up_low, up_in, up_pass, up_last, down_mine, down_in, down_pass, down_last,
-                from_side, local_sem, send_sem, recv_sem):
+                n_send, n_recv, from_side, local_sem, send_sem, recv_sem):
     here = Place()
     i = pl.program_id(0)
     slab, quarter, local = dims.slab, dims.quarter, dims.local
@@ -1724,6 +1741,7 @@
     sent_far = [make(grad_f.at[block(2 * j + 1 - here.x)], from_side.at[j], here.side) for j in range(4)]
     sent_low = in_pair(up_low, up_in)
     pass_low = make(up_pass, up_last, here.opposite)
+    sent_n = make(n_send, n_recv, here.core)
     loaded = [pltpu.make_async_copy(up_keep, up_mine, local_sem.at[0]),
               pltpu.make_async_copy(down_sum.at[here.z], down_mine.at[0], local_sem.at[1]),
               pltpu.make_async_copy(down_sum.at[here.z_far], down_mine.at[1], local_sem.at[2])]
@@ -1731,7 +1749,7 @@
 
     @pl.when(i == 0)
     def _():
-        meet([here.near, here.side, here.paired, here.opposite])
+        meet([here.core, here.near, here.side, here.paired, here.opposite])
         for copy in loaded + sent_near + sent_up + sent_down:
             copy.start()
         for acc, cols in ((acc_far, cols_far), (acc_own, cols_own)):
@@ -1748,13 +1766,13 @@
 
     @pl.when(i % 2 == 0)
     def _():
+        dattn[...] = d_peer[...]
+
+    @pl.when(i % 2 == 1)
+    def _():
         dattn[...] = d_own[...]
 
-    @pl.when(i % 2 == 1)
-    def _():
-        dattn[...] = d_peer[...]
-
-    whose = here.quarter(0, i % 2)
+    whose = here.quarter(0, 1 - i % 2)
 
     @pl.when(i < 2)
     def _():
@@ -1792,11 +1810,12 @@
     def _():
         part = back_step(dims, 1, lens, whose, dattn, normed, qkv_own, mixed_own, dm_own, dq_own, acc_own, cols_own,
                          w_own, o_own)
-        total = (part.reshape(quarter, slab, model) + dn[i - 2]).astype(BF16)
+        total = part.reshape(quarter, slab, model) + dn[i - 2]
 
         @pl.when(i == 2)
         def _():
-            keep[...] = total
+            n_send[...] = total.astype(BF16)
+            sent_n.start()
             for copy in sent_low:
                 copy.wait_recv()
             up_pass[...] = add(up_low[here.z_far], up_in[1]).astype(BF16)
@@ -1804,11 +1823,13 @@
 
         @pl.when(i == 3)
         def _():
-            send[...] = total
+            whole[...] = total
 
     @pl.when(i == 3)
     def _():
         grad_pair[...] = acc_own[...].astype(BF16)
+        sent_n.wait_recv()
+        whole[...] += n_recv[...].astype(F32)
         down_out[...] = add(down_mine[0], down_in[0])
         for j in range(4):
             sent_far[j].wait_recv()
@@ -1822,7 +1843,7 @@
         up_out[...] = add(up_low[here.z], up_in[0], up_last[...])
         for copy in sent_near:
             copy.wait_recv()
-        for copy in sent_near + sent_up + sent_down + sent_far + sent_low + [pass_down, pass_low]:
+        for copy in sent_near + sent_up + sent_down + sent_far + sent_low + [pass_down, pass_low, sent_n]:
             copy.wait_send()
 
 
@@ -1835,9 +1856,9 @@
     held = pl.BlockSpec(memory_space=pltpu.VMEM)
     away = pl.BlockSpec(memory_space=pl.ANY)
     spec = lambda cols, at: pl.BlockSpec((quarter, slab, cols), lambda i: (at(i), 0, 0))
-    early, late = lambda i: jnp.minimum(i, 1), lambda i: jnp.maximum(i - 2, 0)
+    early, late = lambda i: jnp.maximum(1 - i, 0), lambda i: jnp.where(i < 3, 1, 0)
     rows = (quarter, slab, model)
-    outs = [(held, rows, BF16), (held, rows, BF16), (held, (model, 512), BF16), (held, (model, 256), BF16),
+    outs = [(held, rows, F32), (held, (model, 512), BF16), (held, (model, 256), BF16),
             (held, (1, 768), F32), (held, (1, 384), F32),
             (away, fin_img.shape, BF16), (away, fin_txt.shape, BF16),
             (held, (4, piece, model), BF16), (held, (4, piece, hidden), BF16),
@@ -1846,7 +1867,7 @@
     return pl.pallas_call(
         functools.partial(back_kernel, dims),
         grid=(4,),
-        in_specs=[pl.BlockSpec(memory_space=pltpu.SMEM), held, held, spec(model, lambda i: i % 2),
+        in_specs=[pl.BlockSpec(memory_space=pltpu.SMEM), held, held, spec(model, lambda i: 1 - i % 2),
                   spec(768, early), spec(256, early), spec(384, late), spec(128, late), held, held, held]
         + [away] * 5,
         out_specs=[v[0] for v in outs],
@@ -1862,8 +1883,8 @@
             pltpu.VMEM((piece, hidden), BF16), pltpu.VMEM((piece, hidden), BF16),
             pltpu.VMEM((2, 2, piece, hidden), BF16), pltpu.VMEM((2, 2, piece, hidden), BF16),
             pltpu.VMEM((2, piece, hidden), BF16), pltpu.VMEM((2, piece, hidden), BF16),
-            pltpu.VMEM((4, piece, model), BF16),
-            pltpu.SemaphoreType.DMA((3,)), pltpu.SemaphoreType.DMA((20,)), pltpu.SemaphoreType.DMA((20,)),
+            pltpu.VMEM(rows, BF16), pltpu.VMEM(rows, BF16), pltpu.VMEM((4, piece, model), BF16),
+            pltpu.SemaphoreType.DMA((3,)), pltpu.SemaphoreType.DMA((21,)), pltpu.SemaphoreType.DMA((21,)),
         ],
         compiler_params=params(collective_id=4, has_side_effects=True),
         cost_estimate=pl.CostEstimate(
@@ -1876,10 +1897,10 @@
 V_ROWS, V_MP, V_HEADS, V_FAR = 24, 11, 13, 15
 
 
-def finish_kernel(dims, n_keep, n_send, dattended, states_img, states_txt, vec, fin_img, fin_txt,
+def finish_kernel(dims, dnormed, dattended, states_img, states_txt, vec, fin_img, fin_txt,
                   near_img, near_txt, grad_pair, grad_single, grad_far, up_one, own_sums, up_sums, cols_own, cols_far,
                   core_img, core_txt, across_img, across_txt, back_img, back_txt, grad_out, v_out, up_out,
-                  n_recv, s_img, s_txt, d_img, d_txt, rows, xr, zs, z_in, z_pass, z_last, f_in, f_pass, f_last, u_in, u_pass, u_last, far_sum, far_recv, vs, vr,
+                  s_img, s_txt, d_img, d_txt, rows, xr, zs, z_in, z_pass, z_last, f_in, f_pass, f_last, u_in, u_pass, u_last, far_sum, far_recv, vs, vr,
                   local_sem, send_sem, recv_sem):
     quarter = dims.quarter
     here = Place()
@@ -1898,9 +1919,6 @@
         copy.start()
     meet([here.core, here.near, here.side, here.paired, here.opposite])
 
-    n_copies = [send(n_send.at[p], n_recv.at[p], here.core) for p in range(quarter)]
-    for copy in n_copies:
-        copy.start()
     piece = xr.shape[1]
     wide = grad_pair.shape[1]
     spans = ((grad_pair, 0, wide), (grad_single, wide, xr.shape[2]))
@@ -1929,8 +1947,7 @@
     for p in range(quarter):
         load_rows(dims, p, s_img, s_txt, rows)
         n, r = normalise(rows[...])
-        n_copies[p].wait_recv()
-        dy = n_keep[p].astype(F32) + n_recv[p].astype(F32)
+        dy = dnormed[p]
         total[0] = total[0] + jnp.sum(dy * n, axis=0, keepdims=True)
         total[1] = total[1] + jnp.sum(dy, axis=0, keepdims=True)
         d = dattended[p] + norm_back(n, r, dy * vector(vec, GAIN1))
@@ -2037,11 +2054,11 @@
     v_out[V_HEADS:V_HEADS + 2, :] = v[V_HEADS:V_HEADS + 2, :] + there[V_FAR:V_FAR + 2, :]
     for copy in to_other + fin_remote + onward:
         copy.wait()
-    for copy in n_copies + x_copies + far_copies + to_near + z_copies + v_copies + up_copies + [far_copy, v_near, v_far]:
+    for copy in x_copies + far_copies + to_near + z_copies + v_copies + up_copies + [far_copy, v_near, v_far]:
         copy.wait_send()
 
 
-def finish(dims, n_keep, n_send, dattended, states_img, states_txt, vec, fin_img, fin_txt,
+def finish(dims, dnormed, dattended, states_img, states_txt, vec, fin_img, fin_txt,
            near_img, near_txt, grad_pair, grad_single, grad_far, up_one, *tables):
     pairs, patches, model = states_img.shape
     caption = states_txt.shape[1]
@@ -2052,7 +2069,7 @@
     n_remote = 7 * quarter + 28
     return pl.pallas_call(
         functools.partial(finish_kernel, dims),
-        in_specs=[held, away, held] + [away] * 2 + [held] + [away] * 4 + [held] * 8,
+        in_specs=[held, held] + [away] * 2 + [held] + [away] * 4 + [held] * 8,
         out_specs=[away] * 6 + [held] * 3,
         out_shape=[jax.ShapeDtypeStruct(v.shape, BF16) for v in (fin_img, fin_txt) * 2] + [
             jax.ShapeDtypeStruct((pairs, patches, model), BF16),
@@ -2062,7 +2079,6 @@
             jax.ShapeDtypeStruct(up_one.shape[1:], F32),
         ],
         scratch_shapes=[
-            pltpu.VMEM((quarter, slab, model), BF16),
             pltpu.VMEM((quarter, patches, model), BF16),
             pltpu.VMEM((quarter, caption, model), BF16),
             pltpu.VMEM((quarter, patches, model), BF16),
@@ -2080,7 +2096,7 @@
         ],
         compiler_params=params(collective_id=1, has_side_effects=True),
         name="finish",
-    )(n_keep, n_send, dattended, states_img, states_txt, vec, fin_img, fin_txt,
+    )(dnormed, dattended, states_img, states_txt, vec, fin_img, fin_txt,
       near_img, near_txt, grad_pair, grad_single, grad_far, up_one, *tables)
 
 
@@ -2257,7 +2273,7 @@
     contrast_loss = scalars[0, :1]
     grad_logit_scale = scalars[1, :1]
     if one_kernel:
-        (n_keep, n_send, grad_o01, grad_o2, cols_far, cols_own, near_img, near_txt, far_sum, up_one, grad_down,
+        (dnormed, grad_o01, grad_o2, cols_far, cols_own, near_img, near_txt, far_sum, up_one, grad_down,
          up_low) = back(
             dims, caption_lengths, dattn, dattn_peer, normed, qkv_far, mixed_far, qkv_own, mixed_own,
             own_w, output_weight, wf, fin_img, fin_txt, up_keep, up_send, down_sum)
@@ -2272,7 +2288,7 @@
     pair, single = 2 * HEAD_DIM, HEAD_DIM
     if one_kernel:
         core_img, core_txt, across_img, across_txt, back_img, back_txt, attn_grad, sums, up_high = finish(
-            dims, n_keep, n_send, dattended, image_states, text_states, vec, fin_img, fin_txt,
+            dims, dnormed, dattended, image_states, text_states, vec, fin_img, fin_txt,
             near_img, near_txt, grad_o01, grad_o2, far_sum, up_one, own_sums, up_sums, cols_own, cols_far)
         forward = (fin_img, fin_txt, near_img, near_txt, core_img, core_txt, across_img, across_txt)
         (*vectors, grad_qkv, grad_output_weight, grad_up, grad_down, grad_head_weight,

time: 272 us -> 271 us (level)
  no operation moved by 1% of the time
where the time goes in v3:
time: 271 us
  Pallas kernels  269 us (99%)
    pallas_call x1, Pallas kernels, front(): pl.pallas_call(lambda lens, img, txt, *refs: front_kernel(dims, lens, img...  63.2 us
    pallas_call x1, Pallas kernels, middle(): pl.pallas_call(functools.partial(middle_kernel, dims, total), grid=(4,),...  56.2 us
    pallas_call x1, Pallas kernels, back(): pl.pallas_call(functools.partial(back_kernel, dims), grid=(4,), in_specs=...  50.7 us
    pallas_call x1, Pallas kernels, finish(): pl.pallas_call(functools.partial(finish_kernel, dims), in_specs=[held, he...  46.7 us
    pallas_call x1, Pallas kernels, turn(): pl.pallas_call(functools.partial(turn_kernel, dims), grid=(12,), in_specs...  42.3 us
    pallas_call x1, Pallas kernels, spread(): pl.pallas_call(functools.partial(spread_kernel, dims, cols), in_specs=[he...  9.83 us

profile of v3, /device:TPU:0, one launch (start us, length us, event | category | flops | bytes accessed | tf_op | source)
XLA Modules:
  0.0 271.0 jit_solution(1095403793131466746)
XLA Ops:
  1.3 63.2 %front.1 = (f32[16,768]{1,0:T(8,128)}, bf16[6,256,768]{2,1,0:T(8,128)(2,1)}, bf16[6,256,384]{2,1,0:T(8,128)(2,1)}, bf16[6,256,128]{2,1,0:T(8,128)(2,1)}, bf16[6,...) custom-call(s32[12]{0:T(128)} %lens.3, ...), custom_call_target="tpu_custom_call" | custom-call | flops 10871635968 | bytes 40000000 | tf_op jit(solution)/shard_map/front/pallas_call | solution.py:1243
  64.6 56.2 %middle.1 = (bf16[12,256,768]{2,1,0:T(8,128)(2,1)}, bf16[12,256,768]{2,1,0:T(8,128)(2,1)}, bf16[12,256,768]{2,1,0:T(8,128)(2,1)}, f32[3,256,768]{2,1,0:T(8,128)}...) custom-call(bf16[12,197,768]{2,1,0:T(8,128)(2,1)} %img.5, ...), custom_call_target="tpu_custom_call" | custom-call | flops 14495514624 | bytes 40000000 | tf_op jit(solution)/shard_map/middle/pallas_call | solution.py:1516
  120.7 42.3 %turn.1 = (bf16[4,2,96,768]{3,2,1,0:T(8,128)(2,1)}, bf16[4,2,96,768]{3,2,1,0:T(8,128)(2,1)}, bf16[4,2,96,768]{3,2,1,0:T(8,128)(2,1)}, f32[3,256,768]{2,1,0:T(8,1...) custom-call(bf16[12,197,768]{2,1,0:T(8,128)(2,1)} %img.5, ...), custom_call_target="tpu_custom_call" | custom-call | flops 7247757312 | bytes 40000000 | tf_op jit(solution)/shard_map/turn/pallas_call | solution.py:1692
  163.0 0.0 copy-start
  163.0 50.7 %back.1 = (f32[3,256,768]{2,1,0:T(8,128)}, bf16[768,512]{1,0:T(8,128)(2,1)}, bf16[768,256]{1,0:T(8,128)(2,1)}, f32[1,768]{1,0:T(1,128)}, f32[1,384]{1,0:T(1,128)...) custom-call(s32[12]{0:T(128)} %lens.3, ...), custom_call_target="tpu_custom_call" | custom-call | flops 16307453952 | bytes 30000000 | tf_op jit(solution)/shard_map/back/pallas_call | solution.py:1867
  213.7 0.0 copy-done
  213.7 0.5 fusion
  214.2 46.7 %finish.1 = (bf16[3,197,768]{2,1,0:T(8,128)(2,1)}, bf16[3,40,768]{2,1,0:T(8,128)(2,1)}, bf16[3,197,768]{2,1,0:T(8,128)(2,1)}, bf16[3,40,768]{2,1,0:T(8,128)(2,1)...) custom-call(f32[3,256,768]{2,1,0:T(8,128)} %get-tuple-element.134.dn, ...), custom_call_target="tpu_custom_call" | custom-call | tf_op jit(solution)/shard_map/finish/pallas_call | solution.py:2070
  260.9 9.8 %spread.1 = (f32[1,96]{1,0:T(1,128)}, f32[1,96]{1,0:T(1,128)}, f32[1,96]{1,0:T(1,128)}, f32[1,96]{1,0:T(1,128)}, f32[2,96]{1,0:T(2,128)}, /*index=5*/f32[2,96]{1...) custom-call(f32[24,768]{1,0:T(8,128)} %get-tuple-element.146.sums, ...), custom_call_target="tpu_custom_call" | custom-call | flops 1000000 | bytes 20000000 | tf_op jit(solution)/shard_map/spread/pallas_call | solution.py:2168
Async XLA Ops:
  163.0 50.7 %copy-start = (f32[2,128]{1,0:T(2,128)S(1)}, f32[2,128]{1,0:T(2,128)}, u32[]{:S(2)}) copy-start(f32[2,128]{1,0:T(2,128)} %get-tuple-element.163) | copy-start | bytes 3076

commit v4 on v3

--- a/solution.py
+++ b/solution.py
@@ -1714,9 +1714,9 @@
 
 def back_kernel(dims, lens, d_own, d_peer, normed, qkv_far, mixed_far, qkv_own, mixed_own, wq, wo, wf,
                 fin_img, fin_txt, up_keep, up_send, down_sum,
-                whole, grad_pair, grad_single, cols_far, cols_own, near_img, near_txt, far_sum, up_one, down_out, up_out,
+                whole, grad_pair, grad_single, cols_far, cols_own, near_img, near_txt, far_sum, down_out, up_out,
                 dattn, dm_far, dm_own, dq_far, dq_own, acc_far, acc_own, w_far, w_own, o_far, o_own, dn, grad_f,
-                up_mine, up_side, up_low, up_in, up_pass, up_last, down_mine, down_in, down_pass, down_last,
+                up_mine, up_side, up_sum, up_in, up_pass, up_last, down_mine, down_in, down_pass, down_last,
                 n_send, n_recv, from_side, local_sem, send_sem, recv_sem):
     here = Place()
     i = pl.program_id(0)
@@ -1738,9 +1738,12 @@
     in_pair = lambda src, dst: [make(src.at[here.z_pair], dst.at[0], here.paired), make(src.at[here.z_rest], dst.at[1], here.paired)]
     sent_down = in_pair(down_sum, down_in)
     pass_down = make(down_pass, down_last, here.opposite)
-    sent_far = [make(grad_f.at[block(2 * j + 1 - here.x)], from_side.at[j], here.side) for j in range(4)]
-    sent_low = in_pair(up_low, up_in)
-    pass_low = make(up_pass, up_last, here.opposite)
+    wide = grad_f.shape[1]
+    sent_far = [make(grad_f.at[block(2 * j + 1 - here.x)], from_side.at[j, :, pl.ds(0, wide)], here.side) for j in range(4)]
+    sent_far += [make(grad_single.at[block(2 * j + 1 - here.x)], from_side.at[j, :, pl.ds(wide, grad_single.shape[1])],
+                      here.side) for j in range(4)]
+    sent_pair = [in_pair(up_sum.at[m], up_in.at[m]) for m in range(2)]
+    pass_up = [make(up_pass.at[m], up_last.at[m], here.opposite) for m in range(2)]
     sent_n = make(n_send, n_recv, here.core)
     loaded = [pltpu.make_async_copy(up_keep, up_mine, local_sem.at[0]),
               pltpu.make_async_copy(down_sum.at[here.z], down_mine.at[0], local_sem.at[1]),
@@ -1780,6 +1783,19 @@
                          w_far, o_far)
         dn[i] = part.reshape(quarter, slab, model)
 
+    def sum_up(m):
+        for j in range(4):
+            sent_up[4 * m + j].wait_recv()
+            up_sum[m, j] = add(up_mine[j, m], up_side[m, j]).astype(BF16)
+        for copy in sent_pair[m]:
+            copy.start()
+
+    def pass_on(m):
+        for copy in sent_pair[m]:
+            copy.wait_recv()
+        up_pass[m] = add(up_sum[m, here.z_far], up_in[m, 1]).astype(BF16)
+        pass_up[m].start()
+
     @pl.when(i == 0)
     def _():
         for copy in loaded[1:]:
@@ -1788,6 +1804,8 @@
             copy.wait_recv()
         down_pass[...] = add(down_mine[1], down_in[1]).astype(BF16)
         pass_down.start()
+        loaded[0].wait()
+        sum_up(0)
 
     @pl.when(i == 1)
     def _():
@@ -1799,12 +1817,8 @@
             grad_single[:, t * one_head:(t + 1) * one_head] = acc_far[:, at + two:at + two + one_head].astype(BF16)
         for copy in sent_far:
             copy.start()
-        loaded[0].wait()
-        for j in range(4):
-            sent_up[j].wait_recv()
-            up_low[j] = add(up_mine[j, 0], up_side[0, j]).astype(BF16)
-        for copy in sent_low:
-            copy.start()
+        pass_on(0)
+        sum_up(1)
 
     @pl.when(i >= 2)
     def _():
@@ -1816,10 +1830,7 @@
         def _():
             n_send[...] = total.astype(BF16)
             sent_n.start()
-            for copy in sent_low:
-                copy.wait_recv()
-            up_pass[...] = add(up_low[here.z_far], up_in[1]).astype(BF16)
-            pass_low.start()
+            pass_on(1)
 
         @pl.when(i == 3)
         def _():
@@ -1831,19 +1842,19 @@
         sent_n.wait_recv()
         whole[...] += n_recv[...].astype(F32)
         down_out[...] = add(down_mine[0], down_in[0])
+        for copy in sent_far:
+            copy.wait_recv()
         for j in range(4):
-            sent_far[j].wait_recv()
-            far_sum[j] = add(grad_f[block(2 * j + here.x), :], from_side[j]).astype(BF16)
+            far_sum[j, :, 0:wide] = add(grad_f[block(2 * j + here.x), :], from_side[j, :, 0:wide]).astype(BF16)
+            far_sum[j, :, wide:] = add(grad_single[block(2 * j + here.x), :], from_side[j, :, wide:]).astype(BF16)
         pass_down.wait_recv()
         down_out[...] += down_last[...].astype(F32)
-        for j in range(4):
-            sent_up[4 + j].wait_recv()
-            up_one[j] = add(up_mine[j, 1], up_side[1, j]).astype(BF16)
-        pass_low.wait_recv()
-        up_out[...] = add(up_low[here.z], up_in[0], up_last[...])
+        for m in range(2):
+            pass_up[m].wait_recv()
+            up_out[m] = add(up_sum[m, here.z], up_in[m, 0], up_last[m])
         for copy in sent_near:
             copy.wait_recv()
-        for copy in sent_near + sent_up + sent_down + sent_far + sent_low + [pass_down, pass_low, sent_n]:
+        for copy in sent_near + sent_up + sent_down + sent_far + sent_pair[0] + sent_pair[1] + pass_up + [pass_down, sent_n]:
             copy.wait_send()
 
 
@@ -1861,8 +1872,7 @@
     outs = [(held, rows, F32), (held, (model, 512), BF16), (held, (model, 256), BF16),
             (held, (1, 768), F32), (held, (1, 384), F32),
             (away, fin_img.shape, BF16), (away, fin_txt.shape, BF16),
-            (held, (4, piece, model), BF16), (held, (4, piece, hidden), BF16),
-            (held, (2, piece, hidden), F32), (held, (piece, hidden), F32)]
+            (held, (4, piece, model + 256), BF16), (held, (2, piece, hidden), F32), (held, (2, piece, hidden), F32)]
     slabs = lambda cols: pltpu.VMEM((quarter, slab, cols), BF16)
     return pl.pallas_call(
         functools.partial(back_kernel, dims),
@@ -1879,12 +1889,12 @@
             pltpu.VMEM((256, model), BF16), pltpu.VMEM((128, model), BF16),
             pltpu.VMEM((2,) + rows, F32), pltpu.VMEM((model, model), BF16),
             pltpu.VMEM((4, 2, piece, hidden), BF16), pltpu.VMEM((2, 4, piece, hidden), BF16),
-            pltpu.VMEM((4, piece, hidden), BF16), pltpu.VMEM((2, piece, hidden), BF16),
-            pltpu.VMEM((piece, hidden), BF16), pltpu.VMEM((piece, hidden), BF16),
+            pltpu.VMEM((2, 4, piece, hidden), BF16), pltpu.VMEM((2, 2, piece, hidden), BF16),
+            pltpu.VMEM((2, piece, hidden), BF16), pltpu.VMEM((2, piece, hidden), BF16),
             pltpu.VMEM((2, 2, piece, hidden), BF16), pltpu.VMEM((2, 2, piece, hidden), BF16),
             pltpu.VMEM((2, piece, hidden), BF16), pltpu.VMEM((2, piece, hidden), BF16),
-            pltpu.VMEM(rows, BF16), pltpu.VMEM(rows, BF16), pltpu.VMEM((4, piece, model), BF16),
-            pltpu.SemaphoreType.DMA((3,)), pltpu.SemaphoreType.DMA((21,)), pltpu.SemaphoreType.DMA((21,)),
+            pltpu.VMEM(rows, BF16), pltpu.VMEM(rows, BF16), pltpu.VMEM((4, piece, model + 256), BF16),
+            pltpu.SemaphoreType.DMA((3,)), pltpu.SemaphoreType.DMA((28,)), pltpu.SemaphoreType.DMA((28,)),
         ],
         compiler_params=params(collective_id=4, has_side_effects=True),
         cost_estimate=pl.CostEstimate(
@@ -1894,13 +1904,13 @@
       fin_img, fin_txt, up_keep, up_send, down_sum)
 
 
-V_ROWS, V_MP, V_HEADS, V_FAR = 24, 11, 13, 15
+V_ROWS, V_MP, V_HEADS, V_FAR = 16, 11, 13, 256
 
 
 def finish_kernel(dims, dnormed, dattended, states_img, states_txt, vec, fin_img, fin_txt,
-                  near_img, near_txt, grad_pair, grad_single, grad_far, up_one, own_sums, up_sums, cols_own, cols_far,
-                  core_img, core_txt, across_img, across_txt, back_img, back_txt, grad_out, v_out, up_out,
-                  s_img, s_txt, d_img, d_txt, rows, xr, zs, z_in, z_pass, z_last, f_in, f_pass, f_last, u_in, u_pass, u_last, far_sum, far_recv, vs, vr,
+                  near_img, near_txt, grad_pair, grad_far, own_sums, up_sums, cols_own, cols_far,
+                  core_img, core_txt, across_img, across_txt, back_img, back_txt, grad_out, v_out,
+                  s_img, s_txt, d_img, d_txt, rows, xr, zs, z_in, z_pass, z_last, f_in, f_pass, f_last, far_sum, far_recv, vs, vr,
                   local_sem, send_sem, recv_sem):
     quarter = dims.quarter
     here = Place()
@@ -1921,19 +1931,16 @@
 
     piece = xr.shape[1]
     wide = grad_pair.shape[1]
-    spans = ((grad_pair, 0, wide), (grad_single, wide, xr.shape[2]))
     block = lambda j: pl.ds(pl.multiple_of(j * piece, piece), piece)
     x_copies = []
     for j in range(4):
-        for src, lo, hi in spans:
-            x_copies.append(send(src.at[block(2 * j + 1 - x)], xr.at[j, :, pl.ds(lo, hi - lo)], here.side))
-            x_copies[-1].start()
+        x_copies.append(send(grad_pair.at[block(2 * j + 1 - x)], xr.at[j], here.side))
+        x_copies[-1].start()
     add = lambda *parts: functools.reduce(lambda p, q: p + q, [v.astype(F32) for v in parts])
     in_pair = lambda src, dst: [send(src.at[here.z_pair], dst.at[0], here.paired),
                                 send(src.at[here.z_rest], dst.at[1], here.paired)]
     far_copies = in_pair(grad_far, f_in)
-    up_copies = in_pair(up_one, u_in)
-    for copy in far_copies + up_copies:
+    for copy in far_copies:
         copy.start()
 
     fin_remote = [send(src, dst, here.core) for src, dst in (
@@ -1975,8 +1982,8 @@
         own_at, far_at = 2 * j * two, 4 * j * two
         vs[0, V_HEADS + j:V_HEADS + j + 1, 0:two] = cols_own[0:1, own_at:own_at + two]
         vs[0, V_HEADS + j:V_HEADS + j + 1, two:two + one_head] = cols_far[0:1, far_at + two:far_at + two + one_head]
-        vs[0, V_FAR + j:V_FAR + j + 1, 0:two] = cols_far[0:1, far_at:far_at + two]
-        vs[0, V_FAR + j:V_FAR + j + 1, two:two + one_head] = cols_far[0:1, far_at + two + one_head:far_at + 2 * two]
+        vs[0, V_HEADS + j:V_HEADS + j + 1, V_FAR:V_FAR + two] = cols_far[0:1, far_at:far_at + two]
+        vs[0, V_HEADS + j:V_HEADS + j + 1, V_FAR + two:V_FAR + two + one_head] = cols_far[0:1, far_at + two + one_head:far_at + 2 * two]
     v = vs[0]
     v_copies = []
 
@@ -1995,37 +2002,29 @@
     far_copies.append(send(f_pass, f_last, here.opposite))
     far_copies[-1].start()
     v = v + exchange(1, v, here.side)
-    for copy in up_copies:
-        copy.wait_recv()
-    u_pass[...] = add(up_one[here.z_far], u_in[1]).astype(BF16)
     v = v + exchange(2, v, here.paired)
     vs[3] = v
     v_far = send(vs.at[3], vr.at[3], here.opposite)
     v_far.start()
-    up_copies.append(send(u_pass, u_last, here.opposite))
-    up_copies[-1].start()
-
-    def own_sum(j, k):
-        src, lo, hi = spans[k]
-        return src[block(2 * j + x), :].astype(F32) + xr[j, :, lo:hi].astype(F32)
+
+    def own_sum(j):
+        return add(grad_pair[block(2 * j + x), :], xr[j])
 
     for copy in x_copies:
         copy.wait_recv()
     for j in range(4):
-        for k, (src, lo, hi) in enumerate(spans):
-            zs[j, :, lo:hi] = own_sum(j, k).astype(BF16)
+        zs[j] = own_sum(j).astype(BF16)
     z_copies = in_pair(zs, z_in)
     for copy in z_copies:
         copy.start()
 
     far_copies[-1].wait_recv()
-    far_sum[...] = add(grad_far[z], f_in[0], f_last[...]).astype(BF16)
+    narrow = far_sum.shape[1]
+    far_sum[...] = add(grad_far[z, :, 0:narrow], f_in[0, :, 0:narrow], f_last[:, 0:narrow]).astype(BF16)
     far_copy = send(far_sum, far_recv, here.near)
     far_copy.start()
     v_far.wait_recv()
     v = v + vr[3]
-    up_copies[-1].wait_recv()
-    up_out[...] = add(up_one[z], u_in[0], u_last[...])
     for copy in z_copies:
         copy.wait_recv()
     z_pass[...] = add(zs[here.z_far], z_in[1]).astype(BF16)
@@ -2045,38 +2044,39 @@
             onward[-1].start()
     far_copy.wait_recv()
     z_copies[-1].wait_recv()
-    for k, (src, lo, hi) in enumerate(spans):
-        grad_out[:, lo:hi] = own_sum(z, k) + add(
-            far_recv[:, lo:hi], z_in[0, :, lo:hi], z_last[:, lo:hi])
+    grad_out[:, 0:wide] = own_sum(z) + add(far_recv[:, 0:wide], z_in[0], z_last[...])
+    grad_out[:, wide:] = add(
+        far_recv[:, wide:], grad_far[z, :, narrow:], f_in[0, :, narrow:], f_last[:, narrow:])
     v_near.wait_recv()
     there = vr[4]
     v_out[...] = v + jnp.where(at < V_MP, there, 0.0)
-    v_out[V_HEADS:V_HEADS + 2, :] = v[V_HEADS:V_HEADS + 2, :] + there[V_FAR:V_FAR + 2, :]
+    width = two + one_head
+    v_out[V_HEADS:V_HEADS + 2, 0:width] = v[V_HEADS:V_HEADS + 2, 0:width] + there[V_HEADS:V_HEADS + 2, V_FAR:V_FAR + width]
     for copy in to_other + fin_remote + onward:
         copy.wait()
-    for copy in x_copies + far_copies + to_near + z_copies + v_copies + up_copies + [far_copy, v_near, v_far]:
+    for copy in x_copies + far_copies + to_near + z_copies + v_copies + [far_copy, v_near, v_far]:
         copy.wait_send()
 
 
 def finish(dims, dnormed, dattended, states_img, states_txt, vec, fin_img, fin_txt,
-           near_img, near_txt, grad_pair, grad_single, grad_far, up_one, *tables):
+           near_img, near_txt, grad_pair, grad_far, *tables):
     pairs, patches, model = states_img.shape
     caption = states_txt.shape[1]
     quarter, slab = dims.quarter, dims.slab
-    piece, cols = grad_far.shape[1:]
+    piece, cols = grad_far.shape[1], model
+    wide, all_cols = grad_pair.shape[1], grad_far.shape[2]
     held = pl.BlockSpec(memory_space=pltpu.VMEM)
     away = pl.BlockSpec(memory_space=pl.ANY)
     n_remote = 7 * quarter + 28
     return pl.pallas_call(
         functools.partial(finish_kernel, dims),
-        in_specs=[held, held] + [away] * 2 + [held] + [away] * 4 + [held] * 8,
-        out_specs=[away] * 6 + [held] * 3,
+        in_specs=[held, held] + [away] * 2 + [held] + [away] * 4 + [held] * 6,
+        out_specs=[away] * 6 + [held] * 2,
         out_shape=[jax.ShapeDtypeStruct(v.shape, BF16) for v in (fin_img, fin_txt) * 2] + [
             jax.ShapeDtypeStruct((pairs, patches, model), BF16),
             jax.ShapeDtypeStruct((pairs, caption, model), BF16),
             jax.ShapeDtypeStruct((piece, cols), F32),
             jax.ShapeDtypeStruct((V_ROWS, model), F32),
-            jax.ShapeDtypeStruct(up_one.shape[1:], F32),
         ],
         scratch_shapes=[
             pltpu.VMEM((quarter, patches, model), BF16),
@@ -2084,9 +2084,9 @@
             pltpu.VMEM((quarter, patches, model), BF16),
             pltpu.VMEM((quarter, caption, model), BF16),
             pltpu.VMEM((slab, model), F32),
-            pltpu.VMEM((4, piece, cols), BF16), pltpu.VMEM((4, piece, cols), BF16),
-        ] + [pltpu.VMEM((2, piece, cols), BF16), pltpu.VMEM((piece, cols), BF16), pltpu.VMEM((piece, cols), BF16)] * 2 + [
-            pltpu.VMEM((2,) + up_one.shape[1:], BF16), pltpu.VMEM(up_one.shape[1:], BF16), pltpu.VMEM(up_one.shape[1:], BF16),
+            pltpu.VMEM((4, piece, wide), BF16), pltpu.VMEM((4, piece, wide), BF16),
+            pltpu.VMEM((2, piece, wide), BF16), pltpu.VMEM((piece, wide), BF16), pltpu.VMEM((piece, wide), BF16),
+            pltpu.VMEM((2, piece, all_cols), BF16), pltpu.VMEM((piece, all_cols), BF16), pltpu.VMEM((piece, all_cols), BF16),
             pltpu.VMEM((piece, cols), BF16), pltpu.VMEM((piece, cols), BF16),
             pltpu.VMEM((5, V_ROWS, model), F32),
             pltpu.VMEM((5, V_ROWS, model), F32),
@@ -2097,10 +2097,10 @@
         compiler_params=params(collective_id=1, has_side_effects=True),
         name="finish",
     )(dnormed, dattended, states_img, states_txt, vec, fin_img, fin_txt,
-      near_img, near_txt, grad_pair, grad_single, grad_far, up_one, *tables)
-
-
-def spread_kernel(dims, cols, sums, grad, gains, shifts, up_low, up_high, down, head_in, dproj, *refs):
+      near_img, near_txt, grad_pair, grad_far, *tables)
+
+
+def spread_kernel(dims, cols, sums, grad, gains, shifts, up, down, head_in, dproj, *refs):
     forward, refs = refs[:8], refs[8:]
     back_img, back_txt, *refs = refs
     outs, refs = refs[:12], refs[12:]
@@ -2143,8 +2143,7 @@
     turned[0:cols, 0:two] = grad[:, 3 * two:4 * two]
     turned[0:cols, two:two + one] = grad[:, 4 * two + 3 * one:4 * two + 4 * one]
     out_w[...] = turned[...].T[0:two + one, 0:cols]
-    up_out[0] = up_low[...]
-    up_out[1] = up_high[...]
+    up_out[...] = up[...]
     down_out[...] = down[...]
     for come, go in zip(comes, goes):
         come.wait()
@@ -2156,15 +2155,15 @@
         go.wait()
 
 
-def spread(dims, sums, grad, gains, shifts, up_low, up_high, down, head_in, dproj, forward, back_img, back_txt):
+def spread(dims, sums, grad, gains, shifts, up, down, head_in, dproj, forward, back_img, back_txt):
     cols, model = grad.shape[0], sums.shape[1]
     local, quarter = dims.local, dims.quarter
     assert cols <= 128
     shapes = [(1, cols)] * 4 + [(2, cols)] * 3 + [(1, cols)] + [(2, cols)] * 2 + [(2, model), (2, local)]
-    shapes += [(3, cols, local), (local, cols), (2,) + up_low.shape, down.shape, (2, cols, dproj.shape[2])]
+    shapes += [(3, cols, local), (local, cols), up.shape, down.shape, (2, cols, dproj.shape[2])]
     held = pl.BlockSpec(memory_space=pltpu.VMEM)
     away = pl.BlockSpec(memory_space=pl.ANY)
-    args = (sums, grad, gains, shifts, up_low, up_high, down, head_in, dproj)
+    args = (sums, grad, gains, shifts, up, down, head_in, dproj)
     return pl.pallas_call(
         functools.partial(spread_kernel, dims, cols),
         in_specs=[held] * len(args) + [away] * 10,
@@ -2273,8 +2272,8 @@
     contrast_loss = scalars[0, :1]
     grad_logit_scale = scalars[1, :1]
     if one_kernel:
-        (dnormed, grad_o01, grad_o2, cols_far, cols_own, near_img, near_txt, far_sum, up_one, grad_down,
-         up_low) = back(
+        (dnormed, grad_o01, grad_o2, cols_far, cols_own, near_img, near_txt, far_sum, grad_down,
+         grad_up) = back(
             dims, caption_lengths, dattn, dattn_peer, normed, qkv_far, mixed_far, qkv_own, mixed_own,
             own_w, output_weight, wf, fin_img, fin_txt, up_keep, up_send, down_sum)
     else:
@@ -2287,13 +2286,13 @@
     mine = lambda v, axis: lax.dynamic_slice_in_dim(v, batch_at * cols, cols, axis=axis)
     pair, single = 2 * HEAD_DIM, HEAD_DIM
     if one_kernel:
-        core_img, core_txt, across_img, across_txt, back_img, back_txt, attn_grad, sums, up_high = finish(
+        core_img, core_txt, across_img, across_txt, back_img, back_txt, attn_grad, sums = finish(
             dims, dnormed, dattended, image_states, text_states, vec, fin_img, fin_txt,
-            near_img, near_txt, grad_o01, grad_o2, far_sum, up_one, own_sums, up_sums, cols_own, cols_far)
+            near_img, near_txt, grad_o01, far_sum, own_sums, up_sums, cols_own, cols_far)
         forward = (fin_img, fin_txt, near_img, near_txt, core_img, core_txt, across_img, across_txt)
         (*vectors, grad_qkv, grad_output_weight, grad_up, grad_down, grad_head_weight,
          image_output, text_output, image_grad, text_grad) = spread(
-            dims, sums, attn_grad, grad_head_gain, grad_head_shift, up_low, up_high, grad_down, head_in, dproj,
+            dims, sums, attn_grad, grad_head_gain, grad_head_shift, grad_up, grad_down, head_in, dproj,
             forward, back_img, back_txt)
         flat = lambda v: v.reshape(-1)
         return (

time: 271 us -> 264 us (0.974)
  Pallas kernels: 269 us -> 261 us
    pallas_call x1, Pallas kernels: 46.7 us -> 36.8 us  [finish(): pl.pallas_call(functools.partial(finish_kernel, dims), in_specs=[held, he...]
where the time goes in v4:
time: 264 us; the launch traced here: 263 us
  Pallas kernels  261 us (99%)
    pallas_call x1, Pallas kernels, front(): pl.pallas_call(lambda lens, img, txt, *refs: front_kernel(dims, lens, img...  63.2 us
    pallas_call x1, Pallas kernels, middle(): pl.pallas_call(functools.partial(middle_kernel, dims, total), grid=(4,),...  56.2 us
    pallas_call x1, Pallas kernels, back(): pl.pallas_call(functools.partial(back_kernel, dims), grid=(4,), in_specs=...  52.9 us
    pallas_call x1, Pallas kernels, turn(): pl.pallas_call(functools.partial(turn_kernel, dims), grid=(12,), in_specs...  42.3 us
    pallas_call x1, Pallas kernels, finish(): pl.pallas_call(functools.partial(finish_kernel, dims), in_specs=[held, he...  36.8 us
    pallas_call x1, Pallas kernels, spread(): pl.pallas_call(functools.partial(spread_kernel, dims, cols), in_specs=[he...  9.82 us

profile of v4, /device:TPU:0, one launch (start us, length us, event | category | flops | bytes accessed | tf_op | source)
XLA Modules:
  0.0 263.4 jit_solution(18321874699695655703)
XLA Ops:
  1.3 63.2 %front.1 = (f32[16,768]{1,0:T(8,128)}, bf16[6,256,768]{2,1,0:T(8,128)(2,1)}, bf16[6,256,384]{2,1,0:T(8,128)(2,1)}, bf16[6,256,128]{2,1,0:T(8,128)(2,1)}, bf16[6,...) custom-call(s32[12]{0:T(128)} %lens.3, ...), custom_call_target="tpu_custom_call" | custom-call | flops 10871635968 | bytes 40000000 | tf_op jit(solution)/shard_map/front/pallas_call | solution.py:1243
  64.6 56.2 %middle.1 = (bf16[12,256,768]{2,1,0:T(8,128)(2,1)}, bf16[12,256,768]{2,1,0:T(8,128)(2,1)}, bf16[12,256,768]{2,1,0:T(8,128)(2,1)}, f32[3,256,768]{2,1,0:T(8,128)}...) custom-call(bf16[12,197,768]{2,1,0:T(8,128)(2,1)} %img.5, ...), custom_call_target="tpu_custom_call" | custom-call | flops 14495514624 | bytes 40000000 | tf_op jit(solution)/shard_map/middle/pallas_call | solution.py:1516
  120.7 42.3 %turn.1 = (bf16[4,2,96,768]{3,2,1,0:T(8,128)(2,1)}, bf16[4,2,96,768]{3,2,1,0:T(8,128)(2,1)}, bf16[4,2,96,768]{3,2,1,0:T(8,128)(2,1)}, f32[3,256,768]{2,1,0:T(8,1...) custom-call(bf16[12,197,768]{2,1,0:T(8,128)(2,1)} %img.5, ...), custom_call_target="tpu_custom_call" | custom-call | flops 7247757312 | bytes 40000000 | tf_op jit(solution)/shard_map/turn/pallas_call | solution.py:1692
  163.0 0.0 copy-start
  163.0 52.9 %back.1 = (f32[3,256,768]{2,1,0:T(8,128)}, bf16[768,512]{1,0:T(8,128)(2,1)}, bf16[768,256]{1,0:T(8,128)(2,1)}, f32[1,768]{1,0:T(1,128)}, f32[1,384]{1,0:T(1,128)...) custom-call(s32[12]{0:T(128)} %lens.3, ...), custom_call_target="tpu_custom_call" | custom-call | flops 16307453952 | bytes 30000000 | tf_op jit(solution)/shard_map/back/pallas_call | solution.py:1877
  216.0 0.0 copy-done
  216.0 0.5 fusion
  216.5 36.8 %finish.1 = (bf16[3,197,768]{2,1,0:T(8,128)(2,1)}, bf16[3,40,768]{2,1,0:T(8,128)(2,1)}, bf16[3,197,768]{2,1,0:T(8,128)(2,1)}, bf16[3,40,768]{2,1,0:T(8,128)(2,1)...) custom-call(f32[3,256,768]{2,1,0:T(8,128)} %get-tuple-element.131.dnorme, ...), custom_call_target="tpu_custom_call" | custom-call | tf_op jit(solution)/shard_map/finish/pallas_call | solution.py:2071
  253.4 9.8 %spread.1 = (f32[1,96]{1,0:T(1,128)}, f32[1,96]{1,0:T(1,128)}, f32[1,96]{1,0:T(1,128)}, f32[1,96]{1,0:T(1,128)}, f32[2,96]{1,0:T(2,128)}, /*index=5*/f32[2,96]{1...) custom-call(f32[16,768]{1,0:T(8,128)} %get-tuple-element.141.sums, ...), custom_call_target="tpu_custom_call" | custom-call | flops 1000000 | bytes 20000000 | tf_op jit(solution)/shard_map/spread/pallas_call | solution.py:2167
Async XLA Ops:
  163.0 52.9 %copy-start = (f32[2,128]{1,0:T(2,128)S(1)}, f32[2,128]{1,0:T(2,128)}, u32[]{:S(2)}) copy-start(f32[2,128]{1,0:T(2,128)} %get-tuple-element.157) | copy-start | bytes 3076

commit v5 on v4

--- a/solution.py
+++ b/solution.py
@@ -1275,9 +1275,9 @@
 
 
 def middle_kernel(dims, total, img, txt, own, peer, cls_own, cls_peer, vec, up, up_bias, down, head_weight, scale,
-                  act, dup, ddn, dexp, d_own, d_near, bias_grad, class_e, c_act, c_dup, c_ddn, dcls,
+                  dup, down_keep, down_send, dexp, d_own, d_near, bias_grad, class_e, c_act, c_dup, c_ddn, dcls,
                   head_in, dproj, gains, shifts, scalars,
-                  bx, bd, rx, rd, x_near, x_far, ins, rows, part, parts, cls, back, cot, c_rows, extra, extras, hidden_in, weight,
+                  bx, bd, rx, rd, x_near, x_far, ins, rows, part, parts, cls, back, cot, c_rows, extra, extras, hidden_in, weight, ddn, acc,
                   local_sem, send_sem, recv_sem):
     here = Place()
     ip, slab, quarter = dims.ip, dims.slab, dims.quarter
@@ -1297,6 +1297,7 @@
     @pl.when(i == 0)
     def _():
         fetch.start()
+        acc[...] = jnp.zeros_like(acc)
         rows[...] = jnp.zeros_like(rows)
         bias_grad[...] = jnp.zeros_like(bias_grad)
         for m in range(2):
@@ -1411,6 +1412,7 @@
             bias_grad[m:m + 1, :] += jnp.sum(du, axis=0, keepdims=True)
             low = du.astype(BF16)
             c_dup[m] = low
+            acc[m] += t_dot(c_ddn[m], c_act[m])
             extra[m] = dot_t(low, up[m])
         for copy in sent_extra:
             copy.start()
@@ -1432,10 +1434,10 @@
         u = dot(e, up[m]) + up_bias[m:m + 1]
         big, small = gelu_parts(u)
         a = (u * big).astype(BF16)
-        act[:, lo:hi, :] = a.reshape(quarter, hi - lo, -1)
         slope = big + u * small
         bd[i, :, lo:hi, :] = dot(a, down[m]).astype(BF16).reshape(quarter, hi - lo, model)
         g = ddn[:, lo:hi, :].reshape(count, model)
+        acc[m] += t_dot(g, a)
         du = dot_t(g, down[m]) * slope
         bias_grad[m:m + 1, :] += jnp.sum(du, axis=0, keepdims=True)
         low = du.astype(BF16)
@@ -1468,6 +1470,12 @@
 
     @pl.when(i == 3)
     def _():
+        piece = down_keep.shape[2]
+        block = lambda j: pl.ds(pl.multiple_of(j * piece, piece), piece)
+        for j in range(4):
+            for m in range(2):
+                down_keep[j, m] = acc[m, block(2 * j + here.x), :].astype(BF16)
+                down_send[j, m] = acc[m, block(2 * j + 1 - here.x), :].astype(BF16)
         sent_d[1].wait_recv()
 
         def add_d(p, c):
@@ -1508,7 +1516,7 @@
     half = pl.BlockSpec((quarter, slab, model), lambda i: (jnp.where(i < 2, 1, 0), 0, 0))
     step = lambda cols: pl.BlockSpec((quarter, slab, cols), lambda i: (i, 0, 0))
     rows_of = lambda n, t: jax.ShapeDtypeStruct((n, slab, model), t)
-    small = [((quarter, slab, model), F32), ((quarter, slab, model), F32), ((quarter, slab, model), BF16),
+    small = [((4, 2, model // 8, hidden), BF16)] * 2 + [((quarter, slab, model), F32), ((quarter, slab, model), F32), ((quarter, slab, model), BF16),
              ((2, hidden), F32), ((2, 16, model), BF16), ((2, 16, hidden), BF16), ((2, 16, hidden), BF16),
              ((2, 16, model), BF16), ((quarter, 8, model), F32), ((2, 16 * batch, model), BF16),
              ((2, 16 * batch, weight.shape[2]), BF16), ((2, model), F32), ((2, model), F32), ((2, 128), F32)]
@@ -1519,8 +1527,8 @@
         in_specs=[pl.BlockSpec((quarter, dims.patches, model), cot_at),
                   pl.BlockSpec((quarter, dims.caption, model), cot_at)] + [half] * 2 + [held] * 6
         + [pl.BlockSpec(memory_space=pl.ANY), held],
-        out_specs=[step(hidden), step(hidden), step(model)] + [held] * len(small),
-        out_shape=[rows_of(4 * quarter, BF16)] * 3 + [jax.ShapeDtypeStruct(v, t) for v, t in small],
+        out_specs=[step(hidden)] + [held] * len(small),
+        out_shape=[rows_of(4 * quarter, BF16)] + [jax.ShapeDtypeStruct(v, t) for v, t in small],
         scratch_shapes=[
             pltpu.VMEM((4,) + block, BF16), pltpu.VMEM((4,) + block, BF16),
             pltpu.VMEM((2,) + block, BF16), pltpu.VMEM((2,) + block, BF16),
@@ -1530,7 +1538,8 @@
             pltpu.VMEM((batch, 2, 16, model), F32), pltpu.VMEM((2, 16 * batch, model), F32),
             pltpu.VMEM((2, 32, model), F32), pltpu.VMEM((2, 16, model), F32),
             pltpu.VMEM((2, 16, model), F32), pltpu.VMEM((3, 2, 16, model), F32),
-            pltpu.VMEM((2, 16, hidden), F32), pltpu.VMEM(weight.shape, BF16), pltpu.SemaphoreType.DMA((1,)),
+            pltpu.VMEM((2, 16, hidden), F32), pltpu.VMEM(weight.shape, BF16),
+            pltpu.VMEM(block, BF16), pltpu.VMEM((2, model, hidden), F32), pltpu.SemaphoreType.DMA((1,)),
             pltpu.SemaphoreType.DMA((18,)), pltpu.SemaphoreType.DMA((18,)),
         ],
         compiler_params=params(collective_id=2, has_side_effects=True),
@@ -1540,25 +1549,23 @@
     )(img, txt, own, peer, cls_own, cls_peer, vec, up, up_bias, down, weight, scale)
 
 
-def turn_kernel(dims, img, txt, peer, own, act, dup, ddn, ce, ca, cu, cd, dexp, attended, attn, d_own, d_near, dcls, vec,
+def turn_kernel(dims, img, txt, peer, own, dup, ce, cu, down_keep, down_send, dexp, attended, attn, d_own, d_near, dcls, vec,
                 down_sum, up_keep, up_send, dattended, dattn, dattn_peer, fin_img, fin_txt, sums,
-                acc, d_far, n_peer, rows, side_send, side_recv, e_in, dexp_in, attended_in, attn_in, d_own_in,
+                acc, d_far, n_peer, rows, side_keep, side_recv, e_in, dexp_in, attended_in, attn_in, d_own_in,
                 local_sem, send_sem, recv_sem):
     here = Place()
     quarter, ip = dims.quarter, dims.ip
     i = pl.program_id(0)
-    piece = side_send.shape[3]
+    piece = side_keep.shape[2]
     sent_near = remote(d_near, d_far, send_sem, recv_sem, 0, here.near)
 
     def over(p):
         return remote(dattn.at[p], n_peer.at[p], send_sem, recv_sem, 1 + p, here.core)
 
     sent_core = [over(p) for p in range(quarter)]
-    sent_side = [remote(side_send.at[h], side_recv.at[h], send_sem, recv_sem, 1 + quarter + h, here.side)
-                 for h in range(2)]
-    part = acc.shape[2] // 2
+    sent_side = remote(down_send, side_recv, send_sem, recv_sem, 1 + quarter, here.side)
     loaded = [pltpu.make_async_copy(src, dst, local_sem.at[j]) for j, (src, dst) in enumerate((
-        (dexp, dexp_in), (attended, attended_in), (attn, attn_in), (d_own, d_own_in)))]
+        (dexp, dexp_in), (attended, attended_in), (attn, attn_in), (d_own, d_own_in), (down_keep, side_keep)))]
     dexp, attended, attn, d_own = dexp_in, attended_in, attn_in, d_own_in
     spans = ((0, 0, ip), (1, ip, dims.slab))
     flat = lambda v: v.reshape(-1, v.shape[-1])
@@ -1568,45 +1575,24 @@
     def _():
         meet([here.core, here.near, here.side])
         sent_near.start()
+        sent_side.start()
         for copy in loaded:
             copy.start()
         for m in range(2):
-            acc[m] = t_dot(cd[m], ca[m])
-
-    for h in range(2):
-        @pl.when(i // 4 == h)
-        def _():
-            for m, lo, hi in spans:
-                acc[m, :, h * part:(h + 1) * part] += t_dot(flat(ddn[:, lo:hi, :]), flat(act[:, lo:hi, :]))
-
-        @pl.when(i == 4 * h + 3)
-        def _():
-            cols = slice(h * part, (h + 1) * part)
-            for j in range(4):
-                for m in range(2):
-                    side_send[h, j, m] = acc[m, block(2 * j + 1 - here.x), cols].astype(BF16)
-                    down_sum[j, m, :, cols] = acc[m, block(2 * j + here.x), cols].astype(BF16)
-            sent_side[h].start()
-
-    @pl.when(i == 8)
-    def _():
-        for m in range(2):
             acc[m] = t_dot(ce[m], cu[m])
 
-    @pl.when((i >= 8) & (i % 2 == 0))
+    @pl.when(i % 2 == 0)
     def _():
         e_in[...] = peer[...]
 
-    @pl.when((i >= 8) & (i % 2 == 1))
+    @pl.when(i % 2 == 1)
     def _():
         e_in[...] = own[...]
 
-    @pl.when(i >= 8)
-    def _():
-        for m, lo, hi in spans:
-            acc[m] += t_dot(flat(e_in[:, lo:hi, :]), flat(dup[:, lo:hi, :]))
-
-    @pl.when(i == 11)
+    for m, lo, hi in spans:
+        acc[m] += t_dot(flat(e_in[:, lo:hi, :]), flat(dup[:, lo:hi, :]))
+
+    @pl.when(i == 3)
     def _():
         for j in range(4):
             for m in range(2):
@@ -1660,18 +1646,15 @@
         for p in range(quarter):
             sent_core[p].wait()
             dattn_peer[p] = n_peer[p]
-        for h in range(2):
-            sent_side[h].wait()
-            cols = slice(h * part, (h + 1) * part)
-            for j in range(4):
-                down_sum[j, :, :, cols] = (
-                    down_sum[j, :, :, cols].astype(F32) + side_recv[h, j].astype(F32)).astype(BF16)
+        sent_side.wait()
+        for j in range(4):
+            down_sum[j] = (side_keep[j].astype(F32) + side_recv[j].astype(F32)).astype(BF16)
         sent_near.wait_send()
 
 
-def turn(dims, img, txt, peer, own, act, dup, ddn, ce, ca, cu, cd, dexp, attended, attn, d_own, d_near, dcls, vec):
+def turn(dims, img, txt, peer, own, dup, ce, cu, down_keep, down_send, dexp, attended, attn, d_own, d_near, dcls, vec):
     model = own.shape[-1]
-    hidden = act.shape[-1]
+    hidden = dup.shape[-1]
     slab, quarter = dims.slab, dims.quarter
     held = pl.BlockSpec(memory_space=pltpu.VMEM)
 
@@ -1679,37 +1662,33 @@
         return Place().quarter(0, 0), 0, 0
 
     away = pl.BlockSpec(memory_space=pl.ANY)
-    half = pl.BlockSpec((quarter, slab, model), lambda i: (jnp.where(i < 10, 1, 0), 0, 0))
-    row = lambda i: jnp.where(i < 8, i % 4, 3)
-    first = pl.BlockSpec((quarter, slab, model), lambda i: (row(i), 0, 0))
-    piece = pl.BlockSpec((quarter, slab, hidden // 2), lambda i: (row(i), 0, jnp.minimum(i // 4, 1)))
-    last = pl.BlockSpec((quarter, slab, hidden), lambda i: (jnp.maximum(i - 8, 0), 0, 0))
+    half = pl.BlockSpec((quarter, slab, model), lambda i: (jnp.where(i < 2, 1, 0), 0, 0))
+    step = pl.BlockSpec((quarter, slab, hidden), lambda i: (i, 0, 0))
     block = (quarter, slab, model)
     part = (4, 2, model // 8, hidden)
-    split = (2, 4, 2, model // 8, hidden // 2)
     outs = [(part, BF16), (part, BF16), (part, BF16), (block, F32), (block, BF16), (block, BF16),
             ((quarter, dims.patches, model), BF16), ((quarter, dims.caption, model), BF16), ((16, model), F32)]
     return pl.pallas_call(
         functools.partial(turn_kernel, dims),
-        grid=(12,),
+        grid=(4,),
         in_specs=[pl.BlockSpec((quarter, dims.patches, model), own_at),
-                  pl.BlockSpec((quarter, dims.caption, model), own_at)] + [half] * 2 + [piece, last, first]
-        + [held] * 4 + [away] * 4 + [held] * 3,
+                  pl.BlockSpec((quarter, dims.caption, model), own_at)] + [half] * 2 + [step]
+        + [held] * 2 + [away] * 6 + [held] * 3,
         out_specs=[held] * len(outs),
         out_shape=[jax.ShapeDtypeStruct(v, t) for v, t in outs],
         scratch_shapes=[
             pltpu.VMEM((2, model, hidden), F32), pltpu.VMEM(block, BF16), pltpu.VMEM(block, BF16),
-            pltpu.VMEM((slab, model), F32), pltpu.VMEM(split, BF16), pltpu.VMEM(split, BF16),
+            pltpu.VMEM((slab, model), F32), pltpu.VMEM(part, BF16), pltpu.VMEM(part, BF16),
             pltpu.VMEM(block, BF16),
         ] + [pltpu.VMEM(block, F32)] * 4 + [
-            pltpu.SemaphoreType.DMA((4,)),
-            pltpu.SemaphoreType.DMA((3 + quarter,)), pltpu.SemaphoreType.DMA((3 + quarter,)),
+            pltpu.SemaphoreType.DMA((5,)),
+            pltpu.SemaphoreType.DMA((2 + quarter,)), pltpu.SemaphoreType.DMA((2 + quarter,)),
         ],
         compiler_params=params(collective_id=3, has_side_effects=True),
         cost_estimate=pl.CostEstimate(
             flops=16 * quarter * slab * model * hidden, bytes_accessed=40_000_000, transcendentals=0),
         name="turn",
-    )(img, txt, peer, own, act, dup, ddn, ce, ca, cu, cd, dexp, attended, attn, d_own, d_near, dcls, vec)
+    )(img, txt, peer, own, dup, ce, cu, down_keep, down_send, dexp, attended, attn, d_own, d_near, dcls, vec)
 
 
 def back_kernel(dims, lens, d_own, d_peer, normed, qkv_far, mixed_far, qkv_own, mixed_own, wq, wo, wf,
@@ -2222,12 +2201,12 @@
         e_peer = to_core(e_own)
         cls_peer = to_core(cls_own)
     if one_kernel:
-        (act, dup, ddn, dexp, d_own, d_near, up_sums, class_e, c_act, c_dup, c_ddn, dcls, head_in, dproj,
+        (dup, down_keep, down_send, dexp, d_own, d_near, up_sums, class_e, _, c_dup, _, dcls, head_in, dproj,
          grad_head_gain, grad_head_shift, scalars) = middle(
             dims, pairs * batch_size, image_cotangent, text_cotangent, e_own, e_peer, cls_own, cls_peer, vec,
             expert_up, expert_up_bias, expert_down, head_weight, logit_scale.reshape(1, 1))
         down_sum, up_keep, up_send, dattended, dattn, dattn_peer, fin_img, fin_txt, own_sums = turn(
-            dims, image_cotangent, text_cotangent, e_peer, e_own, act, dup, ddn, class_e, c_act, c_dup, c_ddn,
+            dims, image_cotangent, text_cotangent, e_peer, e_own, dup, class_e, c_dup, down_keep, down_send,
             dexp, attended, attn, d_own, d_near, dcls, vec)
     else:
         class_part, class_e = class_forward(dims, cls_own, cls_peer, expert_up, expert_up_bias, expert_down)

time: 264 us -> 259 us (0.981)
  Pallas kernels: 261 us -> 257 us
    pallas_call x1, Pallas kernels: 42.3 us -> 36.8 us  [turn(): pl.pallas_call(functools.partial(turn_kernel, dims), grid=(4,), in_specs=...]
where the time goes in v5:
time: 259 us
  Pallas kernels  257 us (99%)
    pallas_call x1, Pallas kernels, front(): pl.pallas_call(lambda lens, img, txt, *refs: front_kernel(dims, lens, img...  63.1 us
    pallas_call x1, Pallas kernels, middle(): pl.pallas_call(functools.partial(middle_kernel, dims, total), grid=(4,),...  58 us
    pallas_call x1, Pallas kernels, back(): pl.pallas_call(functools.partial(back_kernel, dims), grid=(4,), in_specs=...  51.8 us
    pallas_call x1, Pallas kernels, finish(): pl.pallas_call(functools.partial(finish_kernel, dims), in_specs=[held, he...  37.3 us
    pallas_call x1, Pallas kernels, turn(): pl.pallas_call(functools.partial(turn_kernel, dims), grid=(4,), in_specs=...  36.8 us
    pallas_call x1, Pallas kernels, spread(): pl.pallas_call(functools.partial(spread_kernel, dims, cols), in_specs=[he...  9.82 us

profile of v5, /device:TPU:0, one launch (start us, length us, event | category | flops | bytes accessed | tf_op | source)
XLA Modules:
  0.0 259.0 jit_solution(2302922072408871149)
XLA Ops:
  1.3 63.1 %front.1 = (f32[16,768]{1,0:T(8,128)}, bf16[6,256,768]{2,1,0:T(8,128)(2,1)}, bf16[6,256,384]{2,1,0:T(8,128)(2,1)}, bf16[6,256,128]{2,1,0:T(8,128)(2,1)}, bf16[6,...) custom-call(s32[12]{0:T(128)} %lens.3, ...), custom_call_target="tpu_custom_call" | custom-call | flops 10871635968 | bytes 40000000 | tf_op jit(solution)/shard_map/front/pallas_call | solution.py:1243
  64.5 58.0 %middle.1 = (bf16[12,256,768]{2,1,0:T(8,128)(2,1)}, bf16[4,2,96,768]{3,2,1,0:T(8,128)(2,1)}, bf16[4,2,96,768]{3,2,1,0:T(8,128)(2,1)}, f32[3,256,768]{2,1,0:T(8,1...) custom-call(bf16[12,197,768]{2,1,0:T(8,128)(2,1)} %img.5, ...), custom_call_target="tpu_custom_call" | custom-call | flops 14495514624 | bytes 40000000 | tf_op jit(solution)/shard_map/middle/pallas_call | solution.py:1524
  122.5 36.8 %turn.1 = (bf16[4,2,96,768]{3,2,1,0:T(8,128)(2,1)}, bf16[4,2,96,768]{3,2,1,0:T(8,128)(2,1)}, bf16[4,2,96,768]{3,2,1,0:T(8,128)(2,1)}, f32[3,256,768]{2,1,0:T(8,1...) custom-call(bf16[12,197,768]{2,1,0:T(8,128)(2,1)} %img.5, ...), custom_call_target="tpu_custom_call" | custom-call | flops 7247757312 | bytes 40000000 | tf_op jit(solution)/shard_map/turn/pallas_call | solution.py:1671
  159.3 0.0 copy-start
  159.3 51.8 %back.1 = (f32[3,256,768]{2,1,0:T(8,128)}, bf16[768,512]{1,0:T(8,128)(2,1)}, bf16[768,256]{1,0:T(8,128)(2,1)}, f32[1,768]{1,0:T(1,128)}, f32[1,384]{1,0:T(1,128)...) custom-call(s32[12]{0:T(128)} %lens.3, ...), custom_call_target="tpu_custom_call" | custom-call | flops 16307453952 | bytes 30000000 | tf_op jit(solution)/shard_map/back/pallas_call | solution.py:1856
  211.1 0.0 copy-done
  211.1 0.5 fusion
  211.6 37.3 %finish.1 = (bf16[3,197,768]{2,1,0:T(8,128)(2,1)}, bf16[3,40,768]{2,1,0:T(8,128)(2,1)}, bf16[3,197,768]{2,1,0:T(8,128)(2,1)}, bf16[3,40,768]{2,1,0:T(8,128)(2,1)...) custom-call(f32[3,256,768]{2,1,0:T(8,128)} %get-tuple-element.127.dnorme, ...), custom_call_target="tpu_custom_call" | custom-call | tf_op jit(solution)/shard_map/finish/pallas_call | solution.py:2050
  248.9 9.8 %spread.1 = (f32[1,96]{1,0:T(1,128)}, f32[1,96]{1,0:T(1,128)}, f32[1,96]{1,0:T(1,128)}, f32[1,96]{1,0:T(1,128)}, f32[2,96]{1,0:T(2,128)}, /*index=5*/f32[2,96]{1...) custom-call(f32[16,768]{1,0:T(8,128)} %get-tuple-element.137.sums, ...), custom_call_target="tpu_custom_call" | custom-call | flops 1000000 | bytes 20000000 | tf_op jit(solution)/shard_map/spread/pallas_call | solution.py:2146
Async XLA Ops:
  159.3 51.8 %copy-start = (f32[2,128]{1,0:T(2,128)S(1)}, f32[2,128]{1,0:T(2,128)}, u32[]{:S(2)}) copy-start(f32[2,128]{1,0:T(2,128)} %get-tuple-element.153) | copy-start | bytes 3076

commit v6 on v5

--- a/solution.py
+++ b/solution.py
@@ -1277,7 +1277,7 @@
 def middle_kernel(dims, total, img, txt, own, peer, cls_own, cls_peer, vec, up, up_bias, down, head_weight, scale,
                   dup, down_keep, down_send, dexp, d_own, d_near, bias_grad, class_e, c_act, c_dup, c_ddn, dcls,
                   head_in, dproj, gains, shifts, scalars,
-                  bx, bd, rx, rd, x_near, x_far, ins, rows, part, parts, cls, back, cot, c_rows, extra, extras, hidden_in, weight, ddn, acc,
+                  bx, bd, rx, rd, x_near, x_far, ins, rows, part, parts, cls, back, cot, c_rows, extra, extras, hidden_in, weight, ddn, acc, stage,
                   local_sem, send_sem, recv_sem):
     here = Place()
     ip, slab, quarter = dims.ip, dims.slab, dims.quarter
@@ -1289,7 +1289,10 @@
 
     sent_x = [remote(bx.at[2 * j], rx.at[j], send_sem, recv_sem, j, here.core) for j in range(2)]
     sent_d = [remote(bd.at[2 * j], rd.at[j], send_sem, recv_sem, 2 + j, here.core) for j in range(2)]
-    sent_near = remote(x_near, x_far, send_sem, recv_sem, 4, here.near)
+    def near(p):
+        return remote(x_near.at[p], x_far.at[p], send_sem, recv_sem, 18 + p, here.near)
+
+    sent_near = [near(p) for p in range(quarter)]
     sent_part = [remote(part, parts.at[k], send_sem, recv_sem, 5 + k, mp_peers[k]) for k in range(3)]
     sent_extra = [remote(extra, extras.at[k], send_sem, recv_sem, 8 + k, mp_peers[k]) for k in range(3)]
     sent_cls = [remote(cls.at[here.b], cls.at[here.b], send_sem, recv_sem, 11 + k, here.batch[k]) for k in range(7)]
@@ -1459,7 +1462,8 @@
             return c
 
         lax.fori_loop(0, quarter, add_x, 0)
-        sent_near.start()
+        for copy in sent_near:
+            copy.start()
         sent_d[0].wait_recv()
 
         def add_d(p, c):
@@ -1470,12 +1474,16 @@
 
     @pl.when(i == 3)
     def _():
-        piece = down_keep.shape[2]
+        piece = stage.shape[3]
         block = lambda j: pl.ds(pl.multiple_of(j * piece, piece), piece)
         for j in range(4):
             for m in range(2):
-                down_keep[j, m] = acc[m, block(2 * j + here.x), :].astype(BF16)
-                down_send[j, m] = acc[m, block(2 * j + 1 - here.x), :].astype(BF16)
+                stage[0, j, m] = acc[m, block(2 * j + here.x), :].astype(BF16)
+                stage[1, j, m] = acc[m, block(2 * j + 1 - here.x), :].astype(BF16)
+        leave = [pltpu.make_async_copy(stage.at[k], dst, local_sem.at[1 + k])
+                 for k, dst in enumerate((down_keep, down_send))]
+        for copy in leave:
+            copy.start()
         sent_d[1].wait_recv()
 
         def add_d(p, c):
@@ -1484,9 +1492,9 @@
 
         lax.fori_loop(0, quarter, add_d, 0)
         sent_x[1].wait_recv()
-        sent_near.wait_recv()
 
         def add_x(p, c):
+            near(p).wait_recv()
             dexp[p] = bx[3, p].astype(F32) + rx[1, p].astype(F32) + x_far[p].astype(F32)
             return c
 
@@ -1498,7 +1506,9 @@
                 line = [x[m, own_row(dims, r, p):own_row(dims, r, p) + 1, :]
                         for x, r in ((extra, 0), (extras.at[0], 2), (extras.at[1], 1), (extras.at[2], 3))]
                 dexp[p, m * ip:m * ip + 1, :] += (line[0] + line[1]) + (line[2] + line[3])
-        for copy in sent_x + sent_d + [sent_near] + sent_part + sent_extra + sent_cls:
+        for copy in leave:
+            copy.wait()
+        for copy in sent_x + sent_d + sent_near + sent_part + sent_extra + sent_cls:
             copy.wait_send()
 
 
@@ -1527,7 +1537,7 @@
         in_specs=[pl.BlockSpec((quarter, dims.patches, model), cot_at),
                   pl.BlockSpec((quarter, dims.caption, model), cot_at)] + [half] * 2 + [held] * 6
         + [pl.BlockSpec(memory_space=pl.ANY), held],
-        out_specs=[step(hidden)] + [held] * len(small),
+        out_specs=[step(hidden)] + [pl.BlockSpec(memory_space=pl.ANY)] * 2 + [held] * (len(small) - 2),
         out_shape=[rows_of(4 * quarter, BF16)] + [jax.ShapeDtypeStruct(v, t) for v, t in small],
         scratch_shapes=[
             pltpu.VMEM((4,) + block, BF16), pltpu.VMEM((4,) + block, BF16),
@@ -1539,8 +1549,9 @@
             pltpu.VMEM((2, 32, model), F32), pltpu.VMEM((2, 16, model), F32),
             pltpu.VMEM((2, 16, model), F32), pltpu.VMEM((3, 2, 16, model), F32),
             pltpu.VMEM((2, 16, hidden), F32), pltpu.VMEM(weight.shape, BF16),
-            pltpu.VMEM(block, BF16), pltpu.VMEM((2, model, hidden), F32), pltpu.SemaphoreType.DMA((1,)),
-            pltpu.SemaphoreType.DMA((18,)), pltpu.SemaphoreType.DMA((18,)),
+            pltpu.VMEM(block, BF16), pltpu.VMEM((2, model, hidden), F32),
+            pltpu.VMEM((2, 4, 2, model // 8, hidden), BF16), pltpu.SemaphoreType.DMA((3,)),
+            pltpu.SemaphoreType.DMA((18 + quarter,)), pltpu.SemaphoreType.DMA((18 + quarter,)),
         ],
         compiler_params=params(collective_id=2, has_side_effects=True),
         cost_estimate=pl.CostEstimate(
@@ -1557,7 +1568,11 @@
     quarter, ip = dims.quarter, dims.ip
     i = pl.program_id(0)
     piece = side_keep.shape[2]
-    sent_near = remote(d_near, d_far, send_sem, recv_sem, 0, here.near)
+
+    def near(p):
+        return remote(d_near.at[p], d_far.at[p], send_sem, recv_sem, 2 + quarter + p, here.near)
+
+    sent_near = [near(p) for p in range(quarter)]
 
     def over(p):
         return remote(dattn.at[p], n_peer.at[p], send_sem, recv_sem, 1 + p, here.core)
@@ -1574,7 +1589,8 @@
     @pl.when(i == 0)
     def _():
         meet([here.core, here.near, here.side])
-        sent_near.start()
+        for copy in sent_near:
+            copy.start()
         sent_side.start()
         for copy in loaded:
             copy.start()
@@ -1626,10 +1642,9 @@
             return c
 
         lax.fori_loop(0, quarter, norm, 0)
-        sent_near.wait_recv()
-
         def final(p, c):
             load(p)
+            near(p).wait_recv()
             for m, lo, hi in ((0, 0, ip), (1, ip, dims.slab)):
                 b = d_own[p, lo:hi, :] + d_far[p, lo:hi, :].astype(F32) + vector(vec, F_BIAS + m)
                 f = attended[p, lo:hi, :] + vector(vec, F_SCALE) * b
@@ -1649,7 +1664,8 @@
         sent_side.wait()
         for j in range(4):
             down_sum[j] = (side_keep[j].astype(F32) + side_recv[j].astype(F32)).astype(BF16)
-        sent_near.wait_send()
+        for copy in sent_near:
+            copy.wait_send()
 
 
 def turn(dims, img, txt, peer, own, dup, ce, cu, down_keep, down_send, dexp, attended, attn, d_own, d_near, dcls, vec):
@@ -1682,7 +1698,7 @@
             pltpu.VMEM(block, BF16),
         ] + [pltpu.VMEM(block, F32)] * 4 + [
             pltpu.SemaphoreType.DMA((5,)),
-            pltpu.SemaphoreType.DMA((2 + quarter,)), pltpu.SemaphoreType.DMA((2 + quarter,)),
+            pltpu.SemaphoreType.DMA((2 + 2 * quarter,)), pltpu.SemaphoreType.DMA((2 + 2 * quarter,)),
         ],
         compiler_params=params(collective_id=3, has_side_effects=True),
         cost_estimate=pl.CostEstimate(
@@ -2084,7 +2100,7 @@
     back_img, back_txt, *refs = refs
     outs, refs = refs[:12], refs[12:]
     (qkv, out_w, up_out, down_out, head_out, out_img, out_txt, grad_img, grad_txt,
-     turned, held_img, held_txt, in_sem, out_sem) = refs
+     turned, held_img, held_txt, held_up, held_down, h_in, d_in, in_sem, out_sem) = refs
     here = Place()
     quarter = dims.quarter
     whose = [here.quarter(0, 0), here.quarter(1, 0), here.quarter(0, 1), here.quarter(1, 1)]
@@ -2098,7 +2114,11 @@
                 at = 4 * r + 2 * j + k
                 comes.append(pltpu.make_async_copy(source, held.at[2 * r + k], in_sem.at[at]))
                 goes.append(pltpu.make_async_copy(held.at[2 * r + k], target.at[place(q)], out_sem.at[at]))
-    for copy in comes:
+    for at, (src, held, dst) in enumerate(((up, held_up, up_out), (down, held_down, down_out))):
+        comes.append(pltpu.make_async_copy(src, held, in_sem.at[16 + at]))
+        goes.append(pltpu.make_async_copy(held, dst, out_sem.at[16 + at]))
+    late = [pltpu.make_async_copy(head_in, h_in, in_sem.at[18]), pltpu.make_async_copy(dproj, d_in, in_sem.at[19])]
+    for copy in late + comes:
         copy.start()
     turn_by = sums.shape[1] - here.b * cols
 
@@ -2122,14 +2142,14 @@
     turned[0:cols, 0:two] = grad[:, 3 * two:4 * two]
     turned[0:cols, two:two + one] = grad[:, 4 * two + 3 * one:4 * two + 4 * one]
     out_w[...] = turned[...].T[0:two + one, 0:cols]
-    up_out[...] = up[...]
-    down_out[...] = down[...]
+    for copy in late:
+        copy.wait()
+    for m in range(2):
+        part = pltpu.roll(h_in[m].astype(F32), turn_by, 1)[:, 0:128].astype(BF16)
+        head_out[m] = t_dot(part, d_in[m])[0:cols]
     for come, go in zip(comes, goes):
         come.wait()
         go.start()
-    for m in range(2):
-        part = pltpu.roll(head_in[m].astype(F32), turn_by, 1)[:, 0:128].astype(BF16)
-        head_out[m] = t_dot(part, dproj[m])[0:cols]
     for go in goes:
         go.wait()
 
@@ -2145,14 +2165,16 @@
     args = (sums, grad, gains, shifts, up, down, head_in, dproj)
     return pl.pallas_call(
         functools.partial(spread_kernel, dims, cols),
-        in_specs=[held] * len(args) + [away] * 10,
-        out_specs=[held] * len(shapes) + [away] * 4,
+        in_specs=[held] * 4 + [away] * (len(args) - 4 + 10),
+        out_specs=[held] * (len(shapes) - 3) + [away] * 2 + [held] + [away] * 4,
         out_shape=[jax.ShapeDtypeStruct(v, F32) for v in shapes]
         + [jax.ShapeDtypeStruct(v.shape, BF16) for v in (back_img, back_txt) * 2],
         scratch_shapes=[
             pltpu.VMEM((128, 256), F32),
             pltpu.VMEM((8, quarter, dims.patches, model), BF16), pltpu.VMEM((8, quarter, dims.caption, model), BF16),
-            pltpu.SemaphoreType.DMA((16,)), pltpu.SemaphoreType.DMA((16,)),
+            pltpu.VMEM(up.shape, F32), pltpu.VMEM(down.shape, F32),
+            pltpu.VMEM(head_in.shape, BF16), pltpu.VMEM(dproj.shape, BF16),
+            pltpu.SemaphoreType.DMA((20,)), pltpu.SemaphoreType.DMA((18,)),
         ],
         compiler_params=params(),
         cost_estimate=pl.CostEstimate(flops=1_000_000, bytes_accessed=20_000_000, transcendentals=0),

time: 259 us -> 258 us (level)
  no operation moved by 1% of the time
where the time goes in v6:
time: 258 us
  Pallas kernels  255 us (99%)
    pallas_call x1, Pallas kernels, front(): pl.pallas_call(lambda lens, img, txt, *refs: front_kernel(dims, lens, img...  63.1 us
    pallas_call x1, Pallas kernels, middle(): pl.pallas_call(functools.partial(middle_kernel, dims, total), grid=(4,),...  57.4 us
    pallas_call x1, Pallas kernels, back(): pl.pallas_call(functools.partial(back_kernel, dims), grid=(4,), in_specs=...  51.8 us
    pallas_call x1, Pallas kernels, finish(): pl.pallas_call(functools.partial(finish_kernel, dims), in_specs=[held, he...  37.3 us
    pallas_call x1, Pallas kernels, turn(): pl.pallas_call(functools.partial(turn_kernel, dims), grid=(4,), in_specs=...  35.8 us
    pallas_call x1, Pallas kernels, spread(): pl.pallas_call(functools.partial(spread_kernel, dims, cols), in_specs=[he...  9.97 us

profile of v6, /device:TPU:0, one launch (start us, length us, event | category | flops | bytes accessed | tf_op | source)
XLA Modules:
  0.0 257.5 jit_solution(1310338036465826625)
XLA Ops:
  1.3 63.1 %front.1 = (f32[16,768]{1,0:T(8,128)}, bf16[6,256,768]{2,1,0:T(8,128)(2,1)}, bf16[6,256,384]{2,1,0:T(8,128)(2,1)}, bf16[6,256,128]{2,1,0:T(8,128)(2,1)}, bf16[6,...) custom-call(s32[12]{0:T(128)} %lens.3, ...), custom_call_target="tpu_custom_call" | custom-call | flops 10871635968 | bytes 40000000 | tf_op jit(solution)/shard_map/front/pallas_call | solution.py:1243
  64.5 57.4 %middle.1 = (bf16[12,256,768]{2,1,0:T(8,128)(2,1)}, bf16[4,2,96,768]{3,2,1,0:T(8,128)(2,1)}, bf16[4,2,96,768]{3,2,1,0:T(8,128)(2,1)}, f32[3,256,768]{2,1,0:T(8,1...) custom-call(bf16[12,197,768]{2,1,0:T(8,128)(2,1)} %img.5, ...), custom_call_target="tpu_custom_call" | custom-call | flops 14495514624 | bytes 40000000 | tf_op jit(solution)/shard_map/middle/pallas_call | solution.py:1534
  121.9 35.8 %turn.1 = (bf16[4,2,96,768]{3,2,1,0:T(8,128)(2,1)}, bf16[4,2,96,768]{3,2,1,0:T(8,128)(2,1)}, bf16[4,2,96,768]{3,2,1,0:T(8,128)(2,1)}, f32[3,256,768]{2,1,0:T(8,1...) custom-call(bf16[12,197,768]{2,1,0:T(8,128)(2,1)} %img.5, ...), custom_call_target="tpu_custom_call" | custom-call | flops 7247757312 | bytes 40000000 | tf_op jit(solution)/shard_map/turn/pallas_call | solution.py:1687
  157.7 0.0 copy-start
  157.7 51.8 %back.1 = (f32[3,256,768]{2,1,0:T(8,128)}, bf16[768,512]{1,0:T(8,128)(2,1)}, bf16[768,256]{1,0:T(8,128)(2,1)}, f32[1,768]{1,0:T(1,128)}, f32[1,384]{1,0:T(1,128)...) custom-call(s32[12]{0:T(128)} %lens.3, ...), custom_call_target="tpu_custom_call" | custom-call | flops 16307453952 | bytes 30000000 | tf_op jit(solution)/shard_map/back/pallas_call | solution.py:1872
  209.5 0.0 copy-done
  209.5 0.5 fusion
  210.1 37.3 %finish.1 = (bf16[3,197,768]{2,1,0:T(8,128)(2,1)}, bf16[3,40,768]{2,1,0:T(8,128)(2,1)}, bf16[3,197,768]{2,1,0:T(8,128)(2,1)}, bf16[3,40,768]{2,1,0:T(8,128)(2,1)...) custom-call(f32[3,256,768]{2,1,0:T(8,128)} %get-tuple-element.127.dnorme, ...), custom_call_target="tpu_custom_call" | custom-call | tf_op jit(solution)/shard_map/finish/pallas_call | solution.py:2066
  247.3 10.0 %spread.1 = (f32[1,96]{1,0:T(1,128)}, f32[1,96]{1,0:T(1,128)}, f32[1,96]{1,0:T(1,128)}, f32[1,96]{1,0:T(1,128)}, f32[2,96]{1,0:T(2,128)}, /*index=5*/f32[2,96]{1...) custom-call(f32[16,768]{1,0:T(8,128)} %get-tuple-element.137.sums, ...), custom_call_target="tpu_custom_call" | custom-call | flops 1000000 | bytes 20000000 | tf_op jit(solution)/shard_map/spread/pallas_call | solution.py:2166
Async XLA Ops:
  157.7 51.8 %copy-start = (f32[2,128]{1,0:T(2,128)S(1)}, f32[2,128]{1,0:T(2,128)}, u32[]{:S(2)}) copy-start(f32[2,128]{1,0:T(2,128)} %get-tuple-element.153) | copy-start | bytes 3076

commit v7 on v6

--- a/solution.py
+++ b/solution.py
@@ -1459,11 +1459,10 @@
 
         def add_x(p, c):
             x_near[p] = (bx[1, p].astype(F32) + rx[0, p].astype(F32)).astype(BF16)
+            near(p).start()
             return c
 
         lax.fori_loop(0, quarter, add_x, 0)
-        for copy in sent_near:
-            copy.start()
         sent_d[0].wait_recv()
 
         def add_d(p, c):
@@ -1905,7 +1904,7 @@
 def finish_kernel(dims, dnormed, dattended, states_img, states_txt, vec, fin_img, fin_txt,
                   near_img, near_txt, grad_pair, grad_far, own_sums, up_sums, cols_own, cols_far,
                   core_img, core_txt, across_img, across_txt, back_img, back_txt, grad_out, v_out,
-                  s_img, s_txt, d_img, d_txt, rows, xr, zs, z_in, z_pass, z_last, f_in, f_pass, f_last, far_sum, far_recv, vs, vr,
+                  n_in, a_in, s_img, s_txt, d_img, d_txt, rows, xr, zs, z_in, z_pass, z_last, f_in, f_pass, f_last, far_sum, far_recv, vs, vr,
                   local_sem, send_sem, recv_sem):
     quarter = dims.quarter
     here = Place()
@@ -1920,7 +1919,10 @@
 
     loaded = [pltpu.make_async_copy(states_img.at[pl.ds(m * quarter, quarter)], s_img, local_sem.at[0]),
               pltpu.make_async_copy(states_txt.at[pl.ds(m * quarter, quarter)], s_txt, local_sem.at[1])]
-    for copy in loaded:
+    count = 2 + 2 * quarter
+    pairs_in = [pltpu.make_async_copy(src.at[p], dst.at[p], local_sem.at[count + 2 * p + k])
+                for p in range(quarter) for k, (src, dst) in enumerate(((dnormed, n_in), (dattended, a_in)))]
+    for copy in loaded + pairs_in:
         copy.start()
     meet([here.core, here.near, here.side, here.paired, here.opposite])
 
@@ -1949,10 +1951,12 @@
     for p in range(quarter):
         load_rows(dims, p, s_img, s_txt, rows)
         n, r = normalise(rows[...])
-        dy = dnormed[p]
+        for copy in pairs_in[2 * p:2 * p + 2]:
+            copy.wait()
+        dy = n_in[p]
         total[0] = total[0] + jnp.sum(dy * n, axis=0, keepdims=True)
         total[1] = total[1] + jnp.sum(dy, axis=0, keepdims=True)
-        d = dattended[p] + norm_back(n, r, dy * vector(vec, GAIN1))
+        d = a_in[p] + norm_back(n, r, dy * vector(vec, GAIN1))
         d_img[p] = d[0:dims.patches].astype(BF16)
         d_txt[p] = d[dims.ip:dims.ip + dims.caption].astype(BF16)
         for j, (src, dst) in enumerate(((d_img, back_img), (d_txt, back_txt))):
@@ -2065,7 +2069,7 @@
     n_remote = 7 * quarter + 28
     return pl.pallas_call(
         functools.partial(finish_kernel, dims),
-        in_specs=[held, held] + [away] * 2 + [held] + [away] * 4 + [held] * 6,
+        in_specs=[away] * 4 + [held] + [away] * 4 + [held] * 6,
         out_specs=[away] * 6 + [held] * 2,
         out_shape=[jax.ShapeDtypeStruct(v.shape, BF16) for v in (fin_img, fin_txt) * 2] + [
             jax.ShapeDtypeStruct((pairs, patches, model), BF16),
@@ -2074,6 +2078,7 @@
             jax.ShapeDtypeStruct((V_ROWS, model), F32),
         ],
         scratch_shapes=[
+            pltpu.VMEM((quarter, slab, model), F32), pltpu.VMEM((quarter, slab, model), F32),
             pltpu.VMEM((quarter, patches, model), BF16),
             pltpu.VMEM((quarter, caption, model), BF16),
             pltpu.VMEM((quarter, patches, model), BF16),
@@ -2085,7 +2090,7 @@
             pltpu.VMEM((piece, cols), BF16), pltpu.VMEM((piece, cols), BF16),
             pltpu.VMEM((5, V_ROWS, model), F32),
             pltpu.VMEM((5, V_ROWS, model), F32),
-            pltpu.SemaphoreType.DMA((2 + 2 * quarter,)),
+            pltpu.SemaphoreType.DMA((2 + 4 * quarter,)),
             pltpu.SemaphoreType.DMA((n_remote,)),
             pltpu.SemaphoreType.DMA((n_remote,)),
         ],

time: 258 us -> 256 us (level)
  no operation moved by 1% of the time
where the time goes in v7:
time: 256 us
  Pallas kernels  254 us (99%)
    pallas_call x1, Pallas kernels, front(): pl.pallas_call(lambda lens, img, txt, *refs: front_kernel(dims, lens, img...  63.1 us
    pallas_call x1, Pallas kernels, middle(): pl.pallas_call(functools.partial(middle_kernel, dims, total), grid=(4,),...  57.2 us
    pallas_call x1, Pallas kernels, back(): pl.pallas_call(functools.partial(back_kernel, dims), grid=(4,), in_specs=...  51.8 us
    pallas_call x1, Pallas kernels, finish(): pl.pallas_call(functools.partial(finish_kernel, dims), in_specs=[away] *...  35.8 us
    pallas_call x1, Pallas kernels, turn(): pl.pallas_call(functools.partial(turn_kernel, dims), grid=(4,), in_specs=...  35.8 us
    pallas_call x1, Pallas kernels, spread(): pl.pallas_call(functools.partial(spread_kernel, dims, cols), in_specs=[he...  9.97 us

profile of v7, /device:TPU:0, one launch (start us, length us, event | category | flops | bytes accessed | tf_op | source)
XLA Modules:
  0.0 255.9 jit_solution(4017175222599829265)
XLA Ops:
  1.3 63.1 %front.1 = (f32[16,768]{1,0:T(8,128)}, bf16[6,256,768]{2,1,0:T(8,128)(2,1)}, bf16[6,256,384]{2,1,0:T(8,128)(2,1)}, bf16[6,256,128]{2,1,0:T(8,128)(2,1)}, bf16[6,...) custom-call(s32[12]{0:T(128)} %lens.3, ...), custom_call_target="tpu_custom_call" | custom-call | flops 10871635968 | bytes 40000000 | tf_op jit(solution)/shard_map/front/pallas_call | solution.py:1243
  64.5 57.2 %middle.1 = (bf16[12,256,768]{2,1,0:T(8,128)(2,1)}, bf16[4,2,96,768]{3,2,1,0:T(8,128)(2,1)}, bf16[4,2,96,768]{3,2,1,0:T(8,128)(2,1)}, f32[3,256,768]{2,1,0:T(8,1...) custom-call(bf16[12,197,768]{2,1,0:T(8,128)(2,1)} %img.5, ...), custom_call_target="tpu_custom_call" | custom-call | flops 14495514624 | bytes 40000000 | tf_op jit(solution)/shard_map/middle/pallas_call | solution.py:1533
  121.7 35.8 %turn.1 = (bf16[4,2,96,768]{3,2,1,0:T(8,128)(2,1)}, bf16[4,2,96,768]{3,2,1,0:T(8,128)(2,1)}, bf16[4,2,96,768]{3,2,1,0:T(8,128)(2,1)}, f32[3,256,768]{2,1,0:T(8,1...) custom-call(bf16[12,197,768]{2,1,0:T(8,128)(2,1)} %img.5, ...), custom_call_target="tpu_custom_call" | custom-call | flops 7247757312 | bytes 40000000 | tf_op jit(solution)/shard_map/turn/pallas_call | solution.py:1686
  157.5 0.0 copy-start
  157.5 51.8 %back.1 = (f32[3,256,768]{2,1,0:T(8,128)}, bf16[768,512]{1,0:T(8,128)(2,1)}, bf16[768,256]{1,0:T(8,128)(2,1)}, f32[1,768]{1,0:T(1,128)}, f32[1,384]{1,0:T(1,128)...) custom-call(s32[12]{0:T(128)} %lens.3, ...), custom_call_target="tpu_custom_call" | custom-call | flops 16307453952 | bytes 30000000 | tf_op jit(solution)/shard_map/back/pallas_call | solution.py:1871
  209.3 0.0 copy-done
  209.3 0.5 fusion
  209.9 35.8 %finish.1 = (bf16[3,197,768]{2,1,0:T(8,128)(2,1)}, bf16[3,40,768]{2,1,0:T(8,128)(2,1)}, bf16[3,197,768]{2,1,0:T(8,128)(2,1)}, bf16[3,40,768]{2,1,0:T(8,128)(2,1)...) custom-call(f32[3,256,768]{2,1,0:T(8,128)} %get-tuple-element.127.dnorme, ...), custom_call_target="tpu_custom_call" | custom-call | tf_op jit(solution)/shard_map/finish/pallas_call | solution.py:2070
  245.7 10.0 %spread.1 = (f32[1,96]{1,0:T(1,128)}, f32[1,96]{1,0:T(1,128)}, f32[1,96]{1,0:T(1,128)}, f32[1,96]{1,0:T(1,128)}, f32[2,96]{1,0:T(2,128)}, /*index=5*/f32[2,96]{1...) custom-call(f32[16,768]{1,0:T(8,128)} %get-tuple-element.137.sums, ...), custom_call_target="tpu_custom_call" | custom-call | flops 1000000 | bytes 20000000 | tf_op jit(solution)/shard_map/spread/pallas_call | solution.py:2171
Async XLA Ops:
  157.5 51.8 %copy-start = (f32[2,128]{1,0:T(2,128)S(1)}, f32[2,128]{1,0:T(2,128)}, u32[]{:S(2)}) copy-start(f32[2,128]{1,0:T(2,128)} %get-tuple-element.153) | copy-start | bytes 3076
